TPU v7x, 128 devices: a whole 4x4x4 slice. The times are simulated.
128 devices in a mesh: lat: 8 (over y, core), lon: 16 (over z, x).
Axes of the slice: x: 4, y: 4, z: 4, core: 2. Of those that a mesh axis runs over, the one named last changes fastest.
Arguments:
- increment: float32 [2, 50, 128, 1024], P(None, None, 'lon', 'lat'), may hold values from -6 to 6
- residual: float32 [2, 50, 128, 1024], P(None, None, 'lon', 'lat'), may hold values from -21 to 21
- direction: float32 [2, 50, 128, 1024], P(None, None, 'lon', 'lat'), may hold values from -21 to 21
- diffusivity: float32 [2, 50, 128, 1024], P(None, None, 'lon', 'lat'), may hold values from 0.03 to 0.24
- deviation: float32 [2, 50, 128, 1024], P(None, None, 'lon', 'lat'), may hold values from 0.5 to 2
- stencil: int32 [16384, 128], P(('lat', 'lon')), may hold values from 0 to 51070, as said below
- bilinear: float32 [16384, 4, 128], P(('lat', 'lon')), may hold values from 0 to 1, as said below
- obs_weight: float32 [2, 16384, 128], P(None, ('lat', 'lon')), may hold values from 2 to 6
- block_owner: int32 [16384, 1], P(('lat', 'lon')), may hold values from 0 to 127; in each aligned block of 128 rows (0 to 127, 128 to 255, ...) at most 2 rows name the same one
- correlation: float32 [16384, 128], P(('lat', 'lon')), may hold values from -0.5 to 2, as said below
Outputs:
- next_increment: float32 [2, 50, 128, 1024], P(None, None, 'lon', 'lat')
- next_residual: float32 [2, 50, 128, 1024], P(None, None, 'lon', 'lat')
- next_direction: float32 [2, 50, 128, 1024], P(None, None, 'lon', 'lat')
Inputs may be any that keep to these rules, and one draw needn't show every extreme that they name: `stencil`: each entry is (l * 8 + i) * 128 + j for a level l, a longitude cell i < 7 and a latitude cell j < 127 of the block's tile, so that all four cells of the square lie in that tile. `bilinear`: the four weights of each observation are non-negative and sum to one. `block_owner`: among the 128 blocks of one tile no owner is named more than 2 times, and in every draw some tile names some owner exactly 2 times. `correlation`: each owner's 128 x 128 matrix is symmetric and positive definite.
All inputs are finite; a program needn't handle non-finite values.
Results may differ from a plain program's by a relative error of at most 0.0001.
Values sent between devices are 32-bit elements; how exact they have to be, the bound alone decides.
A program may use at most 64 MiB of HBM per device.

v0:
```python
import functools
import math

import jax
import jax.numpy as jnp
from jax import lax
from jax.experimental import pallas as pl
from jax.experimental.pallas import tpu as pltpu
from jax.sharding import PartitionSpec as P

STEPS = 4
CAP = 2


precise = lax.Precision.HIGHEST


def widen_halo(value, width):
    lat_dim, lon_dim = value.ndim - 1, value.ndim - 2
    for axis, dim, wrap in (("lat", lat_dim, False), ("lon", lon_dim, True)):
        size, length = lax.axis_size(axis), value.shape[dim]
        up = [(i, (i + 1) % size) for i in range(size if wrap else size - 1)]
        down = [(j, i) for i, j in up]
        before = lax.ppermute(lax.slice_in_dim(value, length - width, length, axis=dim), axis, up)
        after = lax.ppermute(lax.slice_in_dim(value, 0, width, axis=dim), axis, down)
        value = jnp.concatenate([before, value, after], axis=dim)
    return value


def face_coeffs(wide, width):
    lat_count = wide.shape[3] - 2 * (width + 1)
    lat_devices = lax.axis_size("lat")
    first = lax.axis_index("lat") * lat_count - width
    cells = first + jnp.arange(lat_count + 2 * width, dtype=jnp.int32)
    inside = ((cells >= 0) & (cells < lat_devices * lat_count)).astype(jnp.float32)
    centre = wide[:, :, 1:-1, 1:-1]
    return (
        inside * (0.5 * (centre + wide[:, :, 1:-1, 2:])),
        inside * (0.5 * (centre + wide[:, :, 1:-1, :-2])),
        inside * (0.5 * (centre + wide[:, :, 2:, 1:-1])),
        inside * (0.5 * (centre + wide[:, :, :-2, 1:-1])),
    )


def diffuse_kernel(steps, field_ref, north_ref, south_ref, east_ref, west_ref, out_ref):
    field = field_ref[...]
    rows, lanes = field.shape[1], field.shape[2]
    north, south, east, west = north_ref[...], south_ref[...], east_ref[...], west_ref[...]
    for sweep in range(steps):
        field = (
            field
            + north * (pltpu.roll(field, lanes - 1, 2) - field)
            + south * (pltpu.roll(field, 1, 2) - field)
            + east * (pltpu.roll(field, rows - 1, 1) - field)
            + west * (pltpu.roll(field, 1, 1) - field)
        )
    field = pltpu.roll(pltpu.roll(field, lanes - steps, 2), rows - steps, 1)
    out_ref[...] = field[:, : out_ref.shape[1], : out_ref.shape[2]]


def pad_lanes(value):
    planes, rows, lanes = value.shape
    return jnp.pad(value, ((0, 0), (0, 0), (0, -lanes % 128)))


def padded_coeffs(coeffs):
    return tuple(pad_lanes(c.reshape((-1,) + c.shape[-2:])) for c in coeffs)


def diffuse(field, coeffs, planes_per_step=50):
    lead = field.shape[:-2]
    flat = pad_lanes(field.reshape((-1,) + field.shape[-2:]))
    planes, rows, lanes = flat.shape
    lon_count, lat_count = rows - 2 * STEPS, field.shape[-1] - 2 * STEPS
    spec = pl.BlockSpec((planes_per_step, rows, lanes), lambda i: (i, 0, 0))
    out = pl.pallas_call(
        functools.partial(diffuse_kernel, STEPS),
        grid=(planes // planes_per_step,),
        in_specs=[spec] * 5,
        out_specs=pl.BlockSpec((planes_per_step, lon_count, lat_count), lambda i: (i, 0, 0)),
        out_shape=jax.ShapeDtypeStruct((planes, lon_count, lat_count), field.dtype),
        cost_estimate=pl.CostEstimate(
            flops=14 * STEPS * planes * rows * lanes, transcendentals=0, bytes_accessed=24 * planes * rows * lanes
        ),
    )(flat, *coeffs)
    return out.reshape(lead + (lon_count, lat_count))


PARTS = 2


def split_parts(value):
    parts = []
    rest = value
    for part in range(PARTS):
        piece = rest.astype(jnp.bfloat16)
        parts.append(piece)
        rest = rest - piece.astype(jnp.float32)
    return parts


def obs_lines(cell_ref, weight_ref, group, lat_count):
    cells = cell_ref[...]
    rows = cells // lat_count
    lats = cells - rows * lat_count
    row_line = jnp.concatenate([rows[g : g + 1, :] for g in range(group)], axis=1)
    lat_line = jnp.concatenate([lats[g : g + 1, :] for g in range(group)], axis=1)
    weights = [
        jnp.concatenate([weight_ref[g, c : c + 1, :] for g in range(group)], axis=1) for c in range(4)
    ]
    return row_line, lat_line, weights


def select_maps(row_line, lat_line, weights, row_count, lat_count):
    width = row_line.shape[1]
    row_ids = lax.broadcasted_iota(jnp.int32, (row_count, width), 0)
    near_rows = (row_ids == row_line).astype(jnp.bfloat16)
    lat_ids = lax.broadcasted_iota(jnp.int32, (lat_count, width), 0)
    at_first = lat_ids == lat_line
    at_second = lat_ids == lat_line + 1
    near_lat = jnp.where(at_first, weights[0], 0.0) + jnp.where(at_second, weights[1], 0.0)
    far_lat = jnp.where(at_first, weights[2], 0.0) + jnp.where(at_second, weights[3], 0.0)
    return near_rows, near_lat, far_lat


def observe_kernel(group, var_count, row_count, lat_count, table_ref, cell_ref, weight_ref, scale_ref, out_ref):
    row_line, lat_line, weights = obs_lines(cell_ref, weight_ref, group, lat_count)
    near_rows, near_lat, far_lat = select_maps(row_line, lat_line, weights, row_count, lat_count)
    table = jnp.concatenate(split_parts(table_ref[...]), axis=1)
    picked = jnp.dot(table, jnp.concatenate([near_rows] * PARTS, axis=0), preferred_element_type=jnp.float32)
    half = var_count * lat_count
    for v in range(var_count):
        near_span = slice(v * lat_count, (v + 1) * lat_count)
        far_span = slice(half + v * lat_count, half + (v + 1) * lat_count)
        line = jnp.sum(picked[near_span] * near_lat + picked[far_span] * far_lat, axis=0, keepdims=True)
        for g in range(group):
            out_ref[v, g : g + 1, :] = scale_ref[v, g : g + 1, :] * line[:, g * 128 : (g + 1) * 128]


def spread_kernel(group, var_count, row_count, lat_count, value_ref, cell_ref, weight_ref, out_ref, total_ref):
    step = pl.program_id(0)

    @pl.when(step == 0)
    def _():
        total_ref[...] = jnp.zeros_like(total_ref)

    row_line, lat_line, weights = obs_lines(cell_ref, weight_ref, group, lat_count)
    near_rows, near_lat, far_lat = select_maps(row_line, lat_line, weights, row_count, lat_count)
    near_parts, far_parts = [], []
    for v in range(var_count):
        line = jnp.concatenate([value_ref[v, g : g + 1, :] for g in range(group)], axis=1)
        near_parts.append(near_lat * line)
        far_parts.append(far_lat * line)
    rhs = jnp.concatenate(split_parts(jnp.concatenate(near_parts + far_parts, axis=0)), axis=1)
    lhs = jnp.concatenate([near_rows] * PARTS, axis=1)
    total_ref[...] += lax.dot_general(
        lhs, rhs, (((1,), (1,)), ((), ())), preferred_element_type=jnp.float32
    )

    @pl.when(step == pl.num_programs(0) - 1)
    def _():
        total = total_ref[...]
        half = var_count * lat_count
        summed = total[:, :half] + pltpu.roll(total[:, half:], 1, 0)
        for v in range(var_count):
            out_ref[v] = summed[:, v * lat_count : (v + 1) * lat_count]


def observe_pallas(field, stencil, bilinear, obs_weight, group=16):
    var_count, level_count, lon_count, lat_count = field.shape
    row_count = level_count * lon_count
    block_count = stencil.shape[0]
    rows_t = jnp.transpose(field.reshape(var_count, row_count, lat_count), (0, 2, 1))
    shifted = jnp.concatenate([rows_t[:, :, 1:], jnp.zeros_like(rows_t[:, :, :1])], axis=2)
    table = jnp.concatenate([rows_t, shifted], axis=0).reshape(2 * var_count * lat_count, row_count)
    kernel = functools.partial(observe_kernel, group, var_count, row_count, lat_count)
    width = group * stencil.shape[1]
    flops = 2 * 2 * var_count * lat_count * PARTS * row_count * width * (block_count // group)
    return pl.pallas_call(
        kernel,
        grid=(block_count // group,),
        in_specs=[
            pl.BlockSpec(table.shape, lambda i: (0, 0)),
            pl.BlockSpec((group, stencil.shape[1]), lambda i: (i, 0)),
            pl.BlockSpec((group, 4, stencil.shape[1]), lambda i: (i, 0, 0)),
            pl.BlockSpec((var_count, group, stencil.shape[1]), lambda i: (0, i, 0)),
        ],
        out_specs=pl.BlockSpec((var_count, group, stencil.shape[1]), lambda i: (0, i, 0)),
        out_shape=jax.ShapeDtypeStruct(obs_weight.shape, jnp.float32),
        cost_estimate=pl.CostEstimate(flops=flops, transcendentals=0, bytes_accessed=4 * 1024 * 1024),
    )(table, stencil, bilinear, obs_weight)


def spread_pallas(values, stencil, bilinear, field_shape, group=16):
    var_count, level_count, lon_count, lat_count = field_shape
    row_count = level_count * lon_count
    block_count = stencil.shape[0]
    kernel = functools.partial(spread_kernel, group, var_count, row_count, lat_count)
    width = group * stencil.shape[1]
    flops = 2 * 2 * var_count * lat_count * PARTS * row_count * width * (block_count // group)
    total = pl.pallas_call(
        kernel,
        grid=(block_count // group,),
        in_specs=[
            pl.BlockSpec((var_count, group, stencil.shape[1]), lambda i: (0, i, 0)),
            pl.BlockSpec((group, stencil.shape[1]), lambda i: (i, 0)),
            pl.BlockSpec((group, 4, stencil.shape[1]), lambda i: (i, 0, 0)),
        ],
        out_specs=pl.BlockSpec((var_count, row_count, lat_count), lambda i: (0, 0, 0)),
        out_shape=jax.ShapeDtypeStruct((var_count, row_count, lat_count), jnp.float32),
        scratch_shapes=[pltpu.VMEM((row_count, 2 * var_count * lat_count), jnp.float32)],
        cost_estimate=pl.CostEstimate(flops=flops, transcendentals=0, bytes_accessed=4 * 1024 * 1024),
    )(values, stencil, bilinear)
    return total.reshape(field_shape)


def allreduce_kernel(lat_devices, lon_devices, part_ref, out_ref, lon_buf, lat_buf, lon_send, lon_recv, lat_send, lat_recv):
    mesh_id = pl.DeviceIdType.MESH
    lat_me = lax.axis_index("lat")
    lon_me = lax.axis_index("lon")
    barrier = pltpu.get_barrier_semaphore()
    for peer in range(1, lon_devices):
        pl.semaphore_signal(barrier, inc=1, device_id=(lat_me, (lon_me + peer) % lon_devices), device_id_type=mesh_id)
    for peer in range(1, lat_devices):
        pl.semaphore_signal(barrier, inc=1, device_id=((lat_me + peer) % lat_devices, lon_me), device_id_type=mesh_id)
    pl.semaphore_wait(barrier, lon_devices + lat_devices - 2)

    def gather(buf, send, recv, count, me, target_of, source):
        copies = []
        for peer in range(1, count):
            target = (me + peer) % count
            copy = pltpu.make_async_remote_copy(
                src_ref=source,
                dst_ref=buf.at[me],
                send_sem=send.at[target],
                recv_sem=recv.at[me],
                device_id=target_of(target),
                device_id_type=mesh_id,
            )
            copy.start()
            copies.append((peer, copy))
        for peer, copy in copies:
            copy.wait_send()
        for peer in range(1, count):
            source_index = (me + count - peer) % count
            pltpu.make_async_remote_copy(
                src_ref=source,
                dst_ref=buf.at[source_index],
                send_sem=send.at[source_index],
                recv_sem=recv.at[source_index],
                device_id=target_of(source_index),
                device_id_type=mesh_id,
            ).wait_recv()

    gather(lon_buf, lon_send, lon_recv, lon_devices, lon_me, lambda t: (lat_me, t), part_ref)
    lon_buf[lon_me] = part_ref[...]
    total = lon_buf[0]
    for i in range(1, lon_devices):
        total = total + lon_buf[i]
    out_ref[...] = total
    gather(lat_buf, lat_send, lat_recv, lat_devices, lat_me, lambda t: (t, lon_me), out_ref)
    lat_buf[lat_me] = out_ref[...]
    total = lat_buf[0]
    for i in range(1, lat_devices):
        total = total + lat_buf[i]
    out_ref[...] = total


def allreduce_pallas(part):
    lat_devices = lax.axis_size("lat")
    lon_devices = lax.axis_size("lon")
    kernel = functools.partial(allreduce_kernel, lat_devices, lon_devices)
    return pl.pallas_call(
        kernel,
        in_specs=[pl.BlockSpec(memory_space=pltpu.VMEM)],
        out_specs=pl.BlockSpec(memory_space=pltpu.VMEM),
        out_shape=jax.ShapeDtypeStruct(part.shape, jnp.float32),
        scratch_shapes=[
            pltpu.VMEM((lon_devices,) + part.shape, jnp.float32),
            pltpu.VMEM((lat_devices,) + part.shape, jnp.float32),
            pltpu.SemaphoreType.DMA((lon_devices,)),
            pltpu.SemaphoreType.DMA((lon_devices,)),
            pltpu.SemaphoreType.DMA((lat_devices,)),
            pltpu.SemaphoreType.DMA((lat_devices,)),
        ],
        compiler_params=pltpu.CompilerParams(collective_id=0, has_side_effects=True),
    )(part)


def slots_of(block_owner, tile_count):
    targets = block_owner[:, 0]
    block_count = targets.shape[0]
    same_owner = (targets[:, None] == jnp.arange(tile_count, dtype=jnp.int32)[None, :]).astype(
        jnp.int32
    )
    order = jnp.arange(block_count, dtype=jnp.int32)
    lower = (order[:, None] > order[None, :]).astype(jnp.int32)
    earlier = jnp.dot(lower, same_owner)
    rank_within = jnp.sum(earlier * same_owner, axis=1)
    return targets * CAP + rank_within


def mix_blocks(values, correlation):
    return jnp.einsum("vsk,ik->vsi", values, correlation, precision=precise)


def shards(
    increment,
    residual,
    direction,
    diffusivity,
    deviation,
    stencil,
    bilinear,
    obs_weight,
    block_owner,
    correlation,
):
    lat_devices = lax.axis_size("lat")
    lon_devices = lax.axis_size("lon")
    tile_count = lat_devices * lon_devices
    both = widen_halo(jnp.stack([direction, diffusivity]), STEPS + 1)
    coeffs = padded_coeffs(face_coeffs(both[1], STEPS))

    def apply_diffusion(field):
        return diffuse(widen_halo(field, STEPS), coeffs)

    slots = slots_of(block_owner, tile_count)
    slot_table = (slots[:, None] == jnp.arange(tile_count * CAP, dtype=jnp.int32)[None, :]).astype(
        jnp.float32
    )
    field_shape = direction.shape
    state_field = deviation * diffuse(both[0][:, :, 1:-1, 1:-1], coeffs)
    observed = observe_pallas(state_field, stencil, bilinear, obs_weight)
    buffer = jnp.einsum("vbk,bs->vsk", observed, slot_table, precision=precise)
    returned = lax.all_to_all(
        mix_blocks(
            lax.all_to_all(buffer, ("lat", "lon"), split_axis=1, concat_axis=1, tiled=True),
            correlation,
        ),
        ("lat", "lon"),
        split_axis=1,
        concat_axis=1,
        tiled=True,
    )
    weighted = obs_weight * jnp.einsum("vsk,bs->vbk", returned, slot_table, precision=precise)
    spread_field = deviation * spread_pallas(weighted, stencil, bilinear, field_shape)
    image_field = direction + apply_diffusion(spread_field)
    local_sums = jnp.stack(
        [
            jnp.sum(residual * residual),
            jnp.sum(direction * image_field),
            jnp.sum(residual * image_field),
            jnp.sum(image_field * image_field),
        ]
    )
    sums = allreduce_pallas(jnp.zeros((8, 128), jnp.float32).at[0, :4].set(local_sums))[0]
    norm_now, curvature, cross, image_norm = sums[0], sums[1], sums[2], sums[3]
    step_size = norm_now / curvature
    increment = increment + step_size * direction
    residual = residual - step_size * image_field
    norm_next = norm_now - 2.0 * step_size * cross + step_size * step_size * image_norm
    direction = residual + norm_next / norm_now * direction
    return (increment, residual, direction)


def solution(mesh):
    in_specs = (
        P(None, None, "lon", "lat"),
        P(None, None, "lon", "lat"),
        P(None, None, "lon", "lat"),
        P(None, None, "lon", "lat"),
        P(None, None, "lon", "lat"),
        P(("lat", "lon"), None),
        P(("lat", "lon"), None, None),
        P(None, ("lat", "lon"), None),
        P(("lat", "lon"), None),
        P(("lat", "lon"), None),
    )
    out_specs = (
        P(None, None, "lon", "lat"),
        P(None, None, "lon", "lat"),
        P(None, None, "lon", "lat"),
    )
    return jax.shard_map(shards, mesh=mesh, in_specs=in_specs, out_specs=out_specs, check_vma=False)
```

profile of v0, /device:TPU:1, one launch (start us, length us, event | category | flops | bytes accessed | tf_op | source)
XLA Modules:
  0.0 217.3 jit_solution(3187641454420263759)
XLA Ops:
  0.6 1.7 slice_maximum_fusion
  2.7 4.6 %collective-permute-start = (f32[2,2,50,8,5]{2,3,4,1,0:T(8,128)S(1)}, f32[2,2,50,8,5]{2,3,4,1,0:T(8,128)S(1)}, u32[]{:S(2)}, u32[]{:S(2)}) collective-permute-start(f32[2,2,50,8,5]{2,3,4,1,0:T(8,128)S(1)} %copy.85), channel_id=1, source_target_pairs={{0,16},{16,32},{32,48},{48,64},{64,80},{80,96},{96,112},{1,17},{17... | collective-permute-start | bytes 96008 | tf_op jit(solution)/shard_map/ppermute | solution.py:24
  7.7 1.9 collective-permute-start.1
  9.7 0.4 copy.68
  10.1 3.4 %collective-permute-done.1 = f32[2,2,50,8,5]{2,3,4,1,0:T(8,128)S(1)} collective-permute-done((f32[2,2,50,8,5]{2,3,4,1,0:T(8,128)S(1)}, f32[2,2,50,8,5]{2,3,4,1,0:T(8,128)S(1)}, u32[]{:S(2)}, u32[]{:S(2)}) %collective-permute-start.1) | collective-permute-done | bytes 32032 | tf_op jit(solution)/shard_map/ppermute | solution.py:25
  13.5 0.4 copy.69
  13.9 0.7 pad_maximum_fusion.2
  14.9 0.8 copy.71
  15.8 6.0 %collective-permute-start.3 = (f32[2,2,50,5,138]{4,1,3,2,0:T(2,128)S(1)}, f32[2,2,50,5,138]{4,1,3,2,0:T(2,128)}, u32[]{:S(2)}, u32[]{:S(2)}) collective-permute-start(f32[2,2,50,5,138]{4,1,3,2,0:T(2,128)S(1)} %copy.71), channel_id=1, source_target_pairs={{1,0},{2,1},{3,2},{4,3},{5,4},{6,5},{7,6},{8,7},{9,8},{10,9},{11,1... | collective-permute-start | bytes 1656008 | tf_op jit(solution)/shard_map/ppermute | solution.py:25
  21.8 1.8 copy.70
  23.8 18.3 %collective-permute-done.3 = f32[2,2,50,5,138]{4,1,3,2,0:T(2,128)} collective-permute-done((f32[2,2,50,5,138]{4,1,3,2,0:T(2,128)S(1)}, f32[2,2,50,5,138]{4,1,3,2,0:T(2,128)}, u32[]{:S(2)}, u32[]{:S(2)}) %collective-permute-start.3) | collective-permute-done | bytes 552032 | tf_op jit(solution)/shard_map/ppermute | solution.py:25
  42.1 1.4 copy.73
  43.5 6.2 %collective-permute-done.2 = f32[2,2,50,5,138]{4,1,3,2,0:T(2,128)} collective-permute-done((f32[2,2,50,5,138]{4,1,3,2,0:T(2,128)}, f32[2,2,50,5,138]{4,1,3,2,0:T(2,128)}, u32[]{:S(2)}, u32[]{:S(2)}) %collective-permute-start.2) | collective-permute-done | bytes 552032 | tf_op jit(solution)/shard_map/ppermute | solution.py:24
  49.8 1.4 copy.72
  51.2 2.5 %pad_maximum_fusion = f32[2,2,50,18,138]{4,3,2,1,0:T(8,128)S(1)} fusion(f32[2,2,50,5,138]{4,3,2,1,0:T(8,128)S(1)} %copy.73, f32[2,2,50,8,5]{4,3,2,1,0:T(8,128)S(1)} %copy.69, f32[1,2,50,8,128]{4,3,2,1,0:T(8,128)S(1)} %bitcast.64, f32[1,2,50,8,128]{4,3,2,1,0:T(8,128)S(1)} %bitcast.53, f32[2,2,50,8,5]{4,3,2,1,0:T(8,128)S(1)} %copy.68, ...), kind=kLoop, calls=%fused_computation | loop fusion | flops 2484000 | bytes 3974400 | tf_op jit(solution)/shard_map/concatenate | solution.py:26
  54.0 0.5 slice.114
  54.5 1.3 pad.25.field_ref
  55.8 1.8 fusion
  57.6 1.4 pad.29.west_ref
  59.0 1.3 pad.28.east_ref
  60.3 1.3 pad.27.south_ref
  61.6 1.3 pad.26.north_ref
  62.9 8.2 %shard_map.121 = f32[100,8,128]{2,1,0:T(8,128)} custom-call(f32[100,16,256]{2,1,0:T(8,128)} %pad.25.field_ref, f32[100,16,256]{2,1,0:T(8,128)} %pad.26.north_ref, f32[100,16,256]{2,1,0:T(8,128)} %pad.27.south_ref, f32[100,16,256]{2,1,0:T(8,128)} %pad.28.east_ref, f32[100,16,256]{2,1,0:T(8,128)} %pad.29.west_ref), custom_call_target="tpu_custom_call" | custom-call | flops 22937600 | bytes 9830400 | tf_op jit(solution)/shard_map/pallas_call | solution.py:76
  71.1 1.0 multiply_bitcast_fusion
  72.6 1.0 select_maximum_fusion
  73.6 25.0 %shard_map.122 = f32[2,128,128]{2,1,0:T(8,128)} custom-call(f32[512,400]{1,0:T(8,128)} %bitcast.67, s32[128,128]{1,0:T(8,128)} %cell_ref.3, f32[128,4,128]{2,1,0:T(4,128)} %weight_ref.3, f32[2,128,128]{2,1,0:T(8,128)} %scale_ref.1), custom_call_target="tpu_custom_call" | custom-call | flops 13421772800 | bytes 4194304 | tf_op jit(solution)/shard_map/pallas_call | solution.py:179
  98.6 1.3 convolution_bitcast_fusion
  100.2 17.1 %all_to_all.10 = f32[2,256,128]{2,0,1:T(2,128)S(1)} all-to-all(f32[2,256,128]{2,0,1:T(2,128)S(1)} %copy.76), channel_id=1, replica_groups=mesh['lat'=8,'lon'=16] {'lat','lon'}, dimensions={1} | all-to-all | bytes 524288 | tf_op jit(solution)/shard_map/all_to_all | solution.py:338
  117.9 15.2 %all_to_all.11 = f32[2,256,128]{2,0,1:T(2,128)S(1)} all-to-all(f32[2,256,128]{2,0,1:T(2,128)S(1)} %copy.78), channel_id=1, replica_groups=mesh['lat'=8,'lon'=16] {'lat','lon'}, dimensions={1} | all-to-all | bytes 524288 | tf_op jit(solution)/shard_map/all_to_all | solution.py:336
  133.1 0.9 fusion.4.value_ref
  134.1 18.4 %shard_map.123 = f32[2,400,128]{2,1,0:T(8,128)} custom-call(f32[2,128,128]{2,1,0:T(8,128)} %fusion.4.value_ref, s32[128,128]{1,0:T(8,128)} %cell_ref.3, f32[128,4,128]{2,1,0:T(4,128)} %weight_ref.3), custom_call_target="tpu_custom_call" | custom-call | flops 13421772800 | bytes 4194304 | tf_op jit(solution)/shard_map/pallas_call | solution.py:201
  152.4 1.1 copy_multiply_fusion
  153.8 2.6 %collective-permute-start.4 = (f32[2,50,8,4]{3,1,2,0:T(8,128)S(1)}, f32[2,50,8,4]{3,1,2,0:T(8,128)S(1)}, u32[]{:S(2)}, u32[]{:S(2)}) collective-permute-start(f32[2,50,8,4]{3,1,2,0:T(8,128)S(1)} %get-tuple-element.34), channel_id=1, source_target_pairs={{0,16},{16,32},{32,48},{48,64},{64,80},{80,96},{96,112},{1,17},{17... | collective-permute-start | bytes 38408 | tf_op jit(solution)/shard_map/ppermute | solution.py:24
  156.4 1.9 collective-permute-start.5
  158.3 3.5 %collective-permute-done.4 = f32[2,50,8,4]{3,1,2,0:T(8,128)S(1)} collective-permute-done((f32[2,50,8,4]{3,1,2,0:T(8,128)S(1)}, f32[2,50,8,4]{3,1,2,0:T(8,128)S(1)}, u32[]{:S(2)}, u32[]{:S(2)}) %collective-permute-start.4) | collective-permute-done | bytes 12832 | tf_op jit(solution)/shard_map/ppermute | solution.py:24
  161.8 4.7 %collective-permute-done.5 = f32[2,50,8,4]{3,1,2,0:T(8,128)S(1)} collective-permute-done((f32[2,50,8,4]{3,1,2,0:T(8,128)S(1)}, f32[2,50,8,4]{3,1,2,0:T(8,128)S(1)}, u32[]{:S(2)}, u32[]{:S(2)}) %collective-permute-start.5) | collective-permute-done | bytes 12832 | tf_op jit(solution)/shard_map/ppermute | solution.py:25
  167.4 4.5 %collective-permute-start.7 = (f32[2,50,4,136]{3,1,2,0:T(8,128)S(1)}, f32[2,50,4,136]{3,1,2,0:T(8,128)S(1)}, u32[]{:S(2)}, u32[]{:S(2)}) collective-permute-start(f32[2,50,4,136]{3,1,2,0:T(8,128)S(1)} %get-tuple-element.31), channel_id=1, source_target_pairs={{1,0},{2,1},{3,2},{4,3},{5,4},{6,5},{7,6},{8,7},{9,8},{10,9},{11,1... | collective-permute-start | bytes 652808 | tf_op jit(solution)/shard_map/ppermute | solution.py:25
  171.9 5.9 %collective-permute-done.6 = f32[2,50,4,136]{3,1,2,0:T(8,128)S(1)} collective-permute-done((f32[2,50,4,136]{3,1,2,0:T(8,128)S(1)}, f32[2,50,4,136]{3,1,2,0:T(8,128)S(1)}, u32[]{:S(2)}, u32[]{:S(2)}) %collective-permute-start.6) | collective-permute-done | bytes 217632 | tf_op jit(solution)/shard_map/ppermute | solution.py:24
  177.7 0.4 pad_maximum_fusion.1
  178.2 0.5 copy.82
  178.7 1.3 pad.30.field_ref
  180.0 8.2 %shard_map.124 = f32[100,8,128]{2,1,0:T(8,128)} custom-call(f32[100,16,256]{2,1,0:T(8,128)} %pad.30.field_ref, f32[100,16,256]{2,1,0:T(8,128)} %pad.26.north_ref, f32[100,16,256]{2,1,0:T(8,128)} %pad.27.south_ref, f32[100,16,256]{2,1,0:T(8,128)} %pad.28.east_ref, f32[100,16,256]{2,1,0:T(8,128)} %pad.29.west_ref), custom_call_target="tpu_custom_call" | custom-call | flops 22937600 | bytes 9830400 | tf_op jit(solution)/shard_map/pallas_call | solution.py:76
  188.2 1.9 multiply_reduce_fusion.3
  190.0 2.6 %maximum_bitcast_fusion = f32[1,4]{1,0:T(1,128)S(1)} fusion(f32[1]{0:T(128)} %bitcast.27, f32[1]{0:T(128)} %bitcast.26, f32[1]{0:T(128)} %bitcast.25, f32[1]{0:T(128)} %bitcast), kind=kLoop, calls=%fused_computation.44 | loop fusion | flops 12 | bytes 32 | tf_op jit(solution)/shard_map/reshape.49
  192.7 0.6 scatter.4.part_ref
  193.3 17.7 %shard_map.125 = f32[8,128]{1,0:T(8,128)} custom-call(f32[8,128]{1,0:T(8,128)} %scatter.4.part_ref), custom_call_target="tpu_custom_call" | custom-call | tf_op jit(solution)/shard_map/pallas_call | solution.py:273
  210.9 1.4 fusion.20
  216.3 1.1 multiply_add_fusion
  (35 shorter events, 3.9 us)
Async XLA Ops:
  0.6 116.7 %copy-start = (f32[128,128]{1,0:T(8,128)S(1)}, f32[128,128]{1,0:T(8,128)}, u32[]{:S(2)}) copy-start(f32[128,128]{1,0:T(8,128)} %param.21) | copy-start | bytes 196612
  2.3 11.6 %copy-start.1 = (f32[2,50,8,128]{3,2,1,0:T(8,128)S(1)}, f32[2,50,8,128]{3,2,1,0:T(8,128)}, u32[]{:S(2)}) copy-start(f32[2,50,8,128]{3,2,1,0:T(8,128)} %param.14) | copy-start | bytes 1228804
  2.3 11.6 %copy-start.2 = (f32[2,50,8,128]{3,2,1,0:T(8,128)S(1)}, f32[2,50,8,128]{3,2,1,0:T(8,128)}, u32[]{:S(2)}) copy-start(f32[2,50,8,128]{3,2,1,0:T(8,128)} %param.15) | copy-start | bytes 1228804
  2.7 6.9 %collective-permute-start = (f32[2,2,50,8,5]{2,3,4,1,0:T(8,128)S(1)}, f32[2,2,50,8,5]{2,3,4,1,0:T(8,128)S(1)}, u32[]{:S(2)}, u32[]{:S(2)}) collective-permute-start(f32[2,2,50,8,5]{2,3,4,1,0:T(8,128)S(1)} %copy.85), channel_id=1, source_target_pairs={{0,16},{16,32},{32,48},{48,64},{64,80},{80,96},{96,112},{1,17},{17... | collective-permute-start | bytes 96008 | tf_op jit(solution)/shard_map/ppermute | solution.py:24
  7.7 5.8 %collective-permute-start.1 = (f32[2,2,50,8,5]{2,3,4,1,0:T(8,128)S(1)}, f32[2,2,50,8,5]{2,3,4,1,0:T(8,128)S(1)}, u32[]{:S(2)}, u32[]{:S(2)}) collective-permute-start(f32[2,2,50,8,5]{2,3,4,1,0:T(8,128)S(1)} %copy.86), channel_id=1, source_target_pairs={{16,0},{32,16},{48,32},{64,48},{80,64},{96,80},{112,96},{17,1},{33... | collective-permute-start | bytes 96008 | tf_op jit(solution)/shard_map/ppermute | solution.py:25
  15.7 7.9 %copy-start.7 = (s32[128,1]{0,1:T(1,128)S(1)}, s32[128,1]{0,1:T(1,128)}, u32[]{:S(2)}) copy-start(s32[128,1]{0,1:T(1,128)} %param.20) | copy-start | bytes 1540
  15.8 26.4 %collective-permute-start.3 = (f32[2,2,50,5,138]{4,1,3,2,0:T(2,128)S(1)}, f32[2,2,50,5,138]{4,1,3,2,0:T(2,128)}, u32[]{:S(2)}, u32[]{:S(2)}) collective-permute-start(f32[2,2,50,5,138]{4,1,3,2,0:T(2,128)S(1)} %copy.71), channel_id=1, source_target_pairs={{1,0},{2,1},{3,2},{4,3},{5,4},{6,5},{7,6},{8,7},{9,8},{10,9},{11,1... | collective-permute-start | bytes 1656008 | tf_op jit(solution)/shard_map/ppermute | solution.py:25
  23.6 26.2 %collective-permute-start.2 = (f32[2,2,50,5,138]{4,1,3,2,0:T(2,128)}, f32[2,2,50,5,138]{4,1,3,2,0:T(2,128)}, u32[]{:S(2)}, u32[]{:S(2)}) collective-permute-start(f32[2,2,50,5,138]{4,1,3,2,0:T(2,128)} %copy.70), channel_id=1, source_target_pairs={{0,1},{1,2},{2,3},{3,4},{4,5},{5,6},{6,7},{7,8},{8,9},{9,10},{10,1... | collective-permute-start | bytes 1656008 | tf_op jit(solution)/shard_map/ppermute | solution.py:24
  62.9 8.2 %copy-start.3 = (f32[2,50,8,128]{3,2,1,0:T(8,128)S(1)}, f32[2,50,8,128]{3,2,1,0:T(8,128)}, u32[]{:S(2)}) copy-start(f32[2,50,8,128]{3,2,1,0:T(8,128)} %param.16) | copy-start | bytes 1228804
  98.6 34.5 %copy-start.6 = (f32[2,128,128]{2,1,0:T(8,128)S(1)}, f32[2,128,128]{2,1,0:T(8,128)}, u32[]{:S(2)}) copy-start(f32[2,128,128]{2,1,0:T(8,128)} %scale_ref.1) | copy-start | bytes 393220
  153.8 8.0 %collective-permute-start.4 = (f32[2,50,8,4]{3,1,2,0:T(8,128)S(1)}, f32[2,50,8,4]{3,1,2,0:T(8,128)S(1)}, u32[]{:S(2)}, u32[]{:S(2)}) collective-permute-start(f32[2,50,8,4]{3,1,2,0:T(8,128)S(1)} %get-tuple-element.34), channel_id=1, source_target_pairs={{0,16},{16,32},{32,48},{48,64},{64,80},{80,96},{96,112},{1,17},{17... | collective-permute-start | bytes 38408 | tf_op jit(solution)/shard_map/ppermute | solution.py:24
  156.4 10.1 %collective-permute-start.5 = (f32[2,50,8,4]{3,1,2,0:T(8,128)S(1)}, f32[2,50,8,4]{3,1,2,0:T(8,128)S(1)}, u32[]{:S(2)}, u32[]{:S(2)}) collective-permute-start(f32[2,50,8,4]{3,1,2,0:T(8,128)S(1)} %get-tuple-element.35), channel_id=1, source_target_pairs={{16,0},{32,16},{48,32},{64,48},{80,64},{96,80},{112,96},{17,1},{33... | collective-permute-start | bytes 38408 | tf_op jit(solution)/shard_map/ppermute | solution.py:25
  167.0 10.7 %collective-permute-start.6 = (f32[2,50,4,136]{3,1,2,0:T(8,128)S(1)}, f32[2,50,4,136]{3,1,2,0:T(8,128)S(1)}, u32[]{:S(2)}, u32[]{:S(2)}) collective-permute-start(f32[2,50,4,136]{3,1,2,0:T(8,128)S(1)} %get-tuple-element.30), channel_id=1, source_target_pairs={{0,1},{1,2},{2,3},{3,4},{4,5},{5,6},{6,7},{7,8},{8,9},{9,10},{10,1... | collective-permute-start | bytes 652808 | tf_op jit(solution)/shard_map/ppermute | solution.py:24
  167.4 10.3 %collective-permute-start.7 = (f32[2,50,4,136]{3,1,2,0:T(8,128)S(1)}, f32[2,50,4,136]{3,1,2,0:T(8,128)S(1)}, u32[]{:S(2)}, u32[]{:S(2)}) collective-permute-start(f32[2,50,4,136]{3,1,2,0:T(8,128)S(1)} %get-tuple-element.31), channel_id=1, source_target_pairs={{1,0},{2,1},{3,2},{4,3},{5,4},{6,5},{7,6},{8,7},{9,8},{10,9},{11,1... | collective-permute-start | bytes 652808 | tf_op jit(solution)/shard_map/ppermute | solution.py:25
  180.0 8.2 %copy-start.4 = (f32[2,50,8,128]{3,2,1,0:T(8,128)S(1)}, f32[2,50,8,128]{3,2,1,0:T(8,128)}, u32[]{:S(2)}) copy-start(f32[2,50,8,128]{3,2,1,0:T(8,128)} %param.13) | copy-start | bytes 1228804
  188.2 28.1 %copy-start.5 = (f32[2,50,8,128]{3,2,1,0:T(8,128)S(1)}, f32[2,50,8,128]{3,2,1,0:T(8,128)}, u32[]{:S(2)}) copy-start(f32[2,50,8,128]{3,2,1,0:T(8,128)} %param.12) | copy-start | bytes 1228804
where the time goes:
time: 218 us; the launch traced here: 217 us
  Pallas kernels  77.4 us (36%)
  waiting for transfers between devices  41.9 us (19%)
  blocking collectives  32.4 us (15%)
  starting transfers between devices  21.9 us (10%)
  local copies, waits for them, and re-layouts  19.9 us (9%)
  other arithmetic  16.3 us (7%)
  between operations  4.79 us (2%)
  matrix products  2.8 us (1%)
    ppermute x4, waiting for transfers between devices, widen_halo(): lax.ppermute(lax.slice_in_dim(value, 0, width, axis=dim), axis, down)  26.4 us
    pallas_call x1, Pallas kernels, observe_pallas(): pl.pallas_call(kernel, grid=(block_count // group,), in_specs=[pl.BlockSp...  25 us
    pallas_call x1, Pallas kernels, spread_pallas(): pl.pallas_call(kernel, grid=(block_count // group,), in_specs=[pl.BlockSp...  18.4 us
    pallas_call x1, Pallas kernels, allreduce_pallas(): pl.pallas_call(kernel, in_specs=[pl.BlockSpec(memory_space=pltpu.VMEM)],...  17.7 us
    all_to_all x1, blocking collectives, shards(): lax.all_to_all(buffer, ('lat', 'lon'), split_axis=1, concat_axis=1, tiled...  17.1 us
    pallas_call x2, Pallas kernels, diffuse(): pl.pallas_call(functools.partial(diffuse_kernel, STEPS), grid=(planes //...  16.3 us
    ppermute x4, waiting for transfers between devices, widen_halo(): lax.ppermute(lax.slice_in_dim(value, length - width, length, axis=dim), a...  15.5 us
    all_to_all x1, blocking collectives, shards(): lax.all_to_all(mix_blocks(lax.all_to_all(buffer, ('lat', 'lon'), split_ax...  15.2 us
  transfers between devices with their start and end apart: 8, of which 6 were waited for; matrix products, arithmetic and copies ran while one was open for 2% of the time, Pallas kernels for 0%

commit v1 on v0

--- a/solution.py
+++ b/solution.py
@@ -46,13 +46,14 @@
     field = field_ref[...]
     rows, lanes = field.shape[1], field.shape[2]
     north, south, east, west = north_ref[...], south_ref[...], east_ref[...], west_ref[...]
+    keep = 1.0 - (north + south + east + west)
     for sweep in range(steps):
         field = (
-            field
-            + north * (pltpu.roll(field, lanes - 1, 2) - field)
-            + south * (pltpu.roll(field, 1, 2) - field)
-            + east * (pltpu.roll(field, rows - 1, 1) - field)
-            + west * (pltpu.roll(field, 1, 1) - field)
+            keep * field
+            + north * pltpu.roll(field, lanes - 1, 2)
+            + south * pltpu.roll(field, 1, 2)
+            + east * pltpu.roll(field, rows - 1, 1)
+            + west * pltpu.roll(field, 1, 1)
         )
     field = pltpu.roll(pltpu.roll(field, lanes - steps, 2), rows - steps, 1)
     out_ref[...] = field[:, : out_ref.shape[1], : out_ref.shape[2]]

time: 218 us -> 218 us (level)
  no operation moved by 1% of the time
where the time goes in v1:
time: 218 us
  Pallas kernels  77.6 us (36%)
  waiting for transfers between devices  41.9 us (19%)
  blocking collectives  32.4 us (15%)
  starting transfers between devices  21.9 us (10%)
  local copies, waits for them, and re-layouts  19.9 us (9%)
  other arithmetic  16.3 us (7%)
  between operations  4.79 us (2%)
  matrix products  2.8 us (1%)
    ppermute x4, waiting for transfers between devices, widen_halo(): lax.ppermute(lax.slice_in_dim(value, 0, width, axis=dim), axis, down)  26.4 us
    pallas_call x1, Pallas kernels, observe_pallas(): pl.pallas_call(kernel, grid=(block_count // group,), in_specs=[pl.BlockSp...  25 us
    pallas_call x1, Pallas kernels, spread_pallas(): pl.pallas_call(kernel, grid=(block_count // group,), in_specs=[pl.BlockSp...  18.4 us
    pallas_call x1, Pallas kernels, allreduce_pallas(): pl.pallas_call(kernel, in_specs=[pl.BlockSpec(memory_space=pltpu.VMEM)],...  17.7 us
    all_to_all x1, blocking collectives, shards(): lax.all_to_all(buffer, ('lat', 'lon'), split_axis=1, concat_axis=1, tiled...  17.1 us
    pallas_call x2, Pallas kernels, diffuse(): pl.pallas_call(functools.partial(diffuse_kernel, STEPS), grid=(planes //...  16.5 us
    ppermute x4, waiting for transfers between devices, widen_halo(): lax.ppermute(lax.slice_in_dim(value, length - width, length, axis=dim), a...  15.5 us
    all_to_all x1, blocking collectives, shards(): lax.all_to_all(mix_blocks(lax.all_to_all(buffer, ('lat', 'lon'), split_ax...  15.2 us
  transfers between devices with their start and end apart: 8, of which 6 were waited for; matrix products, arithmetic and copies ran while one was open for 2% of the time, Pallas kernels for 0%

profile of v1, /device:TPU:1, one launch (start us, length us, event | category | flops | bytes accessed | tf_op | source)
XLA Modules:
  0.0 217.5 jit_solution(14972015289154765016)
XLA Ops:
  0.6 1.7 slice_maximum_fusion
  2.7 4.6 %collective-permute-start = (f32[2,2,50,8,5]{2,3,4,1,0:T(8,128)S(1)}, f32[2,2,50,8,5]{2,3,4,1,0:T(8,128)S(1)}, u32[]{:S(2)}, u32[]{:S(2)}) collective-permute-start(f32[2,2,50,8,5]{2,3,4,1,0:T(8,128)S(1)} %copy.85), channel_id=1, source_target_pairs={{0,16},{16,32},{32,48},{48,64},{64,80},{80,96},{96,112},{1,17},{17... | collective-permute-start | bytes 96008 | tf_op jit(solution)/shard_map/ppermute | solution.py:24
  7.7 1.9 collective-permute-start.1
  9.7 0.4 copy.68
  10.1 3.4 %collective-permute-done.1 = f32[2,2,50,8,5]{2,3,4,1,0:T(8,128)S(1)} collective-permute-done((f32[2,2,50,8,5]{2,3,4,1,0:T(8,128)S(1)}, f32[2,2,50,8,5]{2,3,4,1,0:T(8,128)S(1)}, u32[]{:S(2)}, u32[]{:S(2)}) %collective-permute-start.1) | collective-permute-done | bytes 32032 | tf_op jit(solution)/shard_map/ppermute | solution.py:25
  13.5 0.4 copy.69
  13.9 0.7 pad_maximum_fusion.2
  14.9 0.8 copy.71
  15.8 6.0 %collective-permute-start.3 = (f32[2,2,50,5,138]{4,1,3,2,0:T(2,128)S(1)}, f32[2,2,50,5,138]{4,1,3,2,0:T(2,128)}, u32[]{:S(2)}, u32[]{:S(2)}) collective-permute-start(f32[2,2,50,5,138]{4,1,3,2,0:T(2,128)S(1)} %copy.71), channel_id=1, source_target_pairs={{1,0},{2,1},{3,2},{4,3},{5,4},{6,5},{7,6},{8,7},{9,8},{10,9},{11,1... | collective-permute-start | bytes 1656008 | tf_op jit(solution)/shard_map/ppermute | solution.py:25
  21.8 1.8 copy.70
  23.8 18.3 %collective-permute-done.3 = f32[2,2,50,5,138]{4,1,3,2,0:T(2,128)} collective-permute-done((f32[2,2,50,5,138]{4,1,3,2,0:T(2,128)S(1)}, f32[2,2,50,5,138]{4,1,3,2,0:T(2,128)}, u32[]{:S(2)}, u32[]{:S(2)}) %collective-permute-start.3) | collective-permute-done | bytes 552032 | tf_op jit(solution)/shard_map/ppermute | solution.py:25
  42.1 1.4 copy.73
  43.5 6.2 %collective-permute-done.2 = f32[2,2,50,5,138]{4,1,3,2,0:T(2,128)} collective-permute-done((f32[2,2,50,5,138]{4,1,3,2,0:T(2,128)}, f32[2,2,50,5,138]{4,1,3,2,0:T(2,128)}, u32[]{:S(2)}, u32[]{:S(2)}) %collective-permute-start.2) | collective-permute-done | bytes 552032 | tf_op jit(solution)/shard_map/ppermute | solution.py:24
  49.8 1.4 copy.72
  51.2 2.5 %pad_maximum_fusion = f32[2,2,50,18,138]{4,3,2,1,0:T(8,128)S(1)} fusion(f32[2,2,50,5,138]{4,3,2,1,0:T(8,128)S(1)} %copy.73, f32[2,2,50,8,5]{4,3,2,1,0:T(8,128)S(1)} %copy.69, f32[1,2,50,8,128]{4,3,2,1,0:T(8,128)S(1)} %bitcast.64, f32[1,2,50,8,128]{4,3,2,1,0:T(8,128)S(1)} %bitcast.53, f32[2,2,50,8,5]{4,3,2,1,0:T(8,128)S(1)} %copy.68, ...), kind=kLoop, calls=%fused_computation | loop fusion | flops 2484000 | bytes 3974400 | tf_op jit(solution)/shard_map/concatenate | solution.py:26
  54.0 0.5 slice.114
  54.5 1.3 pad.25.field_ref
  55.8 1.8 fusion
  57.6 1.4 pad.29.west_ref
  59.0 1.3 pad.28.east_ref
  60.3 1.3 pad.27.south_ref
  61.6 1.3 pad.26.north_ref
  62.9 8.3 %shard_map.121 = f32[100,8,128]{2,1,0:T(8,128)} custom-call(f32[100,16,256]{2,1,0:T(8,128)} %pad.25.field_ref, f32[100,16,256]{2,1,0:T(8,128)} %pad.26.north_ref, f32[100,16,256]{2,1,0:T(8,128)} %pad.27.south_ref, f32[100,16,256]{2,1,0:T(8,128)} %pad.28.east_ref, f32[100,16,256]{2,1,0:T(8,128)} %pad.29.west_ref), custom_call_target="tpu_custom_call" | custom-call | flops 22937600 | bytes 9830400 | tf_op jit(solution)/shard_map/pallas_call | solution.py:77
  71.2 1.0 multiply_bitcast_fusion
  72.6 1.0 select_maximum_fusion
  73.7 25.0 %shard_map.122 = f32[2,128,128]{2,1,0:T(8,128)} custom-call(f32[512,400]{1,0:T(8,128)} %bitcast.67, s32[128,128]{1,0:T(8,128)} %cell_ref.3, f32[128,4,128]{2,1,0:T(4,128)} %weight_ref.3, f32[2,128,128]{2,1,0:T(8,128)} %scale_ref.1), custom_call_target="tpu_custom_call" | custom-call | flops 13421772800 | bytes 4194304 | tf_op jit(solution)/shard_map/pallas_call | solution.py:180
  98.7 1.3 convolution_bitcast_fusion
  100.3 17.1 %all_to_all.10 = f32[2,256,128]{2,0,1:T(2,128)S(1)} all-to-all(f32[2,256,128]{2,0,1:T(2,128)S(1)} %copy.76), channel_id=1, replica_groups=mesh['lat'=8,'lon'=16] {'lat','lon'}, dimensions={1} | all-to-all | bytes 524288 | tf_op jit(solution)/shard_map/all_to_all | solution.py:339
  118.0 15.2 %all_to_all.11 = f32[2,256,128]{2,0,1:T(2,128)S(1)} all-to-all(f32[2,256,128]{2,0,1:T(2,128)S(1)} %copy.78), channel_id=1, replica_groups=mesh['lat'=8,'lon'=16] {'lat','lon'}, dimensions={1} | all-to-all | bytes 524288 | tf_op jit(solution)/shard_map/all_to_all | solution.py:337
  133.2 0.9 fusion.4.value_ref
  134.1 18.4 %shard_map.123 = f32[2,400,128]{2,1,0:T(8,128)} custom-call(f32[2,128,128]{2,1,0:T(8,128)} %fusion.4.value_ref, s32[128,128]{1,0:T(8,128)} %cell_ref.3, f32[128,4,128]{2,1,0:T(4,128)} %weight_ref.3), custom_call_target="tpu_custom_call" | custom-call | flops 13421772800 | bytes 4194304 | tf_op jit(solution)/shard_map/pallas_call | solution.py:202
  152.5 1.1 copy_multiply_fusion
  153.9 2.6 %collective-permute-start.4 = (f32[2,50,8,4]{3,1,2,0:T(8,128)S(1)}, f32[2,50,8,4]{3,1,2,0:T(8,128)S(1)}, u32[]{:S(2)}, u32[]{:S(2)}) collective-permute-start(f32[2,50,8,4]{3,1,2,0:T(8,128)S(1)} %get-tuple-element.34), channel_id=1, source_target_pairs={{0,16},{16,32},{32,48},{48,64},{64,80},{80,96},{96,112},{1,17},{17... | collective-permute-start | bytes 38408 | tf_op jit(solution)/shard_map/ppermute | solution.py:24
  156.5 1.9 collective-permute-start.5
  158.4 3.5 %collective-permute-done.4 = f32[2,50,8,4]{3,1,2,0:T(8,128)S(1)} collective-permute-done((f32[2,50,8,4]{3,1,2,0:T(8,128)S(1)}, f32[2,50,8,4]{3,1,2,0:T(8,128)S(1)}, u32[]{:S(2)}, u32[]{:S(2)}) %collective-permute-start.4) | collective-permute-done | bytes 12832 | tf_op jit(solution)/shard_map/ppermute | solution.py:24
  161.9 4.7 %collective-permute-done.5 = f32[2,50,8,4]{3,1,2,0:T(8,128)S(1)} collective-permute-done((f32[2,50,8,4]{3,1,2,0:T(8,128)S(1)}, f32[2,50,8,4]{3,1,2,0:T(8,128)S(1)}, u32[]{:S(2)}, u32[]{:S(2)}) %collective-permute-start.5) | collective-permute-done | bytes 12832 | tf_op jit(solution)/shard_map/ppermute | solution.py:25
  167.5 4.5 %collective-permute-start.7 = (f32[2,50,4,136]{3,1,2,0:T(8,128)S(1)}, f32[2,50,4,136]{3,1,2,0:T(8,128)S(1)}, u32[]{:S(2)}, u32[]{:S(2)}) collective-permute-start(f32[2,50,4,136]{3,1,2,0:T(8,128)S(1)} %get-tuple-element.31), channel_id=1, source_target_pairs={{1,0},{2,1},{3,2},{4,3},{5,4},{6,5},{7,6},{8,7},{9,8},{10,9},{11,1... | collective-permute-start | bytes 652808 | tf_op jit(solution)/shard_map/ppermute | solution.py:25
  171.9 5.9 %collective-permute-done.6 = f32[2,50,4,136]{3,1,2,0:T(8,128)S(1)} collective-permute-done((f32[2,50,4,136]{3,1,2,0:T(8,128)S(1)}, f32[2,50,4,136]{3,1,2,0:T(8,128)S(1)}, u32[]{:S(2)}, u32[]{:S(2)}) %collective-permute-start.6) | collective-permute-done | bytes 217632 | tf_op jit(solution)/shard_map/ppermute | solution.py:24
  177.8 0.4 pad_maximum_fusion.1
  178.2 0.5 copy.82
  178.7 1.3 pad.30.field_ref
  180.1 8.3 %shard_map.124 = f32[100,8,128]{2,1,0:T(8,128)} custom-call(f32[100,16,256]{2,1,0:T(8,128)} %pad.30.field_ref, f32[100,16,256]{2,1,0:T(8,128)} %pad.26.north_ref, f32[100,16,256]{2,1,0:T(8,128)} %pad.27.south_ref, f32[100,16,256]{2,1,0:T(8,128)} %pad.28.east_ref, f32[100,16,256]{2,1,0:T(8,128)} %pad.29.west_ref), custom_call_target="tpu_custom_call" | custom-call | flops 22937600 | bytes 9830400 | tf_op jit(solution)/shard_map/pallas_call | solution.py:77
  188.3 1.9 multiply_reduce_fusion.3
  190.2 2.6 %maximum_bitcast_fusion = f32[1,4]{1,0:T(1,128)S(1)} fusion(f32[1]{0:T(128)} %bitcast.27, f32[1]{0:T(128)} %bitcast.26, f32[1]{0:T(128)} %bitcast.25, f32[1]{0:T(128)} %bitcast), kind=kLoop, calls=%fused_computation.44 | loop fusion | flops 12 | bytes 32 | tf_op jit(solution)/shard_map/reshape.49
  192.8 0.6 scatter.4.part_ref
  193.4 17.7 %shard_map.125 = f32[8,128]{1,0:T(8,128)} custom-call(f32[8,128]{1,0:T(8,128)} %scatter.4.part_ref), custom_call_target="tpu_custom_call" | custom-call | tf_op jit(solution)/shard_map/pallas_call | solution.py:274
  211.1 1.4 fusion.20
  216.4 1.1 multiply_add_fusion
  (35 shorter events, 3.9 us)
Async XLA Ops:
  0.6 116.7 %copy-start = (f32[128,128]{1,0:T(8,128)S(1)}, f32[128,128]{1,0:T(8,128)}, u32[]{:S(2)}) copy-start(f32[128,128]{1,0:T(8,128)} %param.21) | copy-start | bytes 196612
  2.3 11.6 %copy-start.1 = (f32[2,50,8,128]{3,2,1,0:T(8,128)S(1)}, f32[2,50,8,128]{3,2,1,0:T(8,128)}, u32[]{:S(2)}) copy-start(f32[2,50,8,128]{3,2,1,0:T(8,128)} %param.14) | copy-start | bytes 1228804
  2.3 11.6 %copy-start.2 = (f32[2,50,8,128]{3,2,1,0:T(8,128)S(1)}, f32[2,50,8,128]{3,2,1,0:T(8,128)}, u32[]{:S(2)}) copy-start(f32[2,50,8,128]{3,2,1,0:T(8,128)} %param.15) | copy-start | bytes 1228804
  2.7 6.9 %collective-permute-start = (f32[2,2,50,8,5]{2,3,4,1,0:T(8,128)S(1)}, f32[2,2,50,8,5]{2,3,4,1,0:T(8,128)S(1)}, u32[]{:S(2)}, u32[]{:S(2)}) collective-permute-start(f32[2,2,50,8,5]{2,3,4,1,0:T(8,128)S(1)} %copy.85), channel_id=1, source_target_pairs={{0,16},{16,32},{32,48},{48,64},{64,80},{80,96},{96,112},{1,17},{17... | collective-permute-start | bytes 96008 | tf_op jit(solution)/shard_map/ppermute | solution.py:24
  7.7 5.8 %collective-permute-start.1 = (f32[2,2,50,8,5]{2,3,4,1,0:T(8,128)S(1)}, f32[2,2,50,8,5]{2,3,4,1,0:T(8,128)S(1)}, u32[]{:S(2)}, u32[]{:S(2)}) collective-permute-start(f32[2,2,50,8,5]{2,3,4,1,0:T(8,128)S(1)} %copy.86), channel_id=1, source_target_pairs={{16,0},{32,16},{48,32},{64,48},{80,64},{96,80},{112,96},{17,1},{33... | collective-permute-start | bytes 96008 | tf_op jit(solution)/shard_map/ppermute | solution.py:25
  15.7 7.9 %copy-start.7 = (s32[128,1]{0,1:T(1,128)S(1)}, s32[128,1]{0,1:T(1,128)}, u32[]{:S(2)}) copy-start(s32[128,1]{0,1:T(1,128)} %param.20) | copy-start | bytes 1540
  15.8 26.4 %collective-permute-start.3 = (f32[2,2,50,5,138]{4,1,3,2,0:T(2,128)S(1)}, f32[2,2,50,5,138]{4,1,3,2,0:T(2,128)}, u32[]{:S(2)}, u32[]{:S(2)}) collective-permute-start(f32[2,2,50,5,138]{4,1,3,2,0:T(2,128)S(1)} %copy.71), channel_id=1, source_target_pairs={{1,0},{2,1},{3,2},{4,3},{5,4},{6,5},{7,6},{8,7},{9,8},{10,9},{11,1... | collective-permute-start | bytes 1656008 | tf_op jit(solution)/shard_map/ppermute | solution.py:25
  23.6 26.2 %collective-permute-start.2 = (f32[2,2,50,5,138]{4,1,3,2,0:T(2,128)}, f32[2,2,50,5,138]{4,1,3,2,0:T(2,128)}, u32[]{:S(2)}, u32[]{:S(2)}) collective-permute-start(f32[2,2,50,5,138]{4,1,3,2,0:T(2,128)} %copy.70), channel_id=1, source_target_pairs={{0,1},{1,2},{2,3},{3,4},{4,5},{5,6},{6,7},{7,8},{8,9},{9,10},{10,1... | collective-permute-start | bytes 1656008 | tf_op jit(solution)/shard_map/ppermute | solution.py:24
  62.9 8.3 %copy-start.3 = (f32[2,50,8,128]{3,2,1,0:T(8,128)S(1)}, f32[2,50,8,128]{3,2,1,0:T(8,128)}, u32[]{:S(2)}) copy-start(f32[2,50,8,128]{3,2,1,0:T(8,128)} %param.16) | copy-start | bytes 1228804
  98.7 34.5 %copy-start.6 = (f32[2,128,128]{2,1,0:T(8,128)S(1)}, f32[2,128,128]{2,1,0:T(8,128)}, u32[]{:S(2)}) copy-start(f32[2,128,128]{2,1,0:T(8,128)} %scale_ref.1) | copy-start | bytes 393220
  153.9 8.0 %collective-permute-start.4 = (f32[2,50,8,4]{3,1,2,0:T(8,128)S(1)}, f32[2,50,8,4]{3,1,2,0:T(8,128)S(1)}, u32[]{:S(2)}, u32[]{:S(2)}) collective-permute-start(f32[2,50,8,4]{3,1,2,0:T(8,128)S(1)} %get-tuple-element.34), channel_id=1, source_target_pairs={{0,16},{16,32},{32,48},{48,64},{64,80},{80,96},{96,112},{1,17},{17... | collective-permute-start | bytes 38408 | tf_op jit(solution)/shard_map/ppermute | solution.py:24
  156.5 10.1 %collective-permute-start.5 = (f32[2,50,8,4]{3,1,2,0:T(8,128)S(1)}, f32[2,50,8,4]{3,1,2,0:T(8,128)S(1)}, u32[]{:S(2)}, u32[]{:S(2)}) collective-permute-start(f32[2,50,8,4]{3,1,2,0:T(8,128)S(1)} %get-tuple-element.35), channel_id=1, source_target_pairs={{16,0},{32,16},{48,32},{64,48},{80,64},{96,80},{112,96},{17,1},{33... | collective-permute-start | bytes 38408 | tf_op jit(solution)/shard_map/ppermute | solution.py:25
  167.1 10.7 %collective-permute-start.6 = (f32[2,50,4,136]{3,1,2,0:T(8,128)S(1)}, f32[2,50,4,136]{3,1,2,0:T(8,128)S(1)}, u32[]{:S(2)}, u32[]{:S(2)}) collective-permute-start(f32[2,50,4,136]{3,1,2,0:T(8,128)S(1)} %get-tuple-element.30), channel_id=1, source_target_pairs={{0,1},{1,2},{2,3},{3,4},{4,5},{5,6},{6,7},{7,8},{8,9},{9,10},{10,1... | collective-permute-start | bytes 652808 | tf_op jit(solution)/shard_map/ppermute | solution.py:24
  167.5 10.3 %collective-permute-start.7 = (f32[2,50,4,136]{3,1,2,0:T(8,128)S(1)}, f32[2,50,4,136]{3,1,2,0:T(8,128)S(1)}, u32[]{:S(2)}, u32[]{:S(2)}) collective-permute-start(f32[2,50,4,136]{3,1,2,0:T(8,128)S(1)} %get-tuple-element.31), channel_id=1, source_target_pairs={{1,0},{2,1},{3,2},{4,3},{5,4},{6,5},{7,6},{8,7},{9,8},{10,9},{11,1... | collective-permute-start | bytes 652808 | tf_op jit(solution)/shard_map/ppermute | solution.py:25
  180.1 8.3 %copy-start.4 = (f32[2,50,8,128]{3,2,1,0:T(8,128)S(1)}, f32[2,50,8,128]{3,2,1,0:T(8,128)}, u32[]{:S(2)}) copy-start(f32[2,50,8,128]{3,2,1,0:T(8,128)} %param.13) | copy-start | bytes 1228804
  188.3 28.1 %copy-start.5 = (f32[2,50,8,128]{3,2,1,0:T(8,128)S(1)}, f32[2,50,8,128]{3,2,1,0:T(8,128)}, u32[]{:S(2)}) copy-start(f32[2,50,8,128]{3,2,1,0:T(8,128)} %param.12) | copy-start | bytes 1228804

commit v2 on v0

--- a/solution.py
+++ b/solution.py
@@ -43,19 +43,24 @@
 
 
 def diffuse_kernel(steps, field_ref, north_ref, south_ref, east_ref, west_ref, out_ref):
-    field = field_ref[...]
-    rows, lanes = field.shape[1], field.shape[2]
-    north, south, east, west = north_ref[...], south_ref[...], east_ref[...], west_ref[...]
-    for sweep in range(steps):
-        field = (
-            field
-            + north * (pltpu.roll(field, lanes - 1, 2) - field)
-            + south * (pltpu.roll(field, 1, 2) - field)
-            + east * (pltpu.roll(field, rows - 1, 1) - field)
-            + west * (pltpu.roll(field, 1, 1) - field)
-        )
-    field = pltpu.roll(pltpu.roll(field, lanes - steps, 2), rows - steps, 1)
-    out_ref[...] = field[:, : out_ref.shape[1], : out_ref.shape[2]]
+    rows, lanes = field_ref.shape[1], field_ref.shape[2]
+
+    def one_plane(plane, carry):
+        field = field_ref[plane]
+        north, south, east, west = north_ref[plane], south_ref[plane], east_ref[plane], west_ref[plane]
+        for sweep in range(steps):
+            field = (
+                field
+                + north * (pltpu.roll(field, lanes - 1, 1) - field)
+                + south * (pltpu.roll(field, 1, 1) - field)
+                + east * (pltpu.roll(field, rows - 1, 0) - field)
+                + west * (pltpu.roll(field, 1, 0) - field)
+            )
+        field = pltpu.roll(pltpu.roll(field, lanes - steps, 1), rows - steps, 0)
+        out_ref[plane] = field[: out_ref.shape[1], : out_ref.shape[2]]
+        return carry
+
+    lax.fori_loop(0, field_ref.shape[0], one_plane, 0)
 
 
 def pad_lanes(value):

time: 218 us -> 286 us (1.31)
  Pallas kernels: 77.4 us -> 145 us
    pallas_call x2, Pallas kernels: 16.3 us -> 84.1 us  [diffuse(): pl.pallas_call(functools.partial(diffuse_kernel, STEPS), grid=(planes //...]
  transfers between devices with their start and end apart: 8 -> 8, of which waited for: 6 -> 6; matrix products, arithmetic and copies ran while one was open for 2% -> 1% of each run, Pallas kernels for 0% -> 0%
where the time goes in v2:
time: 286 us; the launch traced here: 285 us
  Pallas kernels  145 us (51%)
  waiting for transfers between devices  41.9 us (15%)
  blocking collectives  32.4 us (11%)
  starting transfers between devices  21.9 us (8%)
  local copies, waits for them, and re-layouts  19.9 us (7%)
  other arithmetic  16.3 us (6%)
  between operations  4.79 us (2%)
    pallas_call x2, Pallas kernels, diffuse(): pl.pallas_call(functools.partial(diffuse_kernel, STEPS), grid=(planes //...  84.1 us
    ppermute x4, waiting for transfers between devices, widen_halo(): lax.ppermute(lax.slice_in_dim(value, 0, width, axis=dim), axis, down)  26.4 us
    pallas_call x1, Pallas kernels, observe_pallas(): pl.pallas_call(kernel, grid=(block_count // group,), in_specs=[pl.BlockSp...  25 us
    pallas_call x1, Pallas kernels, spread_pallas(): pl.pallas_call(kernel, grid=(block_count // group,), in_specs=[pl.BlockSp...  18.4 us
    pallas_call x1, Pallas kernels, allreduce_pallas(): pl.pallas_call(kernel, in_specs=[pl.BlockSpec(memory_space=pltpu.VMEM)],...  17.7 us
    all_to_all x1, blocking collectives, shards(): lax.all_to_all(buffer, ('lat', 'lon'), split_axis=1, concat_axis=1, tiled...  17.1 us
    ppermute x4, waiting for transfers between devices, widen_halo(): lax.ppermute(lax.slice_in_dim(value, length - width, length, axis=dim), a...  15.5 us
    all_to_all x1, blocking collectives, shards(): lax.all_to_all(mix_blocks(lax.all_to_all(buffer, ('lat', 'lon'), split_ax...  15.2 us
  transfers between devices with their start and end apart: 8, of which 6 were waited for; matrix products, arithmetic and copies ran while one was open for 1% of the time, Pallas kernels for 0%

profile of v2, /device:TPU:1, one launch (start us, length us, event | category | flops | bytes accessed | tf_op | source)
XLA Modules:
  0.0 285.1 jit_solution(7656035411320875463)
XLA Ops:
  0.6 1.7 slice_maximum_fusion
  2.7 4.6 %collective-permute-start = (f32[2,2,50,8,5]{2,3,4,1,0:T(8,128)S(1)}, f32[2,2,50,8,5]{2,3,4,1,0:T(8,128)S(1)}, u32[]{:S(2)}, u32[]{:S(2)}) collective-permute-start(f32[2,2,50,8,5]{2,3,4,1,0:T(8,128)S(1)} %copy.85), channel_id=1, source_target_pairs={{0,16},{16,32},{32,48},{48,64},{64,80},{80,96},{96,112},{1,17},{17... | collective-permute-start | bytes 96008 | tf_op jit(solution)/shard_map/ppermute | solution.py:24
  7.7 1.9 collective-permute-start.1
  9.7 0.4 copy.68
  10.1 3.4 %collective-permute-done.1 = f32[2,2,50,8,5]{2,3,4,1,0:T(8,128)S(1)} collective-permute-done((f32[2,2,50,8,5]{2,3,4,1,0:T(8,128)S(1)}, f32[2,2,50,8,5]{2,3,4,1,0:T(8,128)S(1)}, u32[]{:S(2)}, u32[]{:S(2)}) %collective-permute-start.1) | collective-permute-done | bytes 32032 | tf_op jit(solution)/shard_map/ppermute | solution.py:25
  13.5 0.4 copy.69
  13.9 0.7 pad_maximum_fusion.2
  14.9 0.8 copy.71
  15.8 6.0 %collective-permute-start.3 = (f32[2,2,50,5,138]{4,1,3,2,0:T(2,128)S(1)}, f32[2,2,50,5,138]{4,1,3,2,0:T(2,128)}, u32[]{:S(2)}, u32[]{:S(2)}) collective-permute-start(f32[2,2,50,5,138]{4,1,3,2,0:T(2,128)S(1)} %copy.71), channel_id=1, source_target_pairs={{1,0},{2,1},{3,2},{4,3},{5,4},{6,5},{7,6},{8,7},{9,8},{10,9},{11,1... | collective-permute-start | bytes 1656008 | tf_op jit(solution)/shard_map/ppermute | solution.py:25
  21.8 1.8 copy.70
  23.8 18.3 %collective-permute-done.3 = f32[2,2,50,5,138]{4,1,3,2,0:T(2,128)} collective-permute-done((f32[2,2,50,5,138]{4,1,3,2,0:T(2,128)S(1)}, f32[2,2,50,5,138]{4,1,3,2,0:T(2,128)}, u32[]{:S(2)}, u32[]{:S(2)}) %collective-permute-start.3) | collective-permute-done | bytes 552032 | tf_op jit(solution)/shard_map/ppermute | solution.py:25
  42.1 1.4 copy.73
  43.5 6.2 %collective-permute-done.2 = f32[2,2,50,5,138]{4,1,3,2,0:T(2,128)} collective-permute-done((f32[2,2,50,5,138]{4,1,3,2,0:T(2,128)}, f32[2,2,50,5,138]{4,1,3,2,0:T(2,128)}, u32[]{:S(2)}, u32[]{:S(2)}) %collective-permute-start.2) | collective-permute-done | bytes 552032 | tf_op jit(solution)/shard_map/ppermute | solution.py:24
  49.8 1.4 copy.72
  51.2 2.5 pad_maximum_fusion
  54.0 0.5 slice.114
  54.5 1.3 pad.25.field_ref
  55.8 1.8 fusion
  57.6 1.4 pad.29.west_ref
  59.0 1.3 pad.28.east_ref
  60.3 1.3 pad.27.south_ref
  61.6 1.3 pad.26.north_ref
  62.9 42.0 %shard_map.121 = f32[100,8,128]{2,1,0:T(8,128)} custom-call(f32[100,16,256]{2,1,0:T(8,128)} %pad.25.field_ref, f32[100,16,256]{2,1,0:T(8,128)} %pad.26.north_ref, f32[100,16,256]{2,1,0:T(8,128)} %pad.27.south_ref, f32[100,16,256]{2,1,0:T(8,128)} %pad.28.east_ref, f32[100,16,256]{2,1,0:T(8,128)} %pad.29.west_ref), custom_call_target="tpu_custom_call" | custom-call | flops 22937600 | bytes 9830400 | tf_op jit(solution)/shard_map/pallas_call | solution.py:81
  105.0 1.0 multiply_bitcast_fusion
  106.4 1.0 select_maximum_fusion
  107.5 25.0 %shard_map.122 = f32[2,128,128]{2,1,0:T(8,128)} custom-call(f32[512,400]{1,0:T(8,128)} %bitcast.67, s32[128,128]{1,0:T(8,128)} %cell_ref.3, f32[128,4,128]{2,1,0:T(4,128)} %weight_ref.3, f32[2,128,128]{2,1,0:T(8,128)} %scale_ref.1), custom_call_target="tpu_custom_call" | custom-call | flops 13421772800 | bytes 4194304 | tf_op jit(solution)/shard_map/pallas_call | solution.py:184
  132.5 1.3 convolution_bitcast_fusion
  134.0 17.1 %all_to_all.10 = f32[2,256,128]{2,0,1:T(2,128)S(1)} all-to-all(f32[2,256,128]{2,0,1:T(2,128)S(1)} %copy.76), channel_id=1, replica_groups=mesh['lat'=8,'lon'=16] {'lat','lon'}, dimensions={1} | all-to-all | bytes 524288 | tf_op jit(solution)/shard_map/all_to_all | solution.py:343
  151.7 15.2 %all_to_all.11 = f32[2,256,128]{2,0,1:T(2,128)S(1)} all-to-all(f32[2,256,128]{2,0,1:T(2,128)S(1)} %copy.78), channel_id=1, replica_groups=mesh['lat'=8,'lon'=16] {'lat','lon'}, dimensions={1} | all-to-all | bytes 524288 | tf_op jit(solution)/shard_map/all_to_all | solution.py:341
  167.0 0.9 fusion.4.value_ref
  167.9 18.4 %shard_map.123 = f32[2,400,128]{2,1,0:T(8,128)} custom-call(f32[2,128,128]{2,1,0:T(8,128)} %fusion.4.value_ref, s32[128,128]{1,0:T(8,128)} %cell_ref.3, f32[128,4,128]{2,1,0:T(4,128)} %weight_ref.3), custom_call_target="tpu_custom_call" | custom-call | flops 13421772800 | bytes 4194304 | tf_op jit(solution)/shard_map/pallas_call | solution.py:206
  186.3 1.1 copy_multiply_fusion
  187.6 2.6 collective-permute-start.4
  190.3 1.9 collective-permute-start.5
  192.2 3.5 %collective-permute-done.4 = f32[2,50,8,4]{3,1,2,0:T(8,128)S(1)} collective-permute-done((f32[2,50,8,4]{3,1,2,0:T(8,128)S(1)}, f32[2,50,8,4]{3,1,2,0:T(8,128)S(1)}, u32[]{:S(2)}, u32[]{:S(2)}) %collective-permute-start.4) | collective-permute-done | bytes 12832 | tf_op jit(solution)/shard_map/ppermute | solution.py:24
  195.7 4.7 %collective-permute-done.5 = f32[2,50,8,4]{3,1,2,0:T(8,128)S(1)} collective-permute-done((f32[2,50,8,4]{3,1,2,0:T(8,128)S(1)}, f32[2,50,8,4]{3,1,2,0:T(8,128)S(1)}, u32[]{:S(2)}, u32[]{:S(2)}) %collective-permute-start.5) | collective-permute-done | bytes 12832 | tf_op jit(solution)/shard_map/ppermute | solution.py:25
  201.3 4.5 %collective-permute-start.7 = (f32[2,50,4,136]{3,1,2,0:T(8,128)S(1)}, f32[2,50,4,136]{3,1,2,0:T(8,128)S(1)}, u32[]{:S(2)}, u32[]{:S(2)}) collective-permute-start(f32[2,50,4,136]{3,1,2,0:T(8,128)S(1)} %get-tuple-element.31), channel_id=1, source_target_pairs={{1,0},{2,1},{3,2},{4,3},{5,4},{6,5},{7,6},{8,7},{9,8},{10,9},{11,1... | collective-permute-start | bytes 652808 | tf_op jit(solution)/shard_map/ppermute | solution.py:25
  205.7 5.9 %collective-permute-done.6 = f32[2,50,4,136]{3,1,2,0:T(8,128)S(1)} collective-permute-done((f32[2,50,4,136]{3,1,2,0:T(8,128)S(1)}, f32[2,50,4,136]{3,1,2,0:T(8,128)S(1)}, u32[]{:S(2)}, u32[]{:S(2)}) %collective-permute-start.6) | collective-permute-done | bytes 217632 | tf_op jit(solution)/shard_map/ppermute | solution.py:24
  211.6 0.4 pad_maximum_fusion.1
  212.0 0.5 copy.82
  212.5 1.3 pad.30.field_ref
  213.9 42.0 %shard_map.124 = f32[100,8,128]{2,1,0:T(8,128)} custom-call(f32[100,16,256]{2,1,0:T(8,128)} %pad.30.field_ref, f32[100,16,256]{2,1,0:T(8,128)} %pad.26.north_ref, f32[100,16,256]{2,1,0:T(8,128)} %pad.27.south_ref, f32[100,16,256]{2,1,0:T(8,128)} %pad.28.east_ref, f32[100,16,256]{2,1,0:T(8,128)} %pad.29.west_ref), custom_call_target="tpu_custom_call" | custom-call | flops 22937600 | bytes 9830400 | tf_op jit(solution)/shard_map/pallas_call | solution.py:81
  255.9 1.9 multiply_reduce_fusion.3
  257.8 2.6 maximum_bitcast_fusion
  260.4 0.6 scatter.4.part_ref
  261.0 17.7 %shard_map.125 = f32[8,128]{1,0:T(8,128)} custom-call(f32[8,128]{1,0:T(8,128)} %scatter.4.part_ref), custom_call_target="tpu_custom_call" | custom-call | tf_op jit(solution)/shard_map/pallas_call | solution.py:278
  278.6 1.4 fusion.20
  284.0 1.1 multiply_add_fusion
  (35 shorter events, 3.9 us)
Async XLA Ops:
  0.6 150.5 %copy-start = (f32[128,128]{1,0:T(8,128)S(1)}, f32[128,128]{1,0:T(8,128)}, u32[]{:S(2)}) copy-start(f32[128,128]{1,0:T(8,128)} %param.21) | copy-start | bytes 196612
  2.3 11.6 %copy-start.1 = (f32[2,50,8,128]{3,2,1,0:T(8,128)S(1)}, f32[2,50,8,128]{3,2,1,0:T(8,128)}, u32[]{:S(2)}) copy-start(f32[2,50,8,128]{3,2,1,0:T(8,128)} %param.14) | copy-start | bytes 1228804
  2.3 11.6 %copy-start.2 = (f32[2,50,8,128]{3,2,1,0:T(8,128)S(1)}, f32[2,50,8,128]{3,2,1,0:T(8,128)}, u32[]{:S(2)}) copy-start(f32[2,50,8,128]{3,2,1,0:T(8,128)} %param.15) | copy-start | bytes 1228804
  2.7 6.9 %collective-permute-start = (f32[2,2,50,8,5]{2,3,4,1,0:T(8,128)S(1)}, f32[2,2,50,8,5]{2,3,4,1,0:T(8,128)S(1)}, u32[]{:S(2)}, u32[]{:S(2)}) collective-permute-start(f32[2,2,50,8,5]{2,3,4,1,0:T(8,128)S(1)} %copy.85), channel_id=1, source_target_pairs={{0,16},{16,32},{32,48},{48,64},{64,80},{80,96},{96,112},{1,17},{17... | collective-permute-start | bytes 96008 | tf_op jit(solution)/shard_map/ppermute | solution.py:24
  7.7 5.8 %collective-permute-start.1 = (f32[2,2,50,8,5]{2,3,4,1,0:T(8,128)S(1)}, f32[2,2,50,8,5]{2,3,4,1,0:T(8,128)S(1)}, u32[]{:S(2)}, u32[]{:S(2)}) collective-permute-start(f32[2,2,50,8,5]{2,3,4,1,0:T(8,128)S(1)} %copy.86), channel_id=1, source_target_pairs={{16,0},{32,16},{48,32},{64,48},{80,64},{96,80},{112,96},{17,1},{33... | collective-permute-start | bytes 96008 | tf_op jit(solution)/shard_map/ppermute | solution.py:25
  15.7 7.9 %copy-start.7 = (s32[128,1]{0,1:T(1,128)S(1)}, s32[128,1]{0,1:T(1,128)}, u32[]{:S(2)}) copy-start(s32[128,1]{0,1:T(1,128)} %param.20) | copy-start | bytes 1540
  15.8 26.4 %collective-permute-start.3 = (f32[2,2,50,5,138]{4,1,3,2,0:T(2,128)S(1)}, f32[2,2,50,5,138]{4,1,3,2,0:T(2,128)}, u32[]{:S(2)}, u32[]{:S(2)}) collective-permute-start(f32[2,2,50,5,138]{4,1,3,2,0:T(2,128)S(1)} %copy.71), channel_id=1, source_target_pairs={{1,0},{2,1},{3,2},{4,3},{5,4},{6,5},{7,6},{8,7},{9,8},{10,9},{11,1... | collective-permute-start | bytes 1656008 | tf_op jit(solution)/shard_map/ppermute | solution.py:25
  23.6 26.2 %collective-permute-start.2 = (f32[2,2,50,5,138]{4,1,3,2,0:T(2,128)}, f32[2,2,50,5,138]{4,1,3,2,0:T(2,128)}, u32[]{:S(2)}, u32[]{:S(2)}) collective-permute-start(f32[2,2,50,5,138]{4,1,3,2,0:T(2,128)} %copy.70), channel_id=1, source_target_pairs={{0,1},{1,2},{2,3},{3,4},{4,5},{5,6},{6,7},{7,8},{8,9},{9,10},{10,1... | collective-permute-start | bytes 1656008 | tf_op jit(solution)/shard_map/ppermute | solution.py:24
  62.9 42.0 %copy-start.3 = (f32[2,50,8,128]{3,2,1,0:T(8,128)S(1)}, f32[2,50,8,128]{3,2,1,0:T(8,128)}, u32[]{:S(2)}) copy-start(f32[2,50,8,128]{3,2,1,0:T(8,128)} %param.16) | copy-start | bytes 1228804
  132.5 34.5 %copy-start.6 = (f32[2,128,128]{2,1,0:T(8,128)S(1)}, f32[2,128,128]{2,1,0:T(8,128)}, u32[]{:S(2)}) copy-start(f32[2,128,128]{2,1,0:T(8,128)} %scale_ref.1) | copy-start | bytes 393220
  187.6 8.0 %collective-permute-start.4 = (f32[2,50,8,4]{3,1,2,0:T(8,128)S(1)}, f32[2,50,8,4]{3,1,2,0:T(8,128)S(1)}, u32[]{:S(2)}, u32[]{:S(2)}) collective-permute-start(f32[2,50,8,4]{3,1,2,0:T(8,128)S(1)} %get-tuple-element.34), channel_id=1, source_target_pairs={{0,16},{16,32},{32,48},{48,64},{64,80},{80,96},{96,112},{1,17},{17... | collective-permute-start | bytes 38408 | tf_op jit(solution)/shard_map/ppermute | solution.py:24
  190.3 10.1 %collective-permute-start.5 = (f32[2,50,8,4]{3,1,2,0:T(8,128)S(1)}, f32[2,50,8,4]{3,1,2,0:T(8,128)S(1)}, u32[]{:S(2)}, u32[]{:S(2)}) collective-permute-start(f32[2,50,8,4]{3,1,2,0:T(8,128)S(1)} %get-tuple-element.35), channel_id=1, source_target_pairs={{16,0},{32,16},{48,32},{64,48},{80,64},{96,80},{112,96},{17,1},{33... | collective-permute-start | bytes 38408 | tf_op jit(solution)/shard_map/ppermute | solution.py:25
  200.9 10.7 %collective-permute-start.6 = (f32[2,50,4,136]{3,1,2,0:T(8,128)S(1)}, f32[2,50,4,136]{3,1,2,0:T(8,128)S(1)}, u32[]{:S(2)}, u32[]{:S(2)}) collective-permute-start(f32[2,50,4,136]{3,1,2,0:T(8,128)S(1)} %get-tuple-element.30), channel_id=1, source_target_pairs={{0,1},{1,2},{2,3},{3,4},{4,5},{5,6},{6,7},{7,8},{8,9},{9,10},{10,1... | collective-permute-start | bytes 652808 | tf_op jit(solution)/shard_map/ppermute | solution.py:24
  201.3 10.3 %collective-permute-start.7 = (f32[2,50,4,136]{3,1,2,0:T(8,128)S(1)}, f32[2,50,4,136]{3,1,2,0:T(8,128)S(1)}, u32[]{:S(2)}, u32[]{:S(2)}) collective-permute-start(f32[2,50,4,136]{3,1,2,0:T(8,128)S(1)} %get-tuple-element.31), channel_id=1, source_target_pairs={{1,0},{2,1},{3,2},{4,3},{5,4},{6,5},{7,6},{8,7},{9,8},{10,9},{11,1... | collective-permute-start | bytes 652808 | tf_op jit(solution)/shard_map/ppermute | solution.py:25
  213.9 42.0 %copy-start.4 = (f32[2,50,8,128]{3,2,1,0:T(8,128)S(1)}, f32[2,50,8,128]{3,2,1,0:T(8,128)}, u32[]{:S(2)}) copy-start(f32[2,50,8,128]{3,2,1,0:T(8,128)} %param.13) | copy-start | bytes 1228804
  255.9 28.1 %copy-start.5 = (f32[2,50,8,128]{3,2,1,0:T(8,128)S(1)}, f32[2,50,8,128]{3,2,1,0:T(8,128)}, u32[]{:S(2)}) copy-start(f32[2,50,8,128]{3,2,1,0:T(8,128)} %param.12) | copy-start | bytes 1228804

commit v3 on v0

--- a/solution.py
+++ b/solution.py
@@ -166,7 +166,7 @@
             out_ref[v] = summed[:, v * lat_count : (v + 1) * lat_count]
 
 
-def observe_pallas(field, stencil, bilinear, obs_weight, group=16):
+def observe_pallas(field, stencil, bilinear, obs_weight, group=32):
     var_count, level_count, lon_count, lat_count = field.shape
     row_count = level_count * lon_count
     block_count = stencil.shape[0]
@@ -191,7 +191,7 @@
     )(table, stencil, bilinear, obs_weight)
 
 
-def spread_pallas(values, stencil, bilinear, field_shape, group=16):
+def spread_pallas(values, stencil, bilinear, field_shape, group=32):
     var_count, level_count, lon_count, lat_count = field_shape
     row_count = level_count * lon_count
     block_count = stencil.shape[0]

time: 218 us -> 217 us (level)
  no operation moved by 1% of the time
where the time goes in v3:
time: 217 us; the launch traced here: 216 us
  Pallas kernels  75.6 us (35%)
  waiting for transfers between devices  41.9 us (19%)
  blocking collectives  32.4 us (15%)
  starting transfers between devices  22.2 us (10%)
  local copies, waits for them, and re-layouts  19.9 us (9%)
  other arithmetic  16.3 us (8%)
  between operations  4.79 us (2%)
  matrix products  2.8 us (1%)
    ppermute x4, waiting for transfers between devices, widen_halo(): lax.ppermute(lax.slice_in_dim(value, 0, width, axis=dim), axis, down)  26.4 us
    pallas_call x1, Pallas kernels, observe_pallas(): pl.pallas_call(kernel, grid=(block_count // group,), in_specs=[pl.BlockSp...  24.2 us
    pallas_call x1, Pallas kernels, allreduce_pallas(): pl.pallas_call(kernel, in_specs=[pl.BlockSpec(memory_space=pltpu.VMEM)],...  17.6 us
    pallas_call x1, Pallas kernels, spread_pallas(): pl.pallas_call(kernel, grid=(block_count // group,), in_specs=[pl.BlockSp...  17.5 us
    all_to_all x1, blocking collectives, shards(): lax.all_to_all(buffer, ('lat', 'lon'), split_axis=1, concat_axis=1, tiled...  17.1 us
    pallas_call x2, Pallas kernels, diffuse(): pl.pallas_call(functools.partial(diffuse_kernel, STEPS), grid=(planes //...  16.3 us
    ppermute x4, waiting for transfers between devices, widen_halo(): lax.ppermute(lax.slice_in_dim(value, length - width, length, axis=dim), a...  15.5 us
    all_to_all x1, blocking collectives, shards(): lax.all_to_all(mix_blocks(lax.all_to_all(buffer, ('lat', 'lon'), split_ax...  15.2 us
  transfers between devices with their start and end apart: 8, of which 6 were waited for; matrix products, arithmetic and copies ran while one was open for 2% of the time, Pallas kernels for 0%

profile of v3, /device:TPU:1, one launch (start us, length us, event | category | flops | bytes accessed | tf_op | source)
XLA Modules:
  0.0 215.8 jit_solution(950929773781931776)
XLA Ops:
  0.6 1.7 slice_maximum_fusion
  2.7 4.6 %collective-permute-start = (f32[2,2,50,8,5]{2,3,4,1,0:T(8,128)S(1)}, f32[2,2,50,8,5]{2,3,4,1,0:T(8,128)S(1)}, u32[]{:S(2)}, u32[]{:S(2)}) collective-permute-start(f32[2,2,50,8,5]{2,3,4,1,0:T(8,128)S(1)} %copy.85), channel_id=1, source_target_pairs={{0,16},{16,32},{32,48},{48,64},{64,80},{80,96},{96,112},{1,17},{17... | collective-permute-start | bytes 96008 | tf_op jit(solution)/shard_map/ppermute | solution.py:24
  7.7 1.9 collective-permute-start.1
  9.7 0.4 copy.68
  10.1 3.4 %collective-permute-done.1 = f32[2,2,50,8,5]{2,3,4,1,0:T(8,128)S(1)} collective-permute-done((f32[2,2,50,8,5]{2,3,4,1,0:T(8,128)S(1)}, f32[2,2,50,8,5]{2,3,4,1,0:T(8,128)S(1)}, u32[]{:S(2)}, u32[]{:S(2)}) %collective-permute-start.1) | collective-permute-done | bytes 32032 | tf_op jit(solution)/shard_map/ppermute | solution.py:25
  13.9 0.7 pad_maximum_fusion.2
  14.9 0.8 copy.71
  15.8 6.0 %collective-permute-start.3 = (f32[2,2,50,5,138]{4,1,3,2,0:T(2,128)S(1)}, f32[2,2,50,5,138]{4,1,3,2,0:T(2,128)}, u32[]{:S(2)}, u32[]{:S(2)}) collective-permute-start(f32[2,2,50,5,138]{4,1,3,2,0:T(2,128)S(1)} %copy.71), channel_id=1, source_target_pairs={{1,0},{2,1},{3,2},{4,3},{5,4},{6,5},{7,6},{8,7},{9,8},{10,9},{11,1... | collective-permute-start | bytes 1656008 | tf_op jit(solution)/shard_map/ppermute | solution.py:25
  21.8 1.8 copy.70
  23.8 18.3 %collective-permute-done.3 = f32[2,2,50,5,138]{4,1,3,2,0:T(2,128)} collective-permute-done((f32[2,2,50,5,138]{4,1,3,2,0:T(2,128)S(1)}, f32[2,2,50,5,138]{4,1,3,2,0:T(2,128)}, u32[]{:S(2)}, u32[]{:S(2)}) %collective-permute-start.3) | collective-permute-done | bytes 552032 | tf_op jit(solution)/shard_map/ppermute | solution.py:25
  42.1 1.4 copy.73
  43.5 6.2 %collective-permute-done.2 = f32[2,2,50,5,138]{4,1,3,2,0:T(2,128)} collective-permute-done((f32[2,2,50,5,138]{4,1,3,2,0:T(2,128)}, f32[2,2,50,5,138]{4,1,3,2,0:T(2,128)}, u32[]{:S(2)}, u32[]{:S(2)}) %collective-permute-start.2) | collective-permute-done | bytes 552032 | tf_op jit(solution)/shard_map/ppermute | solution.py:24
  49.8 1.4 copy.72
  51.2 2.5 %pad_maximum_fusion = f32[2,2,50,18,138]{4,3,2,1,0:T(8,128)S(1)} fusion(f32[2,2,50,5,138]{4,3,2,1,0:T(8,128)S(1)} %copy.73, f32[2,2,50,8,5]{4,3,2,1,0:T(8,128)S(1)} %copy.69, f32[1,2,50,8,128]{4,3,2,1,0:T(8,128)S(1)} %bitcast.64, f32[1,2,50,8,128]{4,3,2,1,0:T(8,128)S(1)} %bitcast.53, f32[2,2,50,8,5]{4,3,2,1,0:T(8,128)S(1)} %copy.68, ...), kind=kLoop, calls=%fused_computation | loop fusion | flops 2484000 | bytes 3974400 | tf_op jit(solution)/shard_map/concatenate | solution.py:26
  54.0 0.5 slice.114
  54.5 1.3 pad.25.field_ref
  55.8 1.8 fusion
  57.6 1.4 pad.29.west_ref
  59.0 1.3 pad.28.east_ref
  60.3 1.3 pad.27.south_ref
  61.6 1.3 pad.26.north_ref
  62.9 8.2 %shard_map.121 = f32[100,8,128]{2,1,0:T(8,128)} custom-call(f32[100,16,256]{2,1,0:T(8,128)} %pad.25.field_ref, f32[100,16,256]{2,1,0:T(8,128)} %pad.26.north_ref, f32[100,16,256]{2,1,0:T(8,128)} %pad.27.south_ref, f32[100,16,256]{2,1,0:T(8,128)} %pad.28.east_ref, f32[100,16,256]{2,1,0:T(8,128)} %pad.29.west_ref), custom_call_target="tpu_custom_call" | custom-call | flops 22937600 | bytes 9830400 | tf_op jit(solution)/shard_map/pallas_call | solution.py:76
  71.1 1.0 multiply_bitcast_fusion
  72.6 1.0 select_maximum_fusion
  73.6 24.2 %shard_map.122 = f32[2,128,128]{2,1,0:T(8,128)} custom-call(f32[512,400]{1,0:T(8,128)} %bitcast.67, s32[128,128]{1,0:T(8,128)} %cell_ref.3, f32[128,4,128]{2,1,0:T(4,128)} %weight_ref.3, f32[2,128,128]{2,1,0:T(8,128)} %scale_ref.1), custom_call_target="tpu_custom_call" | custom-call | flops 13421772800 | bytes 4194304 | tf_op jit(solution)/shard_map/pallas_call | solution.py:179
  97.8 1.3 convolution_bitcast_fusion
  99.3 17.1 %all_to_all.10 = f32[2,256,128]{2,0,1:T(2,128)S(1)} all-to-all(f32[2,256,128]{2,0,1:T(2,128)S(1)} %copy.76), channel_id=1, replica_groups=mesh['lat'=8,'lon'=16] {'lat','lon'}, dimensions={1} | all-to-all | bytes 524288 | tf_op jit(solution)/shard_map/all_to_all | solution.py:338
  117.1 15.2 %all_to_all.11 = f32[2,256,128]{2,0,1:T(2,128)S(1)} all-to-all(f32[2,256,128]{2,0,1:T(2,128)S(1)} %copy.78), channel_id=1, replica_groups=mesh['lat'=8,'lon'=16] {'lat','lon'}, dimensions={1} | all-to-all | bytes 524288 | tf_op jit(solution)/shard_map/all_to_all | solution.py:336
  132.3 0.9 fusion.4.value_ref
  133.2 17.5 %shard_map.123 = f32[2,400,128]{2,1,0:T(8,128)} custom-call(f32[2,128,128]{2,1,0:T(8,128)} %fusion.4.value_ref, s32[128,128]{1,0:T(8,128)} %cell_ref.3, f32[128,4,128]{2,1,0:T(4,128)} %weight_ref.3), custom_call_target="tpu_custom_call" | custom-call | flops 13421772800 | bytes 4194304 | tf_op jit(solution)/shard_map/pallas_call | solution.py:201
  150.7 1.1 copy_multiply_fusion
  152.0 2.6 %collective-permute-start.4 = (f32[2,50,8,4]{3,1,2,0:T(8,128)S(1)}, f32[2,50,8,4]{3,1,2,0:T(8,128)S(1)}, u32[]{:S(2)}, u32[]{:S(2)}) collective-permute-start(f32[2,50,8,4]{3,1,2,0:T(8,128)S(1)} %get-tuple-element.34), channel_id=1, source_target_pairs={{0,16},{16,32},{32,48},{48,64},{64,80},{80,96},{96,112},{1,17},{17... | collective-permute-start | bytes 38408 | tf_op jit(solution)/shard_map/ppermute | solution.py:24
  154.6 1.9 collective-permute-start.5
  156.6 3.5 %collective-permute-done.4 = f32[2,50,8,4]{3,1,2,0:T(8,128)S(1)} collective-permute-done((f32[2,50,8,4]{3,1,2,0:T(8,128)S(1)}, f32[2,50,8,4]{3,1,2,0:T(8,128)S(1)}, u32[]{:S(2)}, u32[]{:S(2)}) %collective-permute-start.4) | collective-permute-done | bytes 12832 | tf_op jit(solution)/shard_map/ppermute | solution.py:24
  160.0 4.7 %collective-permute-done.5 = f32[2,50,8,4]{3,1,2,0:T(8,128)S(1)} collective-permute-done((f32[2,50,8,4]{3,1,2,0:T(8,128)S(1)}, f32[2,50,8,4]{3,1,2,0:T(8,128)S(1)}, u32[]{:S(2)}, u32[]{:S(2)}) %collective-permute-start.5) | collective-permute-done | bytes 12832 | tf_op jit(solution)/shard_map/ppermute | solution.py:25
  165.2 0.7 collective-permute-start.6
  165.9 4.5 %collective-permute-start.7 = (f32[2,50,4,136]{3,1,2,0:T(8,128)S(1)}, f32[2,50,4,136]{3,1,2,0:T(8,128)S(1)}, u32[]{:S(2)}, u32[]{:S(2)}) collective-permute-start(f32[2,50,4,136]{3,1,2,0:T(8,128)S(1)} %get-tuple-element.31), channel_id=1, source_target_pairs={{1,0},{2,1},{3,2},{4,3},{5,4},{6,5},{7,6},{8,7},{9,8},{10,9},{11,1... | collective-permute-start | bytes 652808 | tf_op jit(solution)/shard_map/ppermute | solution.py:25
  170.4 5.9 %collective-permute-done.6 = f32[2,50,4,136]{3,1,2,0:T(8,128)S(1)} collective-permute-done((f32[2,50,4,136]{3,1,2,0:T(8,128)S(1)}, f32[2,50,4,136]{3,1,2,0:T(8,128)S(1)}, u32[]{:S(2)}, u32[]{:S(2)}) %collective-permute-start.6) | collective-permute-done | bytes 217632 | tf_op jit(solution)/shard_map/ppermute | solution.py:24
  176.2 0.4 pad_maximum_fusion.1
  176.7 0.5 copy.82
  177.2 1.3 pad.30.field_ref
  178.5 8.2 %shard_map.124 = f32[100,8,128]{2,1,0:T(8,128)} custom-call(f32[100,16,256]{2,1,0:T(8,128)} %pad.30.field_ref, f32[100,16,256]{2,1,0:T(8,128)} %pad.26.north_ref, f32[100,16,256]{2,1,0:T(8,128)} %pad.27.south_ref, f32[100,16,256]{2,1,0:T(8,128)} %pad.28.east_ref, f32[100,16,256]{2,1,0:T(8,128)} %pad.29.west_ref), custom_call_target="tpu_custom_call" | custom-call | flops 22937600 | bytes 9830400 | tf_op jit(solution)/shard_map/pallas_call | solution.py:76
  186.7 1.9 multiply_reduce_fusion.3
  188.5 2.6 %maximum_bitcast_fusion = f32[1,4]{1,0:T(1,128)S(1)} fusion(f32[1]{0:T(128)} %bitcast.27, f32[1]{0:T(128)} %bitcast.26, f32[1]{0:T(128)} %bitcast.25, f32[1]{0:T(128)} %bitcast), kind=kLoop, calls=%fused_computation.44 | loop fusion | flops 12 | bytes 32 | tf_op jit(solution)/shard_map/reshape.49
  191.2 0.6 scatter.4.part_ref
  191.8 17.6 %shard_map.125 = f32[8,128]{1,0:T(8,128)} custom-call(f32[8,128]{1,0:T(8,128)} %scatter.4.part_ref), custom_call_target="tpu_custom_call" | custom-call | tf_op jit(solution)/shard_map/pallas_call | solution.py:273
  209.4 1.4 fusion.20
  214.7 1.1 multiply_add_fusion
  (35 shorter events, 3.9 us)
Async XLA Ops:
  0.6 115.8 %copy-start = (f32[128,128]{1,0:T(8,128)S(1)}, f32[128,128]{1,0:T(8,128)}, u32[]{:S(2)}) copy-start(f32[128,128]{1,0:T(8,128)} %param.21) | copy-start | bytes 196612
  2.3 11.6 %copy-start.1 = (f32[2,50,8,128]{3,2,1,0:T(8,128)S(1)}, f32[2,50,8,128]{3,2,1,0:T(8,128)}, u32[]{:S(2)}) copy-start(f32[2,50,8,128]{3,2,1,0:T(8,128)} %param.14) | copy-start | bytes 1228804
  2.3 11.6 %copy-start.2 = (f32[2,50,8,128]{3,2,1,0:T(8,128)S(1)}, f32[2,50,8,128]{3,2,1,0:T(8,128)}, u32[]{:S(2)}) copy-start(f32[2,50,8,128]{3,2,1,0:T(8,128)} %param.15) | copy-start | bytes 1228804
  2.7 6.9 %collective-permute-start = (f32[2,2,50,8,5]{2,3,4,1,0:T(8,128)S(1)}, f32[2,2,50,8,5]{2,3,4,1,0:T(8,128)S(1)}, u32[]{:S(2)}, u32[]{:S(2)}) collective-permute-start(f32[2,2,50,8,5]{2,3,4,1,0:T(8,128)S(1)} %copy.85), channel_id=1, source_target_pairs={{0,16},{16,32},{32,48},{48,64},{64,80},{80,96},{96,112},{1,17},{17... | collective-permute-start | bytes 96008 | tf_op jit(solution)/shard_map/ppermute | solution.py:24
  7.7 5.8 %collective-permute-start.1 = (f32[2,2,50,8,5]{2,3,4,1,0:T(8,128)S(1)}, f32[2,2,50,8,5]{2,3,4,1,0:T(8,128)S(1)}, u32[]{:S(2)}, u32[]{:S(2)}) collective-permute-start(f32[2,2,50,8,5]{2,3,4,1,0:T(8,128)S(1)} %copy.86), channel_id=1, source_target_pairs={{16,0},{32,16},{48,32},{64,48},{80,64},{96,80},{112,96},{17,1},{33... | collective-permute-start | bytes 96008 | tf_op jit(solution)/shard_map/ppermute | solution.py:25
  15.7 7.9 %copy-start.7 = (s32[128,1]{0,1:T(1,128)S(1)}, s32[128,1]{0,1:T(1,128)}, u32[]{:S(2)}) copy-start(s32[128,1]{0,1:T(1,128)} %param.20) | copy-start | bytes 1540
  15.8 26.4 %collective-permute-start.3 = (f32[2,2,50,5,138]{4,1,3,2,0:T(2,128)S(1)}, f32[2,2,50,5,138]{4,1,3,2,0:T(2,128)}, u32[]{:S(2)}, u32[]{:S(2)}) collective-permute-start(f32[2,2,50,5,138]{4,1,3,2,0:T(2,128)S(1)} %copy.71), channel_id=1, source_target_pairs={{1,0},{2,1},{3,2},{4,3},{5,4},{6,5},{7,6},{8,7},{9,8},{10,9},{11,1... | collective-permute-start | bytes 1656008 | tf_op jit(solution)/shard_map/ppermute | solution.py:25
  23.6 26.2 %collective-permute-start.2 = (f32[2,2,50,5,138]{4,1,3,2,0:T(2,128)}, f32[2,2,50,5,138]{4,1,3,2,0:T(2,128)}, u32[]{:S(2)}, u32[]{:S(2)}) collective-permute-start(f32[2,2,50,5,138]{4,1,3,2,0:T(2,128)} %copy.70), channel_id=1, source_target_pairs={{0,1},{1,2},{2,3},{3,4},{4,5},{5,6},{6,7},{7,8},{8,9},{9,10},{10,1... | collective-permute-start | bytes 1656008 | tf_op jit(solution)/shard_map/ppermute | solution.py:24
  62.9 8.2 %copy-start.3 = (f32[2,50,8,128]{3,2,1,0:T(8,128)S(1)}, f32[2,50,8,128]{3,2,1,0:T(8,128)}, u32[]{:S(2)}) copy-start(f32[2,50,8,128]{3,2,1,0:T(8,128)} %param.16) | copy-start | bytes 1228804
  97.8 34.5 %copy-start.6 = (f32[2,128,128]{2,1,0:T(8,128)S(1)}, f32[2,128,128]{2,1,0:T(8,128)}, u32[]{:S(2)}) copy-start(f32[2,128,128]{2,1,0:T(8,128)} %scale_ref.1) | copy-start | bytes 393220
  152.0 8.0 %collective-permute-start.4 = (f32[2,50,8,4]{3,1,2,0:T(8,128)S(1)}, f32[2,50,8,4]{3,1,2,0:T(8,128)S(1)}, u32[]{:S(2)}, u32[]{:S(2)}) collective-permute-start(f32[2,50,8,4]{3,1,2,0:T(8,128)S(1)} %get-tuple-element.34), channel_id=1, source_target_pairs={{0,16},{16,32},{32,48},{48,64},{64,80},{80,96},{96,112},{1,17},{17... | collective-permute-start | bytes 38408 | tf_op jit(solution)/shard_map/ppermute | solution.py:24
  154.6 10.1 %collective-permute-start.5 = (f32[2,50,8,4]{3,1,2,0:T(8,128)S(1)}, f32[2,50,8,4]{3,1,2,0:T(8,128)S(1)}, u32[]{:S(2)}, u32[]{:S(2)}) collective-permute-start(f32[2,50,8,4]{3,1,2,0:T(8,128)S(1)} %get-tuple-element.35), channel_id=1, source_target_pairs={{16,0},{32,16},{48,32},{64,48},{80,64},{96,80},{112,96},{17,1},{33... | collective-permute-start | bytes 38408 | tf_op jit(solution)/shard_map/ppermute | solution.py:25
  165.2 11.0 %collective-permute-start.6 = (f32[2,50,4,136]{3,1,2,0:T(8,128)S(1)}, f32[2,50,4,136]{3,1,2,0:T(8,128)S(1)}, u32[]{:S(2)}, u32[]{:S(2)}) collective-permute-start(f32[2,50,4,136]{3,1,2,0:T(8,128)S(1)} %get-tuple-element.30), channel_id=1, source_target_pairs={{0,1},{1,2},{2,3},{3,4},{4,5},{5,6},{6,7},{7,8},{8,9},{9,10},{10,1... | collective-permute-start | bytes 652808 | tf_op jit(solution)/shard_map/ppermute | solution.py:24
  165.9 10.3 %collective-permute-start.7 = (f32[2,50,4,136]{3,1,2,0:T(8,128)S(1)}, f32[2,50,4,136]{3,1,2,0:T(8,128)S(1)}, u32[]{:S(2)}, u32[]{:S(2)}) collective-permute-start(f32[2,50,4,136]{3,1,2,0:T(8,128)S(1)} %get-tuple-element.31), channel_id=1, source_target_pairs={{1,0},{2,1},{3,2},{4,3},{5,4},{6,5},{7,6},{8,7},{9,8},{10,9},{11,1... | collective-permute-start | bytes 652808 | tf_op jit(solution)/shard_map/ppermute | solution.py:25
  178.5 8.2 %copy-start.4 = (f32[2,50,8,128]{3,2,1,0:T(8,128)S(1)}, f32[2,50,8,128]{3,2,1,0:T(8,128)}, u32[]{:S(2)}) copy-start(f32[2,50,8,128]{3,2,1,0:T(8,128)} %param.13) | copy-start | bytes 1228804
  186.7 28.0 %copy-start.5 = (f32[2,50,8,128]{3,2,1,0:T(8,128)S(1)}, f32[2,50,8,128]{3,2,1,0:T(8,128)}, u32[]{:S(2)}) copy-start(f32[2,50,8,128]{3,2,1,0:T(8,128)} %param.12) | copy-start | bytes 1228804

commit v4 on v3

--- a/solution.py
+++ b/solution.py
@@ -28,6 +28,7 @@
 
 
 def face_coeffs(wide, width):
+    wide = jnp.pad(wide, ((0, 0), (0, 0), (1, 1), (1, 1)))
     lat_count = wide.shape[3] - 2 * (width + 1)
     lat_devices = lax.axis_size("lat")
     first = lax.axis_index("lat") * lat_count - width
@@ -319,7 +320,7 @@
     lat_devices = lax.axis_size("lat")
     lon_devices = lax.axis_size("lon")
     tile_count = lat_devices * lon_devices
-    both = widen_halo(jnp.stack([direction, diffusivity]), STEPS + 1)
+    both = widen_halo(jnp.stack([direction, diffusivity]), STEPS)
     coeffs = padded_coeffs(face_coeffs(both[1], STEPS))
 
     def apply_diffusion(field):
@@ -330,7 +331,7 @@
         jnp.float32
     )
     field_shape = direction.shape
-    state_field = deviation * diffuse(both[0][:, :, 1:-1, 1:-1], coeffs)
+    state_field = deviation * diffuse(both[0], coeffs)
     observed = observe_pallas(state_field, stencil, bilinear, obs_weight)
     buffer = jnp.einsum("vbk,bs->vsk", observed, slot_table, precision=precise)
     returned = lax.all_to_all(

time: 217 us -> 205 us (0.945)
  waiting for transfers between devices: 41.9 us -> 33.2 us
  local copies, waits for them, and re-layouts: 19.9 us -> 13.9 us
  blocking collectives: 32.4 us -> 37.2 us
    ppermute x4, waiting for transfers between devices: 26.4 us -> 7.9 us  [widen_halo(): lax.ppermute(lax.slice_in_dim(value, 0, width, axis=dim), axis, down)]
    ppermute x4, waiting for transfers between devices: 15.5 us -> 25.3 us  [widen_halo(): lax.ppermute(lax.slice_in_dim(value, length - width, length, axis=dim), a...]
    all_to_all x1, blocking collectives: 17.1 us -> 22 us  [shards(): lax.all_to_all(buffer, ('lat', 'lon'), split_axis=1, concat_axis=1, tiled...]
  transfers between devices with their start and end apart: 8 -> 8, of which waited for: 6 -> 5; matrix products, arithmetic and copies ran while one was open for 2% -> 0% of each run, Pallas kernels for 0% -> 0%
where the time goes in v4:
time: 205 us; the launch traced here: 204 us
  Pallas kernels  75.6 us (37%)
  blocking collectives  37.2 us (18%)
  waiting for transfers between devices  33.2 us (16%)
  starting transfers between devices  22 us (11%)
  other arithmetic  15 us (7%)
  local copies, waits for them, and re-layouts  13.9 us (7%)
  between operations  4.76 us (2%)
  matrix products  2.8 us (1%)
    ppermute x4, waiting for transfers between devices, widen_halo(): lax.ppermute(lax.slice_in_dim(value, length - width, length, axis=dim), a...  25.3 us
    pallas_call x1, Pallas kernels, observe_pallas(): pl.pallas_call(kernel, grid=(block_count // group,), in_specs=[pl.BlockSp...  24.2 us
    all_to_all x1, blocking collectives, shards(): lax.all_to_all(buffer, ('lat', 'lon'), split_axis=1, concat_axis=1, tiled...  22 us
    pallas_call x1, Pallas kernels, allreduce_pallas(): pl.pallas_call(kernel, in_specs=[pl.BlockSpec(memory_space=pltpu.VMEM)],...  17.6 us
    pallas_call x1, Pallas kernels, spread_pallas(): pl.pallas_call(kernel, grid=(block_count // group,), in_specs=[pl.BlockSp...  17.5 us
    pallas_call x2, Pallas kernels, diffuse(): pl.pallas_call(functools.partial(diffuse_kernel, STEPS), grid=(planes //...  16.3 us
    all_to_all x1, blocking collectives, shards(): lax.all_to_all(mix_blocks(lax.all_to_all(buffer, ('lat', 'lon'), split_ax...  15.2 us
    ppermute x4, starting transfers between devices, widen_halo(): lax.ppermute(lax.slice_in_dim(value, 0, width, axis=dim), axis, down)  13.1 us
  transfers between devices with their start and end apart: 8, of which 5 were waited for; matrix products, arithmetic and copies ran while one was open for 0% of the time, Pallas kernels for 0%

profile of v4, /device:TPU:1, one launch (start us, length us, event | category | flops | bytes accessed | tf_op | source)
XLA Modules:
  0.0 204.4 jit_solution(17631189224460898647)
XLA Ops:
  0.6 1.7 slice_maximum_fusion
  2.4 0.4 copy.52
  2.7 4.6 %collective-permute-start = (f32[2,2,50,8,4]{2,3,4,1,0:T(8,128)S(1)}, f32[2,2,50,8,4]{2,3,4,1,0:T(8,128)S(1)}, u32[]{:S(2)}, u32[]{:S(2)}) collective-permute-start(f32[2,2,50,8,4]{2,3,4,1,0:T(8,128)S(1)} %copy.52), channel_id=1, source_target_pairs={{0,16},{16,32},{32,48},{48,64},{64,80},{80,96},{96,112},{1,17},{17... | collective-permute-start | bytes 76808 | tf_op jit(solution)/shard_map/ppermute | solution.py:24
  7.3 0.4 copy.53
  7.7 1.9 collective-permute-start.1
  9.7 0.4 copy.39
  10.1 3.2 %collective-permute-done.1 = f32[2,2,50,8,4]{2,3,4,1,0:T(8,128)S(1)} collective-permute-done((f32[2,2,50,8,4]{2,3,4,1,0:T(8,128)S(1)}, f32[2,2,50,8,4]{2,3,4,1,0:T(8,128)S(1)}, u32[]{:S(2)}, u32[]{:S(2)}) %collective-permute-start.1) | collective-permute-done | bytes 25632 | tf_op jit(solution)/shard_map/ppermute | solution.py:25
  13.3 0.4 copy.40
  13.7 0.7 pad_maximum_fusion.2
  14.7 1.3 collective-permute-start.2
  16.0 4.8 %collective-permute-start.3 = (f32[2,2,50,4,136]{4,3,2,1,0:T(4,128)S(1)}, f32[2,2,50,4,136]{4,3,2,1,0:T(4,128)S(1)}, u32[]{:S(2)}, u32[]{:S(2)}) collective-permute-start(f32[2,2,50,4,136]{4,3,2,1,0:T(4,128)S(1)} %get-tuple-element.29), channel_id=1, source_target_pairs={{1,0},{2,1},{3,2},{4,3},{5,4},{6,5},{7,6},{8,7},{9,8},{10,9},{11,1... | collective-permute-start | bytes 1305608 | tf_op jit(solution)/shard_map/ppermute | solution.py:25
  21.0 16.0 %collective-permute-done.2 = f32[2,2,50,4,136]{4,3,2,1,0:T(4,128)S(1)} collective-permute-done((f32[2,2,50,4,136]{4,3,2,1,0:T(4,128)S(1)}, f32[2,2,50,4,136]{4,3,2,1,0:T(4,128)S(1)}, u32[]{:S(2)}, u32[]{:S(2)}) %collective-permute-start.2) | collective-permute-done | bytes 435232 | tf_op jit(solution)/shard_map/ppermute | solution.py:24
  37.0 1.6 pad_maximum_fusion
  39.0 1.3 pad.29.field_ref
  40.3 1.3 fusion.7
  41.6 1.4 pad.34.west_ref
  43.0 1.3 pad.33.east_ref
  44.3 1.3 pad.32.south_ref
  45.6 1.3 pad.31.north_ref
  47.0 8.2 %shard_map.121 = f32[100,8,128]{2,1,0:T(8,128)} custom-call(f32[100,16,256]{2,1,0:T(8,128)} %pad.29.field_ref, f32[100,16,256]{2,1,0:T(8,128)} %pad.31.north_ref, f32[100,16,256]{2,1,0:T(8,128)} %pad.32.south_ref, f32[100,16,256]{2,1,0:T(8,128)} %pad.33.east_ref, f32[100,16,256]{2,1,0:T(8,128)} %pad.34.west_ref), custom_call_target="tpu_custom_call" | custom-call | flops 22937600 | bytes 9830400 | tf_op jit(solution)/shard_map/pallas_call | solution.py:77
  55.1 1.0 multiply_bitcast_fusion
  56.6 1.0 select_maximum_fusion
  57.6 24.2 %shard_map.122 = f32[2,128,128]{2,1,0:T(8,128)} custom-call(f32[512,400]{1,0:T(8,128)} %bitcast.65, s32[128,128]{1,0:T(8,128)} %cell_ref.3, f32[128,4,128]{2,1,0:T(4,128)} %weight_ref.3, f32[2,128,128]{2,1,0:T(8,128)} %scale_ref.1), custom_call_target="tpu_custom_call" | custom-call | flops 13421772800 | bytes 4194304 | tf_op jit(solution)/shard_map/pallas_call | solution.py:180
  81.8 1.3 convolution_bitcast_fusion
  83.4 22.0 %all_to_all.10 = f32[2,256,128]{2,0,1:T(2,128)S(1)} all-to-all(f32[2,256,128]{2,0,1:T(2,128)S(1)} %copy.43), channel_id=1, replica_groups=mesh['lat'=8,'lon'=16] {'lat','lon'}, dimensions={1} | all-to-all | bytes 524288 | tf_op jit(solution)/shard_map/all_to_all | solution.py:339
  105.3 0.4 fusion.11
  105.9 15.2 %all_to_all.11 = f32[2,256,128]{2,0,1:T(2,128)S(1)} all-to-all(f32[2,256,128]{2,0,1:T(2,128)S(1)} %copy.45), channel_id=1, replica_groups=mesh['lat'=8,'lon'=16] {'lat','lon'}, dimensions={1} | all-to-all | bytes 524288 | tf_op jit(solution)/shard_map/all_to_all | solution.py:337
  121.2 0.9 fusion.8.value_ref
  122.1 17.5 %shard_map.123 = f32[2,400,128]{2,1,0:T(8,128)} custom-call(f32[2,128,128]{2,1,0:T(8,128)} %fusion.8.value_ref, s32[128,128]{1,0:T(8,128)} %cell_ref.3, f32[128,4,128]{2,1,0:T(4,128)} %weight_ref.3), custom_call_target="tpu_custom_call" | custom-call | flops 13421772800 | bytes 4194304 | tf_op jit(solution)/shard_map/pallas_call | solution.py:202
  139.6 1.1 copy_multiply_fusion
  140.9 2.6 %collective-permute-start.4 = (f32[2,50,8,4]{3,1,2,0:T(8,128)S(1)}, f32[2,50,8,4]{3,1,2,0:T(8,128)S(1)}, u32[]{:S(2)}, u32[]{:S(2)}) collective-permute-start(f32[2,50,8,4]{3,1,2,0:T(8,128)S(1)} %get-tuple-element.34), channel_id=1, source_target_pairs={{0,16},{16,32},{32,48},{48,64},{64,80},{80,96},{96,112},{1,17},{17... | collective-permute-start | bytes 38408 | tf_op jit(solution)/shard_map/ppermute | solution.py:24
  143.5 1.9 collective-permute-start.5
  145.4 3.5 %collective-permute-done.4 = f32[2,50,8,4]{3,1,2,0:T(8,128)S(1)} collective-permute-done((f32[2,50,8,4]{3,1,2,0:T(8,128)S(1)}, f32[2,50,8,4]{3,1,2,0:T(8,128)S(1)}, u32[]{:S(2)}, u32[]{:S(2)}) %collective-permute-start.4) | collective-permute-done | bytes 12832 | tf_op jit(solution)/shard_map/ppermute | solution.py:24
  148.9 4.7 %collective-permute-done.5 = f32[2,50,8,4]{3,1,2,0:T(8,128)S(1)} collective-permute-done((f32[2,50,8,4]{3,1,2,0:T(8,128)S(1)}, f32[2,50,8,4]{3,1,2,0:T(8,128)S(1)}, u32[]{:S(2)}, u32[]{:S(2)}) %collective-permute-start.5) | collective-permute-done | bytes 12832 | tf_op jit(solution)/shard_map/ppermute | solution.py:25
  153.6 0.4 pad_maximum_fusion.3
  154.1 0.4 collective-permute-start.6
  154.5 4.5 %collective-permute-start.7 = (f32[2,50,4,136]{3,1,2,0:T(8,128)S(1)}, f32[2,50,4,136]{3,1,2,0:T(8,128)S(1)}, u32[]{:S(2)}, u32[]{:S(2)}) collective-permute-start(f32[2,50,4,136]{3,1,2,0:T(8,128)S(1)} %get-tuple-element.31), channel_id=1, source_target_pairs={{1,0},{2,1},{3,2},{4,3},{5,4},{6,5},{7,6},{8,7},{9,8},{10,9},{11,1... | collective-permute-start | bytes 652808 | tf_op jit(solution)/shard_map/ppermute | solution.py:25
  159.0 5.9 %collective-permute-done.6 = f32[2,50,4,136]{3,1,2,0:T(8,128)S(1)} collective-permute-done((f32[2,50,4,136]{3,1,2,0:T(8,128)S(1)}, f32[2,50,4,136]{3,1,2,0:T(8,128)S(1)}, u32[]{:S(2)}, u32[]{:S(2)}) %collective-permute-start.6) | collective-permute-done | bytes 217632 | tf_op jit(solution)/shard_map/ppermute | solution.py:24
  164.8 0.4 pad_maximum_fusion.1
  165.3 0.5 copy.49
  165.8 1.3 pad.35.field_ref
  167.1 8.2 %shard_map.124 = f32[100,8,128]{2,1,0:T(8,128)} custom-call(f32[100,16,256]{2,1,0:T(8,128)} %pad.35.field_ref, f32[100,16,256]{2,1,0:T(8,128)} %pad.31.north_ref, f32[100,16,256]{2,1,0:T(8,128)} %pad.32.south_ref, f32[100,16,256]{2,1,0:T(8,128)} %pad.33.east_ref, f32[100,16,256]{2,1,0:T(8,128)} %pad.34.west_ref), custom_call_target="tpu_custom_call" | custom-call | flops 22937600 | bytes 9830400 | tf_op jit(solution)/shard_map/pallas_call | solution.py:77
  175.3 1.9 multiply_reduce_fusion.3
  177.2 2.6 %maximum_bitcast_fusion = f32[1,4]{1,0:T(1,128)S(1)} fusion(f32[1]{0:T(128)} %bitcast.26, f32[1]{0:T(128)} %bitcast.25, f32[1]{0:T(128)} %bitcast.24, f32[1]{0:T(128)} %bitcast), kind=kLoop, calls=%fused_computation.47 | loop fusion | flops 12 | bytes 32 | tf_op jit(solution)/shard_map/reshape.48
  179.8 0.6 scatter.4.part_ref
  180.4 17.6 %shard_map.125 = f32[8,128]{1,0:T(8,128)} custom-call(f32[8,128]{1,0:T(8,128)} %scatter.4.part_ref), custom_call_target="tpu_custom_call" | custom-call | tf_op jit(solution)/shard_map/pallas_call | solution.py:274
  198.0 1.4 fusion.24
  203.3 1.1 multiply_add_fusion
  (30 shorter events, 1.9 us)
Async XLA Ops:
  0.6 104.7 %copy-start = (f32[128,128]{1,0:T(8,128)S(1)}, f32[128,128]{1,0:T(8,128)}, u32[]{:S(2)}) copy-start(f32[128,128]{1,0:T(8,128)} %param.21) | copy-start | bytes 196612
  2.3 11.4 %copy-start.1 = (f32[2,50,8,128]{3,2,1,0:T(8,128)S(1)}, f32[2,50,8,128]{3,2,1,0:T(8,128)}, u32[]{:S(2)}) copy-start(f32[2,50,8,128]{3,2,1,0:T(8,128)} %param.14) | copy-start | bytes 1228804
  2.3 11.4 %copy-start.2 = (f32[2,50,8,128]{3,2,1,0:T(8,128)S(1)}, f32[2,50,8,128]{3,2,1,0:T(8,128)}, u32[]{:S(2)}) copy-start(f32[2,50,8,128]{3,2,1,0:T(8,128)} %param.15) | copy-start | bytes 1228804
  2.7 6.9 %collective-permute-start = (f32[2,2,50,8,4]{2,3,4,1,0:T(8,128)S(1)}, f32[2,2,50,8,4]{2,3,4,1,0:T(8,128)S(1)}, u32[]{:S(2)}, u32[]{:S(2)}) collective-permute-start(f32[2,2,50,8,4]{2,3,4,1,0:T(8,128)S(1)} %copy.52), channel_id=1, source_target_pairs={{0,16},{16,32},{32,48},{48,64},{64,80},{80,96},{96,112},{1,17},{17... | collective-permute-start | bytes 76808 | tf_op jit(solution)/shard_map/ppermute | solution.py:24
  7.7 5.6 %collective-permute-start.1 = (f32[2,2,50,8,4]{2,3,4,1,0:T(8,128)S(1)}, f32[2,2,50,8,4]{2,3,4,1,0:T(8,128)S(1)}, u32[]{:S(2)}, u32[]{:S(2)}) collective-permute-start(f32[2,2,50,8,4]{2,3,4,1,0:T(8,128)S(1)} %copy.53), channel_id=1, source_target_pairs={{16,0},{32,16},{48,32},{64,48},{80,64},{96,80},{112,96},{17,1},{33... | collective-permute-start | bytes 76808 | tf_op jit(solution)/shard_map/ppermute | solution.py:25
  14.5 6.4 %copy-start.7 = (s32[128,1]{0,1:T(1,128)S(1)}, s32[128,1]{0,1:T(1,128)}, u32[]{:S(2)}) copy-start(s32[128,1]{0,1:T(1,128)} %param.20) | copy-start | bytes 1540
  14.7 22.3 %collective-permute-start.2 = (f32[2,2,50,4,136]{4,3,2,1,0:T(4,128)S(1)}, f32[2,2,50,4,136]{4,3,2,1,0:T(4,128)S(1)}, u32[]{:S(2)}, u32[]{:S(2)}) collective-permute-start(f32[2,2,50,4,136]{4,3,2,1,0:T(4,128)S(1)} %get-tuple-element.28), channel_id=1, source_target_pairs={{0,1},{1,2},{2,3},{3,4},{4,5},{5,6},{6,7},{7,8},{8,9},{9,10},{10,1... | collective-permute-start | bytes 1305608 | tf_op jit(solution)/shard_map/ppermute | solution.py:24
  16.0 21.0 %collective-permute-start.3 = (f32[2,2,50,4,136]{4,3,2,1,0:T(4,128)S(1)}, f32[2,2,50,4,136]{4,3,2,1,0:T(4,128)S(1)}, u32[]{:S(2)}, u32[]{:S(2)}) collective-permute-start(f32[2,2,50,4,136]{4,3,2,1,0:T(4,128)S(1)} %get-tuple-element.29), channel_id=1, source_target_pairs={{1,0},{2,1},{3,2},{4,3},{5,4},{6,5},{7,6},{8,7},{9,8},{10,9},{11,1... | collective-permute-start | bytes 1305608 | tf_op jit(solution)/shard_map/ppermute | solution.py:25
  47.0 8.2 %copy-start.3 = (f32[2,50,8,128]{3,2,1,0:T(8,128)S(1)}, f32[2,50,8,128]{3,2,1,0:T(8,128)}, u32[]{:S(2)}) copy-start(f32[2,50,8,128]{3,2,1,0:T(8,128)} %param.16) | copy-start | bytes 1228804
  81.8 39.3 %copy-start.6 = (f32[2,128,128]{2,1,0:T(8,128)S(1)}, f32[2,128,128]{2,1,0:T(8,128)}, u32[]{:S(2)}) copy-start(f32[2,128,128]{2,1,0:T(8,128)} %scale_ref.1) | copy-start | bytes 393220
  140.9 8.0 %collective-permute-start.4 = (f32[2,50,8,4]{3,1,2,0:T(8,128)S(1)}, f32[2,50,8,4]{3,1,2,0:T(8,128)S(1)}, u32[]{:S(2)}, u32[]{:S(2)}) collective-permute-start(f32[2,50,8,4]{3,1,2,0:T(8,128)S(1)} %get-tuple-element.34), channel_id=1, source_target_pairs={{0,16},{16,32},{32,48},{48,64},{64,80},{80,96},{96,112},{1,17},{17... | collective-permute-start | bytes 38408 | tf_op jit(solution)/shard_map/ppermute | solution.py:24
  143.5 10.1 %collective-permute-start.5 = (f32[2,50,8,4]{3,1,2,0:T(8,128)S(1)}, f32[2,50,8,4]{3,1,2,0:T(8,128)S(1)}, u32[]{:S(2)}, u32[]{:S(2)}) collective-permute-start(f32[2,50,8,4]{3,1,2,0:T(8,128)S(1)} %get-tuple-element.35), channel_id=1, source_target_pairs={{16,0},{32,16},{48,32},{64,48},{80,64},{96,80},{112,96},{17,1},{33... | collective-permute-start | bytes 38408 | tf_op jit(solution)/shard_map/ppermute | solution.py:25
  154.1 10.7 %collective-permute-start.6 = (f32[2,50,4,136]{3,1,2,0:T(8,128)S(1)}, f32[2,50,4,136]{3,1,2,0:T(8,128)S(1)}, u32[]{:S(2)}, u32[]{:S(2)}) collective-permute-start(f32[2,50,4,136]{3,1,2,0:T(8,128)S(1)} %get-tuple-element.30), channel_id=1, source_target_pairs={{0,1},{1,2},{2,3},{3,4},{4,5},{5,6},{6,7},{7,8},{8,9},{9,10},{10,1... | collective-permute-start | bytes 652808 | tf_op jit(solution)/shard_map/ppermute | solution.py:24
  154.5 10.3 %collective-permute-start.7 = (f32[2,50,4,136]{3,1,2,0:T(8,128)S(1)}, f32[2,50,4,136]{3,1,2,0:T(8,128)S(1)}, u32[]{:S(2)}, u32[]{:S(2)}) collective-permute-start(f32[2,50,4,136]{3,1,2,0:T(8,128)S(1)} %get-tuple-element.31), channel_id=1, source_target_pairs={{1,0},{2,1},{3,2},{4,3},{5,4},{6,5},{7,6},{8,7},{9,8},{10,9},{11,1... | collective-permute-start | bytes 652808 | tf_op jit(solution)/shard_map/ppermute | solution.py:25
  167.1 8.2 %copy-start.4 = (f32[2,50,8,128]{3,2,1,0:T(8,128)S(1)}, f32[2,50,8,128]{3,2,1,0:T(8,128)}, u32[]{:S(2)}) copy-start(f32[2,50,8,128]{3,2,1,0:T(8,128)} %param.13) | copy-start | bytes 1228804
  175.3 28.0 %copy-start.5 = (f32[2,50,8,128]{3,2,1,0:T(8,128)S(1)}, f32[2,50,8,128]{3,2,1,0:T(8,128)}, u32[]{:S(2)}) copy-start(f32[2,50,8,128]{3,2,1,0:T(8,128)} %param.12) | copy-start | bytes 1228804

commit v5 on v4

--- a/solution.py
+++ b/solution.py
@@ -28,11 +28,12 @@
 
 
 def face_coeffs(wide, width):
-    wide = jnp.pad(wide, ((0, 0), (0, 0), (1, 1), (1, 1)))
-    lat_count = wide.shape[3] - 2 * (width + 1)
+    lat_count = wide.shape[3] - 2 * width
+    lanes = -(-wide.shape[3] // 128) * 128
+    wide = jnp.pad(wide, ((0, 0), (0, 0), (1, 1), (1, 1 + lanes - wide.shape[3])))
     lat_devices = lax.axis_size("lat")
     first = lax.axis_index("lat") * lat_count - width
-    cells = first + jnp.arange(lat_count + 2 * width, dtype=jnp.int32)
+    cells = first + jnp.arange(lanes, dtype=jnp.int32)
     inside = ((cells >= 0) & (cells < lat_devices * lat_count)).astype(jnp.float32)
     centre = wide[:, :, 1:-1, 1:-1]
     return (

time: 205 us -> 202 us (0.985)
  local copies, waits for them, and re-layouts: 13.9 us -> 8.49 us
    pad x6 -> x2, local copies, waits for them, and re-layouts: 8.01 us -> 2.67 us  [pad_lanes(): return jnp.pad(value, ((0, 0), (0, 0), (0, -lanes % 128)))]
  transfers between devices with their start and end apart: 8 -> 8, of which waited for: 5 -> 6; matrix products, arithmetic and copies ran while one was open for 0% -> 0% of each run, Pallas kernels for 0% -> 0%
where the time goes in v5:
time: 202 us; the launch traced here: 201 us
  Pallas kernels  75.6 us (37%)
  blocking collectives  37.1 us (18%)
  waiting for transfers between devices  33.1 us (16%)
  starting transfers between devices  22.2 us (11%)
  other arithmetic  16.9 us (8%)
  local copies, waits for them, and re-layouts  8.49 us (4%)
  between operations  4.76 us (2%)
  matrix products  2.8 us (1%)
    ppermute x4, waiting for transfers between devices, widen_halo(): lax.ppermute(lax.slice_in_dim(value, length - width, length, axis=dim), a...  25.1 us
    pallas_call x1, Pallas kernels, observe_pallas(): pl.pallas_call(kernel, grid=(block_count // group,), in_specs=[pl.BlockSp...  24.2 us
    all_to_all x1, blocking collectives, shards(): lax.all_to_all(buffer, ('lat', 'lon'), split_axis=1, concat_axis=1, tiled...  21.8 us
    pallas_call x1, Pallas kernels, allreduce_pallas(): pl.pallas_call(kernel, in_specs=[pl.BlockSpec(memory_space=pltpu.VMEM)],...  17.6 us
    pallas_call x1, Pallas kernels, spread_pallas(): pl.pallas_call(kernel, grid=(block_count // group,), in_specs=[pl.BlockSp...  17.5 us
    pallas_call x2, Pallas kernels, diffuse(): pl.pallas_call(functools.partial(diffuse_kernel, STEPS), grid=(planes //...  16.3 us
    all_to_all x1, blocking collectives, shards(): lax.all_to_all(mix_blocks(lax.all_to_all(buffer, ('lat', 'lon'), split_ax...  15.2 us
    ppermute x4, starting transfers between devices, widen_halo(): lax.ppermute(lax.slice_in_dim(value, 0, width, axis=dim), axis, down)  13.3 us
  transfers between devices with their start and end apart: 8, of which 6 were waited for; matrix products, arithmetic and copies ran while one was open for 0% of the time, Pallas kernels for 0%

profile of v5, /device:TPU:1, one launch (start us, length us, event | category | flops | bytes accessed | tf_op | source)
XLA Modules:
  0.0 200.9 jit_solution(17317972690613155548)
XLA Ops:
  0.6 1.7 slice_maximum_fusion
  2.4 0.4 copy.52
  2.7 4.6 %collective-permute-start = (f32[2,2,50,8,4]{2,3,4,1,0:T(8,128)S(1)}, f32[2,2,50,8,4]{2,3,4,1,0:T(8,128)S(1)}, u32[]{:S(2)}, u32[]{:S(2)}) collective-permute-start(f32[2,2,50,8,4]{2,3,4,1,0:T(8,128)S(1)} %copy.52), channel_id=1, source_target_pairs={{0,16},{16,32},{32,48},{48,64},{64,80},{80,96},{96,112},{1,17},{17... | collective-permute-start | bytes 76808 | tf_op jit(solution)/shard_map/ppermute | solution.py:24
  7.3 0.4 copy.53
  7.7 1.9 collective-permute-start.1
  9.7 0.4 copy.39
  10.1 3.2 %collective-permute-done.1 = f32[2,2,50,8,4]{2,3,4,1,0:T(8,128)S(1)} collective-permute-done((f32[2,2,50,8,4]{2,3,4,1,0:T(8,128)S(1)}, f32[2,2,50,8,4]{2,3,4,1,0:T(8,128)S(1)}, u32[]{:S(2)}, u32[]{:S(2)}) %collective-permute-start.1) | collective-permute-done | bytes 25632 | tf_op jit(solution)/shard_map/ppermute | solution.py:25
  13.3 0.4 copy.40
  13.7 0.7 pad_maximum_fusion.2
  14.5 0.2 fusion.21
  14.7 1.3 collective-permute-start.2
  16.0 5.0 %collective-permute-start.3 = (f32[2,2,50,4,136]{4,3,2,1,0:T(4,128)S(1)}, f32[2,2,50,4,136]{4,3,2,1,0:T(4,128)S(1)}, u32[]{:S(2)}, u32[]{:S(2)}) collective-permute-start(f32[2,2,50,4,136]{4,3,2,1,0:T(4,128)S(1)} %get-tuple-element.29), channel_id=1, source_target_pairs={{1,0},{2,1},{3,2},{4,3},{5,4},{6,5},{7,6},{8,7},{9,8},{10,9},{11,1... | collective-permute-start | bytes 1305608 | tf_op jit(solution)/shard_map/ppermute | solution.py:25
  21.2 15.8 %collective-permute-done.2 = f32[2,2,50,4,136]{4,3,2,1,0:T(4,128)S(1)} collective-permute-done((f32[2,2,50,4,136]{4,3,2,1,0:T(4,128)S(1)}, f32[2,2,50,4,136]{4,3,2,1,0:T(4,128)S(1)}, u32[]{:S(2)}, u32[]{:S(2)}) %collective-permute-start.2) | collective-permute-done | bytes 435232 | tf_op jit(solution)/shard_map/ppermute | solution.py:24
  37.1 1.6 pad_maximum_fusion
  38.7 0.3 slice_bitcast_fusion
  39.0 1.3 pad.17.field_ref
  40.4 3.2 %fusion.7 = (f32[2,50,16,256]{3,2,1,0:T(8,128)}, f32[2,50,16,256]{3,2,1,0:T(8,128)}, f32[2,50,16,256]{3,2,1,0:T(8,128)}, f32[2,50,16,256]{3,2,1,0:T(8,128)}) fusion(f32[2,50,16,136]{3,2,1,0:T(8,128)S(1)} %get-tuple-element.22, f32[256]{0:T(256)S(1)} %and_select_fusion), kind=kLoop, calls=%fused_computation.14 | loop fusion | flops 3276800 | bytes 7425024 | tf_op jit(solution)/shard_map/mul | solution.py:43
  43.6 8.2 %shard_map.121 = f32[100,8,128]{2,1,0:T(8,128)} custom-call(f32[100,16,256]{2,1,0:T(8,128)} %pad.17.field_ref, f32[100,16,256]{2,1,0:T(8,128)} %bitcast.55, f32[100,16,256]{2,1,0:T(8,128)} %bitcast.51, f32[100,16,256]{2,1,0:T(8,128)} %bitcast.53, f32[100,16,256]{2,1,0:T(8,128)} %bitcast.49), custom_call_target="tpu_custom_call" | custom-call | flops 22937600 | bytes 9830400 | tf_op jit(solution)/shard_map/pallas_call | solution.py:78
  51.8 1.0 multiply_bitcast_fusion
  53.2 1.0 select_maximum_fusion
  54.3 24.2 %shard_map.122 = f32[2,128,128]{2,1,0:T(8,128)} custom-call(f32[512,400]{1,0:T(8,128)} %bitcast.69, s32[128,128]{1,0:T(8,128)} %cell_ref.3, f32[128,4,128]{2,1,0:T(4,128)} %weight_ref.3, f32[2,128,128]{2,1,0:T(8,128)} %scale_ref.1), custom_call_target="tpu_custom_call" | custom-call | flops 13421772800 | bytes 4194304 | tf_op jit(solution)/shard_map/pallas_call | solution.py:181
  78.5 1.3 convolution_bitcast_fusion
  79.8 0.2 copy.43
  80.0 21.8 %all_to_all.10 = f32[2,256,128]{2,0,1:T(2,128)S(1)} all-to-all(f32[2,256,128]{2,0,1:T(2,128)S(1)} %copy.43), channel_id=1, replica_groups=mesh['lat'=8,'lon'=16] {'lat','lon'}, dimensions={1} | all-to-all | bytes 524288 | tf_op jit(solution)/shard_map/all_to_all | solution.py:340
  101.9 0.4 fusion.11
  102.2 0.2 copy.45
  102.5 15.2 %all_to_all.11 = f32[2,256,128]{2,0,1:T(2,128)S(1)} all-to-all(f32[2,256,128]{2,0,1:T(2,128)S(1)} %copy.45), channel_id=1, replica_groups=mesh['lat'=8,'lon'=16] {'lat','lon'}, dimensions={1} | all-to-all | bytes 524288 | tf_op jit(solution)/shard_map/all_to_all | solution.py:338
  117.7 0.9 fusion.8.value_ref
  118.6 17.5 %shard_map.123 = f32[2,400,128]{2,1,0:T(8,128)} custom-call(f32[2,128,128]{2,1,0:T(8,128)} %fusion.8.value_ref, s32[128,128]{1,0:T(8,128)} %cell_ref.3, f32[128,4,128]{2,1,0:T(4,128)} %weight_ref.3), custom_call_target="tpu_custom_call" | custom-call | flops 13421772800 | bytes 4194304 | tf_op jit(solution)/shard_map/pallas_call | solution.py:203
  136.1 1.1 copy_multiply_fusion
  137.4 2.6 %collective-permute-start.4 = (f32[2,50,8,4]{3,1,2,0:T(8,128)S(1)}, f32[2,50,8,4]{3,1,2,0:T(8,128)S(1)}, u32[]{:S(2)}, u32[]{:S(2)}) collective-permute-start(f32[2,50,8,4]{3,1,2,0:T(8,128)S(1)} %get-tuple-element.34), channel_id=1, source_target_pairs={{0,16},{16,32},{32,48},{48,64},{64,80},{80,96},{96,112},{1,17},{17... | collective-permute-start | bytes 38408 | tf_op jit(solution)/shard_map/ppermute | solution.py:24
  140.1 1.9 collective-permute-start.5
  142.0 3.5 %collective-permute-done.4 = f32[2,50,8,4]{3,1,2,0:T(8,128)S(1)} collective-permute-done((f32[2,50,8,4]{3,1,2,0:T(8,128)S(1)}, f32[2,50,8,4]{3,1,2,0:T(8,128)S(1)}, u32[]{:S(2)}, u32[]{:S(2)}) %collective-permute-start.4) | collective-permute-done | bytes 12832 | tf_op jit(solution)/shard_map/ppermute | solution.py:24
  145.5 4.7 %collective-permute-done.5 = f32[2,50,8,4]{3,1,2,0:T(8,128)S(1)} collective-permute-done((f32[2,50,8,4]{3,1,2,0:T(8,128)S(1)}, f32[2,50,8,4]{3,1,2,0:T(8,128)S(1)}, u32[]{:S(2)}, u32[]{:S(2)}) %collective-permute-start.5) | collective-permute-done | bytes 12832 | tf_op jit(solution)/shard_map/ppermute | solution.py:25
  150.1 0.4 pad_maximum_fusion.3
  150.7 0.4 collective-permute-start.6
  151.0 4.5 %collective-permute-start.7 = (f32[2,50,4,136]{3,1,2,0:T(8,128)S(1)}, f32[2,50,4,136]{3,1,2,0:T(8,128)S(1)}, u32[]{:S(2)}, u32[]{:S(2)}) collective-permute-start(f32[2,50,4,136]{3,1,2,0:T(8,128)S(1)} %get-tuple-element.31), channel_id=1, source_target_pairs={{1,0},{2,1},{3,2},{4,3},{5,4},{6,5},{7,6},{8,7},{9,8},{10,9},{11,1... | collective-permute-start | bytes 652808 | tf_op jit(solution)/shard_map/ppermute | solution.py:25
  155.5 5.9 %collective-permute-done.6 = f32[2,50,4,136]{3,1,2,0:T(8,128)S(1)} collective-permute-done((f32[2,50,4,136]{3,1,2,0:T(8,128)S(1)}, f32[2,50,4,136]{3,1,2,0:T(8,128)S(1)}, u32[]{:S(2)}, u32[]{:S(2)}) %collective-permute-start.6) | collective-permute-done | bytes 217632 | tf_op jit(solution)/shard_map/ppermute | solution.py:24
  161.4 0.4 pad_maximum_fusion.1
  161.8 0.5 copy.49
  162.3 1.3 pad.19.field_ref
  163.7 8.2 %shard_map.124 = f32[100,8,128]{2,1,0:T(8,128)} custom-call(f32[100,16,256]{2,1,0:T(8,128)} %pad.19.field_ref, f32[100,16,256]{2,1,0:T(8,128)} %bitcast.56, f32[100,16,256]{2,1,0:T(8,128)} %bitcast.52, f32[100,16,256]{2,1,0:T(8,128)} %bitcast.54, f32[100,16,256]{2,1,0:T(8,128)} %bitcast.50), custom_call_target="tpu_custom_call" | custom-call | flops 22937600 | bytes 9830400 | tf_op jit(solution)/shard_map/pallas_call | solution.py:78
  171.8 1.9 multiply_reduce_fusion.3
  173.7 2.6 %maximum_bitcast_fusion = f32[1,4]{1,0:T(1,128)S(1)} fusion(f32[1]{0:T(128)} %bitcast.26, f32[1]{0:T(128)} %bitcast.25, f32[1]{0:T(128)} %bitcast.24, f32[1]{0:T(128)} %bitcast), kind=kLoop, calls=%fused_computation.48 | loop fusion | flops 12 | bytes 32 | tf_op jit(solution)/shard_map/reshape.48
  176.3 0.6 scatter.4.part_ref
  176.9 17.6 %shard_map.125 = f32[8,128]{1,0:T(8,128)} custom-call(f32[8,128]{1,0:T(8,128)} %scatter.4.part_ref), custom_call_target="tpu_custom_call" | custom-call | tf_op jit(solution)/shard_map/pallas_call | solution.py:275
  194.5 1.4 fusion.24
  199.8 1.1 multiply_add_fusion
  (26 shorter events, 1.0 us)
Async XLA Ops:
  0.6 101.2 %copy-start = (f32[128,128]{1,0:T(8,128)S(1)}, f32[128,128]{1,0:T(8,128)}, u32[]{:S(2)}) copy-start(f32[128,128]{1,0:T(8,128)} %param.21) | copy-start | bytes 196612
  2.3 11.4 %copy-start.1 = (f32[2,50,8,128]{3,2,1,0:T(8,128)S(1)}, f32[2,50,8,128]{3,2,1,0:T(8,128)}, u32[]{:S(2)}) copy-start(f32[2,50,8,128]{3,2,1,0:T(8,128)} %param.14) | copy-start | bytes 1228804
  2.3 11.4 %copy-start.2 = (f32[2,50,8,128]{3,2,1,0:T(8,128)S(1)}, f32[2,50,8,128]{3,2,1,0:T(8,128)}, u32[]{:S(2)}) copy-start(f32[2,50,8,128]{3,2,1,0:T(8,128)} %param.15) | copy-start | bytes 1228804
  2.7 6.9 %collective-permute-start = (f32[2,2,50,8,4]{2,3,4,1,0:T(8,128)S(1)}, f32[2,2,50,8,4]{2,3,4,1,0:T(8,128)S(1)}, u32[]{:S(2)}, u32[]{:S(2)}) collective-permute-start(f32[2,2,50,8,4]{2,3,4,1,0:T(8,128)S(1)} %copy.52), channel_id=1, source_target_pairs={{0,16},{16,32},{32,48},{48,64},{64,80},{80,96},{96,112},{1,17},{17... | collective-permute-start | bytes 76808 | tf_op jit(solution)/shard_map/ppermute | solution.py:24
  7.7 5.6 %collective-permute-start.1 = (f32[2,2,50,8,4]{2,3,4,1,0:T(8,128)S(1)}, f32[2,2,50,8,4]{2,3,4,1,0:T(8,128)S(1)}, u32[]{:S(2)}, u32[]{:S(2)}) collective-permute-start(f32[2,2,50,8,4]{2,3,4,1,0:T(8,128)S(1)} %copy.53), channel_id=1, source_target_pairs={{16,0},{32,16},{48,32},{64,48},{80,64},{96,80},{112,96},{17,1},{33... | collective-permute-start | bytes 76808 | tf_op jit(solution)/shard_map/ppermute | solution.py:25
  14.5 6.6 %copy-start.7 = (s32[128,1]{0,1:T(1,128)S(1)}, s32[128,1]{0,1:T(1,128)}, u32[]{:S(2)}) copy-start(s32[128,1]{0,1:T(1,128)} %param.20) | copy-start | bytes 1540
  14.7 22.3 %collective-permute-start.2 = (f32[2,2,50,4,136]{4,3,2,1,0:T(4,128)S(1)}, f32[2,2,50,4,136]{4,3,2,1,0:T(4,128)S(1)}, u32[]{:S(2)}, u32[]{:S(2)}) collective-permute-start(f32[2,2,50,4,136]{4,3,2,1,0:T(4,128)S(1)} %get-tuple-element.28), channel_id=1, source_target_pairs={{0,1},{1,2},{2,3},{3,4},{4,5},{5,6},{6,7},{7,8},{8,9},{9,10},{10,1... | collective-permute-start | bytes 1305608 | tf_op jit(solution)/shard_map/ppermute | solution.py:24
  16.0 21.1 %collective-permute-start.3 = (f32[2,2,50,4,136]{4,3,2,1,0:T(4,128)S(1)}, f32[2,2,50,4,136]{4,3,2,1,0:T(4,128)S(1)}, u32[]{:S(2)}, u32[]{:S(2)}) collective-permute-start(f32[2,2,50,4,136]{4,3,2,1,0:T(4,128)S(1)} %get-tuple-element.29), channel_id=1, source_target_pairs={{1,0},{2,1},{3,2},{4,3},{5,4},{6,5},{7,6},{8,7},{9,8},{10,9},{11,1... | collective-permute-start | bytes 1305608 | tf_op jit(solution)/shard_map/ppermute | solution.py:25
  43.6 8.2 %copy-start.3 = (f32[2,50,8,128]{3,2,1,0:T(8,128)S(1)}, f32[2,50,8,128]{3,2,1,0:T(8,128)}, u32[]{:S(2)}) copy-start(f32[2,50,8,128]{3,2,1,0:T(8,128)} %param.16) | copy-start | bytes 1228804
  78.5 39.2 %copy-start.6 = (f32[2,128,128]{2,1,0:T(8,128)S(1)}, f32[2,128,128]{2,1,0:T(8,128)}, u32[]{:S(2)}) copy-start(f32[2,128,128]{2,1,0:T(8,128)} %scale_ref.1) | copy-start | bytes 393220
  137.4 8.0 %collective-permute-start.4 = (f32[2,50,8,4]{3,1,2,0:T(8,128)S(1)}, f32[2,50,8,4]{3,1,2,0:T(8,128)S(1)}, u32[]{:S(2)}, u32[]{:S(2)}) collective-permute-start(f32[2,50,8,4]{3,1,2,0:T(8,128)S(1)} %get-tuple-element.34), channel_id=1, source_target_pairs={{0,16},{16,32},{32,48},{48,64},{64,80},{80,96},{96,112},{1,17},{17... | collective-permute-start | bytes 38408 | tf_op jit(solution)/shard_map/ppermute | solution.py:24
  140.1 10.1 %collective-permute-start.5 = (f32[2,50,8,4]{3,1,2,0:T(8,128)S(1)}, f32[2,50,8,4]{3,1,2,0:T(8,128)S(1)}, u32[]{:S(2)}, u32[]{:S(2)}) collective-permute-start(f32[2,50,8,4]{3,1,2,0:T(8,128)S(1)} %get-tuple-element.35), channel_id=1, source_target_pairs={{16,0},{32,16},{48,32},{64,48},{80,64},{96,80},{112,96},{17,1},{33... | collective-permute-start | bytes 38408 | tf_op jit(solution)/shard_map/ppermute | solution.py:25
  150.7 10.7 %collective-permute-start.6 = (f32[2,50,4,136]{3,1,2,0:T(8,128)S(1)}, f32[2,50,4,136]{3,1,2,0:T(8,128)S(1)}, u32[]{:S(2)}, u32[]{:S(2)}) collective-permute-start(f32[2,50,4,136]{3,1,2,0:T(8,128)S(1)} %get-tuple-element.30), channel_id=1, source_target_pairs={{0,1},{1,2},{2,3},{3,4},{4,5},{5,6},{6,7},{7,8},{8,9},{9,10},{10,1... | collective-permute-start | bytes 652808 | tf_op jit(solution)/shard_map/ppermute | solution.py:24
  151.0 10.3 %collective-permute-start.7 = (f32[2,50,4,136]{3,1,2,0:T(8,128)S(1)}, f32[2,50,4,136]{3,1,2,0:T(8,128)S(1)}, u32[]{:S(2)}, u32[]{:S(2)}) collective-permute-start(f32[2,50,4,136]{3,1,2,0:T(8,128)S(1)} %get-tuple-element.31), channel_id=1, source_target_pairs={{1,0},{2,1},{3,2},{4,3},{5,4},{6,5},{7,6},{8,7},{9,8},{10,9},{11,1... | collective-permute-start | bytes 652808 | tf_op jit(solution)/shard_map/ppermute | solution.py:25
  163.6 8.2 %copy-start.4 = (f32[2,50,8,128]{3,2,1,0:T(8,128)S(1)}, f32[2,50,8,128]{3,2,1,0:T(8,128)}, u32[]{:S(2)}) copy-start(f32[2,50,8,128]{3,2,1,0:T(8,128)} %param.13) | copy-start | bytes 1228804
  171.8 28.0 %copy-start.5 = (f32[2,50,8,128]{3,2,1,0:T(8,128)S(1)}, f32[2,50,8,128]{3,2,1,0:T(8,128)}, u32[]{:S(2)}) copy-start(f32[2,50,8,128]{3,2,1,0:T(8,128)} %param.12) | copy-start | bytes 1228804

commit v6 on v5

--- a/solution.py
+++ b/solution.py
@@ -23,12 +23,15 @@
         down = [(j, i) for i, j in up]
         before = lax.ppermute(lax.slice_in_dim(value, length - width, length, axis=dim), axis, up)
         after = lax.ppermute(lax.slice_in_dim(value, 0, width, axis=dim), axis, down)
-        value = jnp.concatenate([before, value, after], axis=dim)
+        pieces = [before, value, after]
+        spare = -(length + 2 * width) % 128
+        if dim == lat_dim and spare:
+            pieces.append(jnp.zeros(value.shape[:-1] + (spare,), value.dtype))
+        value = jnp.concatenate(pieces, axis=dim)
     return value
 
 
-def face_coeffs(wide, width):
-    lat_count = wide.shape[3] - 2 * width
+def face_coeffs(wide, width, lat_count):
     lanes = -(-wide.shape[3] // 128) * 128
     wide = jnp.pad(wide, ((0, 0), (0, 0), (1, 1), (1, 1 + lanes - wide.shape[3])))
     lat_devices = lax.axis_size("lat")
@@ -69,11 +72,11 @@
     return tuple(pad_lanes(c.reshape((-1,) + c.shape[-2:])) for c in coeffs)
 
 
-def diffuse(field, coeffs, planes_per_step=50):
+def diffuse(field, coeffs, lat_count, planes_per_step=50):
     lead = field.shape[:-2]
     flat = pad_lanes(field.reshape((-1,) + field.shape[-2:]))
     planes, rows, lanes = flat.shape
-    lon_count, lat_count = rows - 2 * STEPS, field.shape[-1] - 2 * STEPS
+    lon_count = rows - 2 * STEPS
     spec = pl.BlockSpec((planes_per_step, rows, lanes), lambda i: (i, 0, 0))
     out = pl.pallas_call(
         functools.partial(diffuse_kernel, STEPS),
@@ -322,17 +325,17 @@
     lon_devices = lax.axis_size("lon")
     tile_count = lat_devices * lon_devices
     both = widen_halo(jnp.stack([direction, diffusivity]), STEPS)
-    coeffs = padded_coeffs(face_coeffs(both[1], STEPS))
+    coeffs = padded_coeffs(face_coeffs(both[1], STEPS, direction.shape[3]))
 
     def apply_diffusion(field):
-        return diffuse(widen_halo(field, STEPS), coeffs)
+        return diffuse(widen_halo(field, STEPS), coeffs, field.shape[3])
 
     slots = slots_of(block_owner, tile_count)
     slot_table = (slots[:, None] == jnp.arange(tile_count * CAP, dtype=jnp.int32)[None, :]).astype(
         jnp.float32
     )
     field_shape = direction.shape
-    state_field = deviation * diffuse(both[0], coeffs)
+    state_field = deviation * diffuse(both[0], coeffs, direction.shape[3])
     observed = observe_pallas(state_field, stencil, bilinear, obs_weight)
     buffer = jnp.einsum("vbk,bs->vsk", observed, slot_table, precision=precise)
     returned = lax.all_to_all(

time: 202 us -> 206 us (1.020)
  other arithmetic: 16.9 us -> 19.9 us
    pad x2 -> x0, local copies, waits for them, and re-layouts: 2.67 us -> none  [pad_lanes(): return jnp.pad(value, ((0, 0), (0, 0), (0, -lanes % 128)))]
    concatenate x4, other arithmetic: 3.15 us -> 5.67 us  [widen_halo(): value = jnp.concatenate(pieces, axis=dim)]
  transfers between devices with their start and end apart: 8 -> 8, of which waited for: 6 -> 5; matrix products, arithmetic and copies ran while one was open for 0% -> 0% of each run, Pallas kernels for 0% -> 0%
where the time goes in v6:
time: 206 us; the launch traced here: 205 us
  Pallas kernels  75.6 us (37%)
  blocking collectives  37.2 us (18%)
  waiting for transfers between devices  33.6 us (16%)
  starting transfers between devices  21.9 us (11%)
  other arithmetic  19.9 us (10%)
  local copies, waits for them, and re-layouts  9.46 us (5%)
  between operations  4.74 us (2%)
  matrix products  2.8 us (1%)
    ppermute x4, waiting for transfers between devices, widen_halo(): lax.ppermute(lax.slice_in_dim(value, length - width, length, axis=dim), a...  25.7 us
    pallas_call x1, Pallas kernels, observe_pallas(): pl.pallas_call(kernel, grid=(block_count // group,), in_specs=[pl.BlockSp...  24.2 us
    all_to_all x1, blocking collectives, shards(): lax.all_to_all(buffer, ('lat', 'lon'), split_axis=1, concat_axis=1, tiled...  21.9 us
    pallas_call x1, Pallas kernels, allreduce_pallas(): pl.pallas_call(kernel, in_specs=[pl.BlockSpec(memory_space=pltpu.VMEM)],...  17.6 us
    pallas_call x1, Pallas kernels, spread_pallas(): pl.pallas_call(kernel, grid=(block_count // group,), in_specs=[pl.BlockSp...  17.5 us
    pallas_call x2, Pallas kernels, diffuse(): pl.pallas_call(functools.partial(diffuse_kernel, STEPS), grid=(planes //...  16.3 us
    all_to_all x1, blocking collectives, shards(): lax.all_to_all(mix_blocks(lax.all_to_all(buffer, ('lat', 'lon'), split_ax...  15.2 us
    ppermute x4, starting transfers between devices, widen_halo(): lax.ppermute(lax.slice_in_dim(value, 0, width, axis=dim), axis, down)  13.1 us
  transfers between devices with their start and end apart: 8, of which 5 were waited for; matrix products, arithmetic and copies ran while one was open for 0% of the time, Pallas kernels for 0%

profile of v6, /device:TPU:1, one launch (start us, length us, event | category | flops | bytes accessed | tf_op | source)
XLA Modules:
  0.0 205.2 jit_solution(5021325306125709542)
XLA Ops:
  0.6 1.7 slice_maximum_fusion
  2.3 0.4 copy.52
  2.7 4.6 %collective-permute-start = (f32[2,2,50,8,4]{2,3,4,1,0:T(8,128)S(1)}, f32[2,2,50,8,4]{2,3,4,1,0:T(8,128)S(1)}, u32[]{:S(2)}, u32[]{:S(2)}) collective-permute-start(f32[2,2,50,8,4]{2,3,4,1,0:T(8,128)S(1)} %copy.52), channel_id=1, source_target_pairs={{0,16},{16,32},{32,48},{48,64},{64,80},{80,96},{96,112},{1,17},{17... | collective-permute-start | bytes 76808 | tf_op jit(solution)/shard_map/ppermute | solution.py:24
  7.3 0.4 copy.53
  7.7 1.9 collective-permute-start.1
  9.7 0.4 copy.39
  10.1 3.2 %collective-permute-done.1 = f32[2,2,50,8,4]{2,3,4,1,0:T(8,128)S(1)} collective-permute-done((f32[2,2,50,8,4]{2,3,4,1,0:T(8,128)S(1)}, f32[2,2,50,8,4]{2,3,4,1,0:T(8,128)S(1)}, u32[]{:S(2)}, u32[]{:S(2)}) %collective-permute-start.1) | collective-permute-done | bytes 25632 | tf_op jit(solution)/shard_map/ppermute | solution.py:25
  13.3 0.4 copy.40
  13.8 0.9 pad_maximum_fusion.2
  14.7 1.4 fusion.21
  16.2 1.2 collective-permute-start.2
  17.4 4.7 %collective-permute-start.3 = (f32[2,2,50,4,256]{4,3,2,1,0:T(4,128)}, f32[2,2,50,4,256]{4,3,2,1,0:T(4,128)}, u32[]{:S(2)}, u32[]{:S(2)}) collective-permute-start(f32[2,2,50,4,256]{4,3,2,1,0:T(4,128)} %get-tuple-element.29), channel_id=1, source_target_pairs={{1,0},{2,1},{3,2},{4,3},{5,4},{6,5},{7,6},{8,7},{9,8},{10,9},{11,1... | collective-permute-start | bytes 2457608 | tf_op jit(solution)/shard_map/ppermute | solution.py:25
  22.3 16.4 %collective-permute-done.2 = f32[2,2,50,4,256]{4,3,2,1,0:T(4,128)} collective-permute-done((f32[2,2,50,4,256]{4,3,2,1,0:T(4,128)}, f32[2,2,50,4,256]{4,3,2,1,0:T(4,128)}, u32[]{:S(2)}, u32[]{:S(2)}) %collective-permute-start.2) | collective-permute-done | bytes 819232 | tf_op jit(solution)/shard_map/ppermute | solution.py:24
  38.7 3.7 %pad_maximum_fusion = f32[2,2,50,16,256]{4,3,2,1,0:T(8,128)S(1)} fusion(f32[2,2,50,4,256]{4,3,2,1,0:T(4,128)} %collective-permute-done.3, f32[2,2,50,8,120]{4,3,2,1,0:T(8,128)S(1)} %broadcast_in_dim.4, f32[2,2,50,8,4]{4,3,2,1,0:T(8,128)S(1)} %copy.40, f32[1,2,50,8,128]{4,3,2,1,0:T(8,128)S(1)} %bitcast.66, f32[1,2,50,8,128]{4,3,2,1,0:T(8,128)S(1)} %bitcast.59, ...), kind=kLoop, calls=%fused_computation.4 | loop fusion | flops 4915200 | bytes 6553600 | tf_op jit(solution)/shard_map/concatenate | solution.py:30
  42.4 1.5 slice_bitcast_fusion
  43.9 3.7 %fusion.7 = (f32[2,50,16,256]{3,2,1,0:T(8,128)}, f32[2,50,16,256]{3,2,1,0:T(8,128)}, f32[2,50,16,256]{3,2,1,0:T(8,128)}, f32[2,50,16,256]{3,2,1,0:T(8,128)}) fusion(f32[2,50,16,256]{3,2,1,0:T(8,128)S(1)} %get-tuple-element.22, f32[256]{0:T(256)S(1)} %and_select_fusion), kind=kLoop, calls=%fused_computation.13 | loop fusion | flops 3276800 | bytes 8193024 | tf_op jit(solution)/shard_map/mul | solution.py:46
  47.6 8.2 %shard_map.121 = f32[100,8,128]{2,1,0:T(8,128)} custom-call(f32[100,16,256]{2,1,0:T(8,128)} %bitcast.60, f32[100,16,256]{2,1,0:T(8,128)} %bitcast.55, f32[100,16,256]{2,1,0:T(8,128)} %bitcast.53, f32[100,16,256]{2,1,0:T(8,128)} %bitcast.51, f32[100,16,256]{2,1,0:T(8,128)} %bitcast.49), custom_call_target="tpu_custom_call" | custom-call | flops 22937600 | bytes 9830400 | tf_op jit(solution)/shard_map/pallas_call | solution.py:81
  55.8 1.0 multiply_bitcast_fusion
  56.8 0.2 copy.41
  57.0 0.2 slice.108
  57.2 1.0 select_maximum_fusion
  58.3 24.2 %shard_map.122 = f32[2,128,128]{2,1,0:T(8,128)} custom-call(f32[512,400]{1,0:T(8,128)} %bitcast.69, s32[128,128]{1,0:T(8,128)} %cell_ref.3, f32[128,4,128]{2,1,0:T(4,128)} %weight_ref.3, f32[2,128,128]{2,1,0:T(8,128)} %scale_ref.1), custom_call_target="tpu_custom_call" | custom-call | flops 13421772800 | bytes 4194304 | tf_op jit(solution)/shard_map/pallas_call | solution.py:184
  82.5 1.3 convolution_bitcast_fusion
  83.8 0.2 copy.43
  84.0 21.9 %all_to_all.10 = f32[2,256,128]{2,0,1:T(2,128)S(1)} all-to-all(f32[2,256,128]{2,0,1:T(2,128)S(1)} %copy.43), channel_id=1, replica_groups=mesh['lat'=8,'lon'=16] {'lat','lon'}, dimensions={1} | all-to-all | bytes 524288 | tf_op jit(solution)/shard_map/all_to_all | solution.py:343
  106.0 0.4 fusion.11
  106.4 0.2 copy.45
  106.6 15.2 %all_to_all.11 = f32[2,256,128]{2,0,1:T(2,128)S(1)} all-to-all(f32[2,256,128]{2,0,1:T(2,128)S(1)} %copy.45), channel_id=1, replica_groups=mesh['lat'=8,'lon'=16] {'lat','lon'}, dimensions={1} | all-to-all | bytes 524288 | tf_op jit(solution)/shard_map/all_to_all | solution.py:341
  121.8 0.9 fusion.8.value_ref
  122.8 17.5 %shard_map.123 = f32[2,400,128]{2,1,0:T(8,128)} custom-call(f32[2,128,128]{2,1,0:T(8,128)} %fusion.8.value_ref, s32[128,128]{1,0:T(8,128)} %cell_ref.3, f32[128,4,128]{2,1,0:T(4,128)} %weight_ref.3), custom_call_target="tpu_custom_call" | custom-call | flops 13421772800 | bytes 4194304 | tf_op jit(solution)/shard_map/pallas_call | solution.py:206
  140.2 1.1 copy_multiply_fusion
  141.5 2.6 %collective-permute-start.4 = (f32[2,50,8,4]{3,1,2,0:T(8,128)S(1)}, f32[2,50,8,4]{3,1,2,0:T(8,128)S(1)}, u32[]{:S(2)}, u32[]{:S(2)}) collective-permute-start(f32[2,50,8,4]{3,1,2,0:T(8,128)S(1)} %get-tuple-element.34), channel_id=1, source_target_pairs={{0,16},{16,32},{32,48},{48,64},{64,80},{80,96},{96,112},{1,17},{17... | collective-permute-start | bytes 38408 | tf_op jit(solution)/shard_map/ppermute | solution.py:24
  144.2 1.9 collective-permute-start.5
  146.1 3.5 %collective-permute-done.4 = f32[2,50,8,4]{3,1,2,0:T(8,128)S(1)} collective-permute-done((f32[2,50,8,4]{3,1,2,0:T(8,128)S(1)}, f32[2,50,8,4]{3,1,2,0:T(8,128)S(1)}, u32[]{:S(2)}, u32[]{:S(2)}) %collective-permute-start.4) | collective-permute-done | bytes 12832 | tf_op jit(solution)/shard_map/ppermute | solution.py:24
  149.6 4.7 %collective-permute-done.5 = f32[2,50,8,4]{3,1,2,0:T(8,128)S(1)} collective-permute-done((f32[2,50,8,4]{3,1,2,0:T(8,128)S(1)}, f32[2,50,8,4]{3,1,2,0:T(8,128)S(1)}, u32[]{:S(2)}, u32[]{:S(2)}) %collective-permute-start.5) | collective-permute-done | bytes 12832 | tf_op jit(solution)/shard_map/ppermute | solution.py:25
  154.3 0.5 pad_maximum_fusion.3
  154.9 0.4 collective-permute-start.6
  155.3 4.5 %collective-permute-start.7 = (f32[2,50,4,256]{3,1,2,0:T(8,128)S(1)}, f32[2,50,4,256]{3,1,2,0:T(8,128)S(1)}, u32[]{:S(2)}, u32[]{:S(2)}) collective-permute-start(f32[2,50,4,256]{3,1,2,0:T(8,128)S(1)} %get-tuple-element.31), channel_id=1, source_target_pairs={{1,0},{2,1},{3,2},{4,3},{5,4},{6,5},{7,6},{8,7},{9,8},{10,9},{11,1... | collective-permute-start | bytes 1228808 | tf_op jit(solution)/shard_map/ppermute | solution.py:25
  159.8 5.9 %collective-permute-done.6 = f32[2,50,4,256]{3,1,2,0:T(8,128)S(1)} collective-permute-done((f32[2,50,4,256]{3,1,2,0:T(8,128)S(1)}, f32[2,50,4,256]{3,1,2,0:T(8,128)S(1)}, u32[]{:S(2)}, u32[]{:S(2)}) %collective-permute-start.6) | collective-permute-done | bytes 409632 | tf_op jit(solution)/shard_map/ppermute | solution.py:24
  165.6 0.6 pad_maximum_fusion.1
  166.2 1.7 copy.49
  167.9 8.2 %shard_map.124 = f32[100,8,128]{2,1,0:T(8,128)} custom-call(f32[100,16,256]{2,1,0:T(8,128)} %bitcast.61, f32[100,16,256]{2,1,0:T(8,128)} %bitcast.56, f32[100,16,256]{2,1,0:T(8,128)} %bitcast.54, f32[100,16,256]{2,1,0:T(8,128)} %bitcast.52, f32[100,16,256]{2,1,0:T(8,128)} %bitcast.50), custom_call_target="tpu_custom_call" | custom-call | flops 22937600 | bytes 9830400 | tf_op jit(solution)/shard_map/pallas_call | solution.py:81
  176.1 1.9 multiply_reduce_fusion.3
  177.9 2.6 %maximum_bitcast_fusion = f32[1,4]{1,0:T(1,128)S(1)} fusion(f32[1]{0:T(128)} %bitcast.26, f32[1]{0:T(128)} %bitcast.25, f32[1]{0:T(128)} %bitcast.24, f32[1]{0:T(128)} %bitcast), kind=kLoop, calls=%fused_computation.47 | loop fusion | flops 12 | bytes 32 | tf_op jit(solution)/shard_map/reshape.48
  180.5 0.6 scatter.4.part_ref
  181.1 17.6 %shard_map.125 = f32[8,128]{1,0:T(8,128)} custom-call(f32[8,128]{1,0:T(8,128)} %scatter.4.part_ref), custom_call_target="tpu_custom_call" | custom-call | tf_op jit(solution)/shard_map/pallas_call | solution.py:278
  198.7 1.4 fusion.24
  204.1 1.1 multiply_add_fusion
  (26 shorter events, 0.6 us)
Async XLA Ops:
  0.6 105.3 %copy-start = (f32[128,128]{1,0:T(8,128)S(1)}, f32[128,128]{1,0:T(8,128)}, u32[]{:S(2)}) copy-start(f32[128,128]{1,0:T(8,128)} %param.21) | copy-start | bytes 196612
  2.7 6.9 %collective-permute-start = (f32[2,2,50,8,4]{2,3,4,1,0:T(8,128)S(1)}, f32[2,2,50,8,4]{2,3,4,1,0:T(8,128)S(1)}, u32[]{:S(2)}, u32[]{:S(2)}) collective-permute-start(f32[2,2,50,8,4]{2,3,4,1,0:T(8,128)S(1)} %copy.52), channel_id=1, source_target_pairs={{0,16},{16,32},{32,48},{48,64},{64,80},{80,96},{96,112},{1,17},{17... | collective-permute-start | bytes 76808 | tf_op jit(solution)/shard_map/ppermute | solution.py:24
  7.3 6.5 %copy-start.1 = (f32[2,50,8,128]{3,2,1,0:T(8,128)S(1)}, f32[2,50,8,128]{3,2,1,0:T(8,128)}, u32[]{:S(2)}) copy-start(f32[2,50,8,128]{3,2,1,0:T(8,128)} %param.14) | copy-start | bytes 1228804
  7.3 6.5 %copy-start.2 = (f32[2,50,8,128]{3,2,1,0:T(8,128)S(1)}, f32[2,50,8,128]{3,2,1,0:T(8,128)}, u32[]{:S(2)}) copy-start(f32[2,50,8,128]{3,2,1,0:T(8,128)} %param.15) | copy-start | bytes 1228804
  7.7 5.6 %collective-permute-start.1 = (f32[2,2,50,8,4]{2,3,4,1,0:T(8,128)S(1)}, f32[2,2,50,8,4]{2,3,4,1,0:T(8,128)S(1)}, u32[]{:S(2)}, u32[]{:S(2)}) collective-permute-start(f32[2,2,50,8,4]{2,3,4,1,0:T(8,128)S(1)} %copy.53), channel_id=1, source_target_pairs={{16,0},{32,16},{48,32},{64,48},{80,64},{96,80},{112,96},{17,1},{33... | collective-permute-start | bytes 76808 | tf_op jit(solution)/shard_map/ppermute | solution.py:25
  14.7 7.4 %copy-start.7 = (s32[128,1]{0,1:T(1,128)S(1)}, s32[128,1]{0,1:T(1,128)}, u32[]{:S(2)}) copy-start(s32[128,1]{0,1:T(1,128)} %param.20) | copy-start | bytes 1540
  16.2 22.5 %collective-permute-start.2 = (f32[2,2,50,4,256]{4,3,2,1,0:T(4,128)}, f32[2,2,50,4,256]{4,3,2,1,0:T(4,128)}, u32[]{:S(2)}, u32[]{:S(2)}) collective-permute-start(f32[2,2,50,4,256]{4,3,2,1,0:T(4,128)} %get-tuple-element.28), channel_id=1, source_target_pairs={{0,1},{1,2},{2,3},{3,4},{4,5},{5,6},{6,7},{7,8},{8,9},{9,10},{10,1... | collective-permute-start | bytes 2457608 | tf_op jit(solution)/shard_map/ppermute | solution.py:24
  17.4 21.3 %collective-permute-start.3 = (f32[2,2,50,4,256]{4,3,2,1,0:T(4,128)}, f32[2,2,50,4,256]{4,3,2,1,0:T(4,128)}, u32[]{:S(2)}, u32[]{:S(2)}) collective-permute-start(f32[2,2,50,4,256]{4,3,2,1,0:T(4,128)} %get-tuple-element.29), channel_id=1, source_target_pairs={{1,0},{2,1},{3,2},{4,3},{5,4},{6,5},{7,6},{8,7},{9,8},{10,9},{11,1... | collective-permute-start | bytes 2457608 | tf_op jit(solution)/shard_map/ppermute | solution.py:25
  47.6 8.2 %copy-start.3 = (f32[2,50,8,128]{3,2,1,0:T(8,128)S(1)}, f32[2,50,8,128]{3,2,1,0:T(8,128)}, u32[]{:S(2)}) copy-start(f32[2,50,8,128]{3,2,1,0:T(8,128)} %param.16) | copy-start | bytes 1228804
  82.5 39.3 %copy-start.6 = (f32[2,128,128]{2,1,0:T(8,128)S(1)}, f32[2,128,128]{2,1,0:T(8,128)}, u32[]{:S(2)}) copy-start(f32[2,128,128]{2,1,0:T(8,128)} %scale_ref.1) | copy-start | bytes 393220
  141.5 8.0 %collective-permute-start.4 = (f32[2,50,8,4]{3,1,2,0:T(8,128)S(1)}, f32[2,50,8,4]{3,1,2,0:T(8,128)S(1)}, u32[]{:S(2)}, u32[]{:S(2)}) collective-permute-start(f32[2,50,8,4]{3,1,2,0:T(8,128)S(1)} %get-tuple-element.34), channel_id=1, source_target_pairs={{0,16},{16,32},{32,48},{48,64},{64,80},{80,96},{96,112},{1,17},{17... | collective-permute-start | bytes 38408 | tf_op jit(solution)/shard_map/ppermute | solution.py:24
  144.2 10.1 %collective-permute-start.5 = (f32[2,50,8,4]{3,1,2,0:T(8,128)S(1)}, f32[2,50,8,4]{3,1,2,0:T(8,128)S(1)}, u32[]{:S(2)}, u32[]{:S(2)}) collective-permute-start(f32[2,50,8,4]{3,1,2,0:T(8,128)S(1)} %get-tuple-element.35), channel_id=1, source_target_pairs={{16,0},{32,16},{48,32},{64,48},{80,64},{96,80},{112,96},{17,1},{33... | collective-permute-start | bytes 38408 | tf_op jit(solution)/shard_map/ppermute | solution.py:25
  154.9 10.7 %collective-permute-start.6 = (f32[2,50,4,256]{3,1,2,0:T(8,128)S(1)}, f32[2,50,4,256]{3,1,2,0:T(8,128)S(1)}, u32[]{:S(2)}, u32[]{:S(2)}) collective-permute-start(f32[2,50,4,256]{3,1,2,0:T(8,128)S(1)} %get-tuple-element.30), channel_id=1, source_target_pairs={{0,1},{1,2},{2,3},{3,4},{4,5},{5,6},{6,7},{7,8},{8,9},{9,10},{10,1... | collective-permute-start | bytes 1228808 | tf_op jit(solution)/shard_map/ppermute | solution.py:24
  155.3 10.3 %collective-permute-start.7 = (f32[2,50,4,256]{3,1,2,0:T(8,128)S(1)}, f32[2,50,4,256]{3,1,2,0:T(8,128)S(1)}, u32[]{:S(2)}, u32[]{:S(2)}) collective-permute-start(f32[2,50,4,256]{3,1,2,0:T(8,128)S(1)} %get-tuple-element.31), channel_id=1, source_target_pairs={{1,0},{2,1},{3,2},{4,3},{5,4},{6,5},{7,6},{8,7},{9,8},{10,9},{11,1... | collective-permute-start | bytes 1228808 | tf_op jit(solution)/shard_map/ppermute | solution.py:25
  167.9 8.2 %copy-start.4 = (f32[2,50,8,128]{3,2,1,0:T(8,128)S(1)}, f32[2,50,8,128]{3,2,1,0:T(8,128)}, u32[]{:S(2)}) copy-start(f32[2,50,8,128]{3,2,1,0:T(8,128)} %param.13) | copy-start | bytes 1228804
  176.0 28.0 %copy-start.5 = (f32[2,50,8,128]{3,2,1,0:T(8,128)S(1)}, f32[2,50,8,128]{3,2,1,0:T(8,128)}, u32[]{:S(2)}) copy-start(f32[2,50,8,128]{3,2,1,0:T(8,128)} %param.12) | copy-start | bytes 1228804

commit v7 on v5

--- a/solution.py
+++ b/solution.py
@@ -69,7 +69,7 @@
     return tuple(pad_lanes(c.reshape((-1,) + c.shape[-2:])) for c in coeffs)
 
 
-def diffuse(field, coeffs, planes_per_step=50):
+def diffuse(field, coeffs, planes_per_step=25):
     lead = field.shape[:-2]
     flat = pad_lanes(field.reshape((-1,) + field.shape[-2:]))
     planes, rows, lanes = flat.shape

time: 202 us -> 201 us (level)
  transfers between devices with their start and end apart: 8 -> 8, of which waited for: 6 -> 6; matrix products, arithmetic and copies ran while one was open for 0% -> 1% of each run, Pallas kernels for 0% -> 0%
where the time goes in v7:
time: 201 us; the launch traced here: 200 us
  Pallas kernels  74.9 us (37%)
  blocking collectives  37.1 us (18%)
  waiting for transfers between devices  33.1 us (16%)
  starting transfers between devices  22.2 us (11%)
  other arithmetic  16.9 us (8%)
  local copies, waits for them, and re-layouts  8.49 us (4%)
  between operations  4.76 us (2%)
  matrix products  2.8 us (1%)
    ppermute x4, waiting for transfers between devices, widen_halo(): lax.ppermute(lax.slice_in_dim(value, length - width, length, axis=dim), a...  25.1 us
    pallas_call x1, Pallas kernels, observe_pallas(): pl.pallas_call(kernel, grid=(block_count // group,), in_specs=[pl.BlockSp...  24.2 us
    all_to_all x1, blocking collectives, shards(): lax.all_to_all(buffer, ('lat', 'lon'), split_axis=1, concat_axis=1, tiled...  21.9 us
    pallas_call x1, Pallas kernels, allreduce_pallas(): pl.pallas_call(kernel, in_specs=[pl.BlockSpec(memory_space=pltpu.VMEM)],...  17.6 us
    pallas_call x1, Pallas kernels, spread_pallas(): pl.pallas_call(kernel, grid=(block_count // group,), in_specs=[pl.BlockSp...  17.5 us
    pallas_call x2, Pallas kernels, diffuse(): pl.pallas_call(functools.partial(diffuse_kernel, STEPS), grid=(planes //...  15.6 us
    all_to_all x1, blocking collectives, shards(): lax.all_to_all(mix_blocks(lax.all_to_all(buffer, ('lat', 'lon'), split_ax...  15.2 us
    ppermute x4, starting transfers between devices, widen_halo(): lax.ppermute(lax.slice_in_dim(value, 0, width, axis=dim), axis, down)  13.3 us
  transfers between devices with their start and end apart: 8, of which 6 were waited for; matrix products, arithmetic and copies ran while one was open for 1% of the time, Pallas kernels for 0%

profile of v7, /device:TPU:1, one launch (start us, length us, event | category | flops | bytes accessed | tf_op | source)
XLA Modules:
  0.0 200.2 jit_solution(9043872246988494531)
XLA Ops:
  0.6 1.7 slice_maximum_fusion
  2.4 0.4 copy.52
  2.7 4.6 %collective-permute-start = (f32[2,2,50,8,4]{2,3,4,1,0:T(8,128)S(1)}, f32[2,2,50,8,4]{2,3,4,1,0:T(8,128)S(1)}, u32[]{:S(2)}, u32[]{:S(2)}) collective-permute-start(f32[2,2,50,8,4]{2,3,4,1,0:T(8,128)S(1)} %copy.52), channel_id=1, source_target_pairs={{0,16},{16,32},{32,48},{48,64},{64,80},{80,96},{96,112},{1,17},{17... | collective-permute-start | bytes 76808 | tf_op jit(solution)/shard_map/ppermute | solution.py:24
  7.3 0.4 copy.53
  7.7 1.9 collective-permute-start.1
  9.7 0.4 copy.39
  10.1 3.2 %collective-permute-done.1 = f32[2,2,50,8,4]{2,3,4,1,0:T(8,128)S(1)} collective-permute-done((f32[2,2,50,8,4]{2,3,4,1,0:T(8,128)S(1)}, f32[2,2,50,8,4]{2,3,4,1,0:T(8,128)S(1)}, u32[]{:S(2)}, u32[]{:S(2)}) %collective-permute-start.1) | collective-permute-done | bytes 25632 | tf_op jit(solution)/shard_map/ppermute | solution.py:25
  13.3 0.4 copy.40
  13.7 0.7 pad_maximum_fusion.2
  14.5 0.2 fusion.21
  14.7 1.3 collective-permute-start.2
  16.0 5.0 %collective-permute-start.3 = (f32[2,2,50,4,136]{4,3,2,1,0:T(4,128)S(1)}, f32[2,2,50,4,136]{4,3,2,1,0:T(4,128)S(1)}, u32[]{:S(2)}, u32[]{:S(2)}) collective-permute-start(f32[2,2,50,4,136]{4,3,2,1,0:T(4,128)S(1)} %get-tuple-element.29), channel_id=1, source_target_pairs={{1,0},{2,1},{3,2},{4,3},{5,4},{6,5},{7,6},{8,7},{9,8},{10,9},{11,1... | collective-permute-start | bytes 1305608 | tf_op jit(solution)/shard_map/ppermute | solution.py:25
  21.2 15.8 %collective-permute-done.2 = f32[2,2,50,4,136]{4,3,2,1,0:T(4,128)S(1)} collective-permute-done((f32[2,2,50,4,136]{4,3,2,1,0:T(4,128)S(1)}, f32[2,2,50,4,136]{4,3,2,1,0:T(4,128)S(1)}, u32[]{:S(2)}, u32[]{:S(2)}) %collective-permute-start.2) | collective-permute-done | bytes 435232 | tf_op jit(solution)/shard_map/ppermute | solution.py:24
  37.1 1.6 pad_maximum_fusion
  38.7 0.3 slice_bitcast_fusion
  39.0 1.3 pad.17.field_ref
  40.4 3.2 %fusion.7 = (f32[2,50,16,256]{3,2,1,0:T(8,128)}, f32[2,50,16,256]{3,2,1,0:T(8,128)}, f32[2,50,16,256]{3,2,1,0:T(8,128)}, f32[2,50,16,256]{3,2,1,0:T(8,128)}) fusion(f32[2,50,16,136]{3,2,1,0:T(8,128)S(1)} %get-tuple-element.22, f32[256]{0:T(256)S(1)} %and_select_fusion), kind=kLoop, calls=%fused_computation.14 | loop fusion | flops 3276800 | bytes 7425024 | tf_op jit(solution)/shard_map/mul | solution.py:43
  43.6 7.8 %shard_map.121 = f32[100,8,128]{2,1,0:T(8,128)} custom-call(f32[100,16,256]{2,1,0:T(8,128)} %pad.17.field_ref, f32[100,16,256]{2,1,0:T(8,128)} %bitcast.55, f32[100,16,256]{2,1,0:T(8,128)} %bitcast.51, f32[100,16,256]{2,1,0:T(8,128)} %bitcast.53, f32[100,16,256]{2,1,0:T(8,128)} %bitcast.49), custom_call_target="tpu_custom_call" | custom-call | flops 22937600 | bytes 9830400 | tf_op jit(solution)/shard_map/pallas_call | solution.py:78
  51.4 1.0 multiply_bitcast_fusion
  52.9 1.0 select_maximum_fusion
  53.9 24.2 %shard_map.122 = f32[2,128,128]{2,1,0:T(8,128)} custom-call(f32[512,400]{1,0:T(8,128)} %bitcast.69, s32[128,128]{1,0:T(8,128)} %cell_ref.3, f32[128,4,128]{2,1,0:T(4,128)} %weight_ref.3, f32[2,128,128]{2,1,0:T(8,128)} %scale_ref.1), custom_call_target="tpu_custom_call" | custom-call | flops 13421772800 | bytes 4194304 | tf_op jit(solution)/shard_map/pallas_call | solution.py:181
  78.1 1.3 convolution_bitcast_fusion
  79.4 0.2 copy.43
  79.6 21.9 %all_to_all.10 = f32[2,256,128]{2,0,1:T(2,128)S(1)} all-to-all(f32[2,256,128]{2,0,1:T(2,128)S(1)} %copy.43), channel_id=1, replica_groups=mesh['lat'=8,'lon'=16] {'lat','lon'}, dimensions={1} | all-to-all | bytes 524288 | tf_op jit(solution)/shard_map/all_to_all | solution.py:340
  101.5 0.4 fusion.11
  101.9 0.2 copy.45
  102.1 15.2 %all_to_all.11 = f32[2,256,128]{2,0,1:T(2,128)S(1)} all-to-all(f32[2,256,128]{2,0,1:T(2,128)S(1)} %copy.45), channel_id=1, replica_groups=mesh['lat'=8,'lon'=16] {'lat','lon'}, dimensions={1} | all-to-all | bytes 524288 | tf_op jit(solution)/shard_map/all_to_all | solution.py:338
  117.4 0.9 fusion.8.value_ref
  118.3 17.5 %shard_map.123 = f32[2,400,128]{2,1,0:T(8,128)} custom-call(f32[2,128,128]{2,1,0:T(8,128)} %fusion.8.value_ref, s32[128,128]{1,0:T(8,128)} %cell_ref.3, f32[128,4,128]{2,1,0:T(4,128)} %weight_ref.3), custom_call_target="tpu_custom_call" | custom-call | flops 13421772800 | bytes 4194304 | tf_op jit(solution)/shard_map/pallas_call | solution.py:203
  135.7 1.1 copy_multiply_fusion
  137.1 2.6 %collective-permute-start.4 = (f32[2,50,8,4]{3,1,2,0:T(8,128)S(1)}, f32[2,50,8,4]{3,1,2,0:T(8,128)S(1)}, u32[]{:S(2)}, u32[]{:S(2)}) collective-permute-start(f32[2,50,8,4]{3,1,2,0:T(8,128)S(1)} %get-tuple-element.34), channel_id=1, source_target_pairs={{0,16},{16,32},{32,48},{48,64},{64,80},{80,96},{96,112},{1,17},{17... | collective-permute-start | bytes 38408 | tf_op jit(solution)/shard_map/ppermute | solution.py:24
  139.7 1.9 collective-permute-start.5
  141.6 3.5 %collective-permute-done.4 = f32[2,50,8,4]{3,1,2,0:T(8,128)S(1)} collective-permute-done((f32[2,50,8,4]{3,1,2,0:T(8,128)S(1)}, f32[2,50,8,4]{3,1,2,0:T(8,128)S(1)}, u32[]{:S(2)}, u32[]{:S(2)}) %collective-permute-start.4) | collective-permute-done | bytes 12832 | tf_op jit(solution)/shard_map/ppermute | solution.py:24
  145.1 4.7 %collective-permute-done.5 = f32[2,50,8,4]{3,1,2,0:T(8,128)S(1)} collective-permute-done((f32[2,50,8,4]{3,1,2,0:T(8,128)S(1)}, f32[2,50,8,4]{3,1,2,0:T(8,128)S(1)}, u32[]{:S(2)}, u32[]{:S(2)}) %collective-permute-start.5) | collective-permute-done | bytes 12832 | tf_op jit(solution)/shard_map/ppermute | solution.py:25
  149.8 0.4 pad_maximum_fusion.3
  150.3 0.4 collective-permute-start.6
  150.7 4.5 %collective-permute-start.7 = (f32[2,50,4,136]{3,1,2,0:T(8,128)S(1)}, f32[2,50,4,136]{3,1,2,0:T(8,128)S(1)}, u32[]{:S(2)}, u32[]{:S(2)}) collective-permute-start(f32[2,50,4,136]{3,1,2,0:T(8,128)S(1)} %get-tuple-element.31), channel_id=1, source_target_pairs={{1,0},{2,1},{3,2},{4,3},{5,4},{6,5},{7,6},{8,7},{9,8},{10,9},{11,1... | collective-permute-start | bytes 652808 | tf_op jit(solution)/shard_map/ppermute | solution.py:25
  155.2 5.9 %collective-permute-done.6 = f32[2,50,4,136]{3,1,2,0:T(8,128)S(1)} collective-permute-done((f32[2,50,4,136]{3,1,2,0:T(8,128)S(1)}, f32[2,50,4,136]{3,1,2,0:T(8,128)S(1)}, u32[]{:S(2)}, u32[]{:S(2)}) %collective-permute-start.6) | collective-permute-done | bytes 217632 | tf_op jit(solution)/shard_map/ppermute | solution.py:24
  161.0 0.4 pad_maximum_fusion.1
  161.5 0.5 copy.49
  162.0 1.3 pad.19.field_ref
  163.3 7.8 %shard_map.124 = f32[100,8,128]{2,1,0:T(8,128)} custom-call(f32[100,16,256]{2,1,0:T(8,128)} %pad.19.field_ref, f32[100,16,256]{2,1,0:T(8,128)} %bitcast.56, f32[100,16,256]{2,1,0:T(8,128)} %bitcast.52, f32[100,16,256]{2,1,0:T(8,128)} %bitcast.54, f32[100,16,256]{2,1,0:T(8,128)} %bitcast.50), custom_call_target="tpu_custom_call" | custom-call | flops 22937600 | bytes 9830400 | tf_op jit(solution)/shard_map/pallas_call | solution.py:78
  171.1 1.9 multiply_reduce_fusion.3
  173.0 2.6 %maximum_bitcast_fusion = f32[1,4]{1,0:T(1,128)S(1)} fusion(f32[1]{0:T(128)} %bitcast.26, f32[1]{0:T(128)} %bitcast.25, f32[1]{0:T(128)} %bitcast.24, f32[1]{0:T(128)} %bitcast), kind=kLoop, calls=%fused_computation.48 | loop fusion | flops 12 | bytes 32 | tf_op jit(solution)/shard_map/reshape.48
  175.6 0.6 scatter.4.part_ref
  176.2 17.6 %shard_map.125 = f32[8,128]{1,0:T(8,128)} custom-call(f32[8,128]{1,0:T(8,128)} %scatter.4.part_ref), custom_call_target="tpu_custom_call" | custom-call | tf_op jit(solution)/shard_map/pallas_call | solution.py:275
  193.8 1.4 fusion.24
  199.1 1.1 multiply_add_fusion
  (26 shorter events, 1.0 us)
Async XLA Ops:
  0.6 100.9 %copy-start = (f32[128,128]{1,0:T(8,128)S(1)}, f32[128,128]{1,0:T(8,128)}, u32[]{:S(2)}) copy-start(f32[128,128]{1,0:T(8,128)} %param.21) | copy-start | bytes 196612
  2.3 11.4 %copy-start.1 = (f32[2,50,8,128]{3,2,1,0:T(8,128)S(1)}, f32[2,50,8,128]{3,2,1,0:T(8,128)}, u32[]{:S(2)}) copy-start(f32[2,50,8,128]{3,2,1,0:T(8,128)} %param.14) | copy-start | bytes 1228804
  2.3 11.4 %copy-start.2 = (f32[2,50,8,128]{3,2,1,0:T(8,128)S(1)}, f32[2,50,8,128]{3,2,1,0:T(8,128)}, u32[]{:S(2)}) copy-start(f32[2,50,8,128]{3,2,1,0:T(8,128)} %param.15) | copy-start | bytes 1228804
  2.7 6.9 %collective-permute-start = (f32[2,2,50,8,4]{2,3,4,1,0:T(8,128)S(1)}, f32[2,2,50,8,4]{2,3,4,1,0:T(8,128)S(1)}, u32[]{:S(2)}, u32[]{:S(2)}) collective-permute-start(f32[2,2,50,8,4]{2,3,4,1,0:T(8,128)S(1)} %copy.52), channel_id=1, source_target_pairs={{0,16},{16,32},{32,48},{48,64},{64,80},{80,96},{96,112},{1,17},{17... | collective-permute-start | bytes 76808 | tf_op jit(solution)/shard_map/ppermute | solution.py:24
  7.7 5.6 %collective-permute-start.1 = (f32[2,2,50,8,4]{2,3,4,1,0:T(8,128)S(1)}, f32[2,2,50,8,4]{2,3,4,1,0:T(8,128)S(1)}, u32[]{:S(2)}, u32[]{:S(2)}) collective-permute-start(f32[2,2,50,8,4]{2,3,4,1,0:T(8,128)S(1)} %copy.53), channel_id=1, source_target_pairs={{16,0},{32,16},{48,32},{64,48},{80,64},{96,80},{112,96},{17,1},{33... | collective-permute-start | bytes 76808 | tf_op jit(solution)/shard_map/ppermute | solution.py:25
  14.5 6.6 %copy-start.7 = (s32[128,1]{0,1:T(1,128)S(1)}, s32[128,1]{0,1:T(1,128)}, u32[]{:S(2)}) copy-start(s32[128,1]{0,1:T(1,128)} %param.20) | copy-start | bytes 1540
  14.7 22.3 %collective-permute-start.2 = (f32[2,2,50,4,136]{4,3,2,1,0:T(4,128)S(1)}, f32[2,2,50,4,136]{4,3,2,1,0:T(4,128)S(1)}, u32[]{:S(2)}, u32[]{:S(2)}) collective-permute-start(f32[2,2,50,4,136]{4,3,2,1,0:T(4,128)S(1)} %get-tuple-element.28), channel_id=1, source_target_pairs={{0,1},{1,2},{2,3},{3,4},{4,5},{5,6},{6,7},{7,8},{8,9},{9,10},{10,1... | collective-permute-start | bytes 1305608 | tf_op jit(solution)/shard_map/ppermute | solution.py:24
  16.0 21.1 %collective-permute-start.3 = (f32[2,2,50,4,136]{4,3,2,1,0:T(4,128)S(1)}, f32[2,2,50,4,136]{4,3,2,1,0:T(4,128)S(1)}, u32[]{:S(2)}, u32[]{:S(2)}) collective-permute-start(f32[2,2,50,4,136]{4,3,2,1,0:T(4,128)S(1)} %get-tuple-element.29), channel_id=1, source_target_pairs={{1,0},{2,1},{3,2},{4,3},{5,4},{6,5},{7,6},{8,7},{9,8},{10,9},{11,1... | collective-permute-start | bytes 1305608 | tf_op jit(solution)/shard_map/ppermute | solution.py:25
  43.6 7.8 %copy-start.3 = (f32[2,50,8,128]{3,2,1,0:T(8,128)S(1)}, f32[2,50,8,128]{3,2,1,0:T(8,128)}, u32[]{:S(2)}) copy-start(f32[2,50,8,128]{3,2,1,0:T(8,128)} %param.16) | copy-start | bytes 1228804
  78.1 39.3 %copy-start.6 = (f32[2,128,128]{2,1,0:T(8,128)S(1)}, f32[2,128,128]{2,1,0:T(8,128)}, u32[]{:S(2)}) copy-start(f32[2,128,128]{2,1,0:T(8,128)} %scale_ref.1) | copy-start | bytes 393220
  137.1 8.0 %collective-permute-start.4 = (f32[2,50,8,4]{3,1,2,0:T(8,128)S(1)}, f32[2,50,8,4]{3,1,2,0:T(8,128)S(1)}, u32[]{:S(2)}, u32[]{:S(2)}) collective-permute-start(f32[2,50,8,4]{3,1,2,0:T(8,128)S(1)} %get-tuple-element.34), channel_id=1, source_target_pairs={{0,16},{16,32},{32,48},{48,64},{64,80},{80,96},{96,112},{1,17},{17... | collective-permute-start | bytes 38408 | tf_op jit(solution)/shard_map/ppermute | solution.py:24
  139.7 10.1 %collective-permute-start.5 = (f32[2,50,8,4]{3,1,2,0:T(8,128)S(1)}, f32[2,50,8,4]{3,1,2,0:T(8,128)S(1)}, u32[]{:S(2)}, u32[]{:S(2)}) collective-permute-start(f32[2,50,8,4]{3,1,2,0:T(8,128)S(1)} %get-tuple-element.35), channel_id=1, source_target_pairs={{16,0},{32,16},{48,32},{64,48},{80,64},{96,80},{112,96},{17,1},{33... | collective-permute-start | bytes 38408 | tf_op jit(solution)/shard_map/ppermute | solution.py:25
  150.3 10.7 %collective-permute-start.6 = (f32[2,50,4,136]{3,1,2,0:T(8,128)S(1)}, f32[2,50,4,136]{3,1,2,0:T(8,128)S(1)}, u32[]{:S(2)}, u32[]{:S(2)}) collective-permute-start(f32[2,50,4,136]{3,1,2,0:T(8,128)S(1)} %get-tuple-element.30), channel_id=1, source_target_pairs={{0,1},{1,2},{2,3},{3,4},{4,5},{5,6},{6,7},{7,8},{8,9},{9,10},{10,1... | collective-permute-start | bytes 652808 | tf_op jit(solution)/shard_map/ppermute | solution.py:24
  150.7 10.3 %collective-permute-start.7 = (f32[2,50,4,136]{3,1,2,0:T(8,128)S(1)}, f32[2,50,4,136]{3,1,2,0:T(8,128)S(1)}, u32[]{:S(2)}, u32[]{:S(2)}) collective-permute-start(f32[2,50,4,136]{3,1,2,0:T(8,128)S(1)} %get-tuple-element.31), channel_id=1, source_target_pairs={{1,0},{2,1},{3,2},{4,3},{5,4},{6,5},{7,6},{8,7},{9,8},{10,9},{11,1... | collective-permute-start | bytes 652808 | tf_op jit(solution)/shard_map/ppermute | solution.py:25
  163.3 7.8 %copy-start.4 = (f32[2,50,8,128]{3,2,1,0:T(8,128)S(1)}, f32[2,50,8,128]{3,2,1,0:T(8,128)}, u32[]{:S(2)}) copy-start(f32[2,50,8,128]{3,2,1,0:T(8,128)} %param.13) | copy-start | bytes 1228804
  171.1 28.0 %copy-start.5 = (f32[2,50,8,128]{3,2,1,0:T(8,128)S(1)}, f32[2,50,8,128]{3,2,1,0:T(8,128)}, u32[]{:S(2)}) copy-start(f32[2,50,8,128]{3,2,1,0:T(8,128)} %param.12) | copy-start | bytes 1228804

commit v8 on v7

--- a/solution.py
+++ b/solution.py
@@ -69,7 +69,7 @@
     return tuple(pad_lanes(c.reshape((-1,) + c.shape[-2:])) for c in coeffs)
 
 
-def diffuse(field, coeffs, planes_per_step=25):
+def diffuse(field, coeffs, planes_per_step=20):
     lead = field.shape[:-2]
     flat = pad_lanes(field.reshape((-1,) + field.shape[-2:]))
     planes, rows, lanes = flat.shape

time: 201 us -> 202 us (level)
  transfers between devices with their start and end apart: 8 -> 8, of which waited for: 6 -> 6; matrix products, arithmetic and copies ran while one was open for 1% -> 0% of each run, Pallas kernels for 0% -> 0%
where the time goes in v8:
time: 202 us; the launch traced here: 201 us
  Pallas kernels  75.9 us (38%)
  blocking collectives  37.1 us (18%)
  waiting for transfers between devices  33.1 us (16%)
  starting transfers between devices  22.2 us (11%)
  other arithmetic  16.9 us (8%)
  local copies, waits for them, and re-layouts  8.49 us (4%)
  between operations  4.76 us (2%)
  matrix products  2.8 us (1%)
    ppermute x4, waiting for transfers between devices, widen_halo(): lax.ppermute(lax.slice_in_dim(value, length - width, length, axis=dim), a...  25.1 us
    pallas_call x1, Pallas kernels, observe_pallas(): pl.pallas_call(kernel, grid=(block_count // group,), in_specs=[pl.BlockSp...  24.2 us
    all_to_all x1, blocking collectives, shards(): lax.all_to_all(buffer, ('lat', 'lon'), split_axis=1, concat_axis=1, tiled...  21.8 us
    pallas_call x1, Pallas kernels, allreduce_pallas(): pl.pallas_call(kernel, in_specs=[pl.BlockSpec(memory_space=pltpu.VMEM)],...  17.6 us
    pallas_call x1, Pallas kernels, spread_pallas(): pl.pallas_call(kernel, grid=(block_count // group,), in_specs=[pl.BlockSp...  17.5 us
    pallas_call x2, Pallas kernels, diffuse(): pl.pallas_call(functools.partial(diffuse_kernel, STEPS), grid=(planes //...  16.6 us
    all_to_all x1, blocking collectives, shards(): lax.all_to_all(mix_blocks(lax.all_to_all(buffer, ('lat', 'lon'), split_ax...  15.2 us
    ppermute x4, starting transfers between devices, widen_halo(): lax.ppermute(lax.slice_in_dim(value, 0, width, axis=dim), axis, down)  13.3 us
  transfers between devices with their start and end apart: 8, of which 6 were waited for; matrix products, arithmetic and copies ran while one was open for 0% of the time, Pallas kernels for 0%

profile of v8, /device:TPU:1, one launch (start us, length us, event | category | flops | bytes accessed | tf_op | source)
XLA Modules:
  0.0 201.2 jit_solution(11858146171577593021)
XLA Ops:
  0.6 1.7 slice_maximum_fusion
  2.4 0.4 copy.52
  2.7 4.6 %collective-permute-start = (f32[2,2,50,8,4]{2,3,4,1,0:T(8,128)S(1)}, f32[2,2,50,8,4]{2,3,4,1,0:T(8,128)S(1)}, u32[]{:S(2)}, u32[]{:S(2)}) collective-permute-start(f32[2,2,50,8,4]{2,3,4,1,0:T(8,128)S(1)} %copy.52), channel_id=1, source_target_pairs={{0,16},{16,32},{32,48},{48,64},{64,80},{80,96},{96,112},{1,17},{17... | collective-permute-start | bytes 76808 | tf_op jit(solution)/shard_map/ppermute | solution.py:24
  7.3 0.4 copy.53
  7.7 1.9 collective-permute-start.1
  9.7 0.4 copy.39
  10.1 3.2 %collective-permute-done.1 = f32[2,2,50,8,4]{2,3,4,1,0:T(8,128)S(1)} collective-permute-done((f32[2,2,50,8,4]{2,3,4,1,0:T(8,128)S(1)}, f32[2,2,50,8,4]{2,3,4,1,0:T(8,128)S(1)}, u32[]{:S(2)}, u32[]{:S(2)}) %collective-permute-start.1) | collective-permute-done | bytes 25632 | tf_op jit(solution)/shard_map/ppermute | solution.py:25
  13.3 0.4 copy.40
  13.7 0.7 pad_maximum_fusion.2
  14.5 0.2 fusion.21
  14.7 1.3 collective-permute-start.2
  16.0 5.0 %collective-permute-start.3 = (f32[2,2,50,4,136]{4,3,2,1,0:T(4,128)S(1)}, f32[2,2,50,4,136]{4,3,2,1,0:T(4,128)S(1)}, u32[]{:S(2)}, u32[]{:S(2)}) collective-permute-start(f32[2,2,50,4,136]{4,3,2,1,0:T(4,128)S(1)} %get-tuple-element.29), channel_id=1, source_target_pairs={{1,0},{2,1},{3,2},{4,3},{5,4},{6,5},{7,6},{8,7},{9,8},{10,9},{11,1... | collective-permute-start | bytes 1305608 | tf_op jit(solution)/shard_map/ppermute | solution.py:25
  21.2 15.8 %collective-permute-done.2 = f32[2,2,50,4,136]{4,3,2,1,0:T(4,128)S(1)} collective-permute-done((f32[2,2,50,4,136]{4,3,2,1,0:T(4,128)S(1)}, f32[2,2,50,4,136]{4,3,2,1,0:T(4,128)S(1)}, u32[]{:S(2)}, u32[]{:S(2)}) %collective-permute-start.2) | collective-permute-done | bytes 435232 | tf_op jit(solution)/shard_map/ppermute | solution.py:24
  37.1 1.6 pad_maximum_fusion
  38.7 0.3 slice_bitcast_fusion
  39.0 1.3 pad.17.field_ref
  40.4 3.2 %fusion.7 = (f32[2,50,16,256]{3,2,1,0:T(8,128)}, f32[2,50,16,256]{3,2,1,0:T(8,128)}, f32[2,50,16,256]{3,2,1,0:T(8,128)}, f32[2,50,16,256]{3,2,1,0:T(8,128)}) fusion(f32[2,50,16,136]{3,2,1,0:T(8,128)S(1)} %get-tuple-element.22, f32[256]{0:T(256)S(1)} %and_select_fusion), kind=kLoop, calls=%fused_computation.14 | loop fusion | flops 3276800 | bytes 7425024 | tf_op jit(solution)/shard_map/mul | solution.py:43
  43.6 8.3 %shard_map.121 = f32[100,8,128]{2,1,0:T(8,128)} custom-call(f32[100,16,256]{2,1,0:T(8,128)} %pad.17.field_ref, f32[100,16,256]{2,1,0:T(8,128)} %bitcast.55, f32[100,16,256]{2,1,0:T(8,128)} %bitcast.51, f32[100,16,256]{2,1,0:T(8,128)} %bitcast.53, f32[100,16,256]{2,1,0:T(8,128)} %bitcast.49), custom_call_target="tpu_custom_call" | custom-call | flops 22937600 | bytes 9830400 | tf_op jit(solution)/shard_map/pallas_call | solution.py:78
  51.9 1.0 multiply_bitcast_fusion
  53.4 1.0 select_maximum_fusion
  54.4 24.2 %shard_map.122 = f32[2,128,128]{2,1,0:T(8,128)} custom-call(f32[512,400]{1,0:T(8,128)} %bitcast.69, s32[128,128]{1,0:T(8,128)} %cell_ref.3, f32[128,4,128]{2,1,0:T(4,128)} %weight_ref.3, f32[2,128,128]{2,1,0:T(8,128)} %scale_ref.1), custom_call_target="tpu_custom_call" | custom-call | flops 13421772800 | bytes 4194304 | tf_op jit(solution)/shard_map/pallas_call | solution.py:181
  78.6 1.3 convolution_bitcast_fusion
  79.9 0.2 copy.43
  80.1 21.8 %all_to_all.10 = f32[2,256,128]{2,0,1:T(2,128)S(1)} all-to-all(f32[2,256,128]{2,0,1:T(2,128)S(1)} %copy.43), channel_id=1, replica_groups=mesh['lat'=8,'lon'=16] {'lat','lon'}, dimensions={1} | all-to-all | bytes 524288 | tf_op jit(solution)/shard_map/all_to_all | solution.py:340
  102.0 0.4 fusion.11
  102.4 0.2 copy.45
  102.6 15.2 %all_to_all.11 = f32[2,256,128]{2,0,1:T(2,128)S(1)} all-to-all(f32[2,256,128]{2,0,1:T(2,128)S(1)} %copy.45), channel_id=1, replica_groups=mesh['lat'=8,'lon'=16] {'lat','lon'}, dimensions={1} | all-to-all | bytes 524288 | tf_op jit(solution)/shard_map/all_to_all | solution.py:338
  117.8 0.9 fusion.8.value_ref
  118.8 17.5 %shard_map.123 = f32[2,400,128]{2,1,0:T(8,128)} custom-call(f32[2,128,128]{2,1,0:T(8,128)} %fusion.8.value_ref, s32[128,128]{1,0:T(8,128)} %cell_ref.3, f32[128,4,128]{2,1,0:T(4,128)} %weight_ref.3), custom_call_target="tpu_custom_call" | custom-call | flops 13421772800 | bytes 4194304 | tf_op jit(solution)/shard_map/pallas_call | solution.py:203
  136.2 1.1 copy_multiply_fusion
  137.5 2.6 %collective-permute-start.4 = (f32[2,50,8,4]{3,1,2,0:T(8,128)S(1)}, f32[2,50,8,4]{3,1,2,0:T(8,128)S(1)}, u32[]{:S(2)}, u32[]{:S(2)}) collective-permute-start(f32[2,50,8,4]{3,1,2,0:T(8,128)S(1)} %get-tuple-element.34), channel_id=1, source_target_pairs={{0,16},{16,32},{32,48},{48,64},{64,80},{80,96},{96,112},{1,17},{17... | collective-permute-start | bytes 38408 | tf_op jit(solution)/shard_map/ppermute | solution.py:24
  140.2 1.9 collective-permute-start.5
  142.1 3.5 %collective-permute-done.4 = f32[2,50,8,4]{3,1,2,0:T(8,128)S(1)} collective-permute-done((f32[2,50,8,4]{3,1,2,0:T(8,128)S(1)}, f32[2,50,8,4]{3,1,2,0:T(8,128)S(1)}, u32[]{:S(2)}, u32[]{:S(2)}) %collective-permute-start.4) | collective-permute-done | bytes 12832 | tf_op jit(solution)/shard_map/ppermute | solution.py:24
  145.6 4.7 %collective-permute-done.5 = f32[2,50,8,4]{3,1,2,0:T(8,128)S(1)} collective-permute-done((f32[2,50,8,4]{3,1,2,0:T(8,128)S(1)}, f32[2,50,8,4]{3,1,2,0:T(8,128)S(1)}, u32[]{:S(2)}, u32[]{:S(2)}) %collective-permute-start.5) | collective-permute-done | bytes 12832 | tf_op jit(solution)/shard_map/ppermute | solution.py:25
  150.3 0.4 pad_maximum_fusion.3
  150.8 0.4 collective-permute-start.6
  151.2 4.5 %collective-permute-start.7 = (f32[2,50,4,136]{3,1,2,0:T(8,128)S(1)}, f32[2,50,4,136]{3,1,2,0:T(8,128)S(1)}, u32[]{:S(2)}, u32[]{:S(2)}) collective-permute-start(f32[2,50,4,136]{3,1,2,0:T(8,128)S(1)} %get-tuple-element.31), channel_id=1, source_target_pairs={{1,0},{2,1},{3,2},{4,3},{5,4},{6,5},{7,6},{8,7},{9,8},{10,9},{11,1... | collective-permute-start | bytes 652808 | tf_op jit(solution)/shard_map/ppermute | solution.py:25
  155.6 5.9 %collective-permute-done.6 = f32[2,50,4,136]{3,1,2,0:T(8,128)S(1)} collective-permute-done((f32[2,50,4,136]{3,1,2,0:T(8,128)S(1)}, f32[2,50,4,136]{3,1,2,0:T(8,128)S(1)}, u32[]{:S(2)}, u32[]{:S(2)}) %collective-permute-start.6) | collective-permute-done | bytes 217632 | tf_op jit(solution)/shard_map/ppermute | solution.py:24
  161.5 0.4 pad_maximum_fusion.1
  161.9 0.5 copy.49
  162.4 1.3 pad.19.field_ref
  163.8 8.3 %shard_map.124 = f32[100,8,128]{2,1,0:T(8,128)} custom-call(f32[100,16,256]{2,1,0:T(8,128)} %pad.19.field_ref, f32[100,16,256]{2,1,0:T(8,128)} %bitcast.56, f32[100,16,256]{2,1,0:T(8,128)} %bitcast.52, f32[100,16,256]{2,1,0:T(8,128)} %bitcast.54, f32[100,16,256]{2,1,0:T(8,128)} %bitcast.50), custom_call_target="tpu_custom_call" | custom-call | flops 22937600 | bytes 9830400 | tf_op jit(solution)/shard_map/pallas_call | solution.py:78
  172.1 1.9 multiply_reduce_fusion.3
  173.9 2.6 %maximum_bitcast_fusion = f32[1,4]{1,0:T(1,128)S(1)} fusion(f32[1]{0:T(128)} %bitcast.26, f32[1]{0:T(128)} %bitcast.25, f32[1]{0:T(128)} %bitcast.24, f32[1]{0:T(128)} %bitcast), kind=kLoop, calls=%fused_computation.48 | loop fusion | flops 12 | bytes 32 | tf_op jit(solution)/shard_map/reshape.48
  176.6 0.6 scatter.4.part_ref
  177.2 17.6 %shard_map.125 = f32[8,128]{1,0:T(8,128)} custom-call(f32[8,128]{1,0:T(8,128)} %scatter.4.part_ref), custom_call_target="tpu_custom_call" | custom-call | tf_op jit(solution)/shard_map/pallas_call | solution.py:275
  194.8 1.4 fusion.24
  200.1 1.1 multiply_add_fusion
  (26 shorter events, 1.0 us)
Async XLA Ops:
  0.6 101.4 %copy-start = (f32[128,128]{1,0:T(8,128)S(1)}, f32[128,128]{1,0:T(8,128)}, u32[]{:S(2)}) copy-start(f32[128,128]{1,0:T(8,128)} %param.21) | copy-start | bytes 196612
  2.3 11.4 %copy-start.1 = (f32[2,50,8,128]{3,2,1,0:T(8,128)S(1)}, f32[2,50,8,128]{3,2,1,0:T(8,128)}, u32[]{:S(2)}) copy-start(f32[2,50,8,128]{3,2,1,0:T(8,128)} %param.14) | copy-start | bytes 1228804
  2.3 11.4 %copy-start.2 = (f32[2,50,8,128]{3,2,1,0:T(8,128)S(1)}, f32[2,50,8,128]{3,2,1,0:T(8,128)}, u32[]{:S(2)}) copy-start(f32[2,50,8,128]{3,2,1,0:T(8,128)} %param.15) | copy-start | bytes 1228804
  2.7 6.9 %collective-permute-start = (f32[2,2,50,8,4]{2,3,4,1,0:T(8,128)S(1)}, f32[2,2,50,8,4]{2,3,4,1,0:T(8,128)S(1)}, u32[]{:S(2)}, u32[]{:S(2)}) collective-permute-start(f32[2,2,50,8,4]{2,3,4,1,0:T(8,128)S(1)} %copy.52), channel_id=1, source_target_pairs={{0,16},{16,32},{32,48},{48,64},{64,80},{80,96},{96,112},{1,17},{17... | collective-permute-start | bytes 76808 | tf_op jit(solution)/shard_map/ppermute | solution.py:24
  7.7 5.6 %collective-permute-start.1 = (f32[2,2,50,8,4]{2,3,4,1,0:T(8,128)S(1)}, f32[2,2,50,8,4]{2,3,4,1,0:T(8,128)S(1)}, u32[]{:S(2)}, u32[]{:S(2)}) collective-permute-start(f32[2,2,50,8,4]{2,3,4,1,0:T(8,128)S(1)} %copy.53), channel_id=1, source_target_pairs={{16,0},{32,16},{48,32},{64,48},{80,64},{96,80},{112,96},{17,1},{33... | collective-permute-start | bytes 76808 | tf_op jit(solution)/shard_map/ppermute | solution.py:25
  14.5 6.6 %copy-start.7 = (s32[128,1]{0,1:T(1,128)S(1)}, s32[128,1]{0,1:T(1,128)}, u32[]{:S(2)}) copy-start(s32[128,1]{0,1:T(1,128)} %param.20) | copy-start | bytes 1540
  14.7 22.3 %collective-permute-start.2 = (f32[2,2,50,4,136]{4,3,2,1,0:T(4,128)S(1)}, f32[2,2,50,4,136]{4,3,2,1,0:T(4,128)S(1)}, u32[]{:S(2)}, u32[]{:S(2)}) collective-permute-start(f32[2,2,50,4,136]{4,3,2,1,0:T(4,128)S(1)} %get-tuple-element.28), channel_id=1, source_target_pairs={{0,1},{1,2},{2,3},{3,4},{4,5},{5,6},{6,7},{7,8},{8,9},{9,10},{10,1... | collective-permute-start | bytes 1305608 | tf_op jit(solution)/shard_map/ppermute | solution.py:24
  16.0 21.1 %collective-permute-start.3 = (f32[2,2,50,4,136]{4,3,2,1,0:T(4,128)S(1)}, f32[2,2,50,4,136]{4,3,2,1,0:T(4,128)S(1)}, u32[]{:S(2)}, u32[]{:S(2)}) collective-permute-start(f32[2,2,50,4,136]{4,3,2,1,0:T(4,128)S(1)} %get-tuple-element.29), channel_id=1, source_target_pairs={{1,0},{2,1},{3,2},{4,3},{5,4},{6,5},{7,6},{8,7},{9,8},{10,9},{11,1... | collective-permute-start | bytes 1305608 | tf_op jit(solution)/shard_map/ppermute | solution.py:25
  43.6 8.3 %copy-start.3 = (f32[2,50,8,128]{3,2,1,0:T(8,128)S(1)}, f32[2,50,8,128]{3,2,1,0:T(8,128)}, u32[]{:S(2)}) copy-start(f32[2,50,8,128]{3,2,1,0:T(8,128)} %param.16) | copy-start | bytes 1228804
  78.6 39.2 %copy-start.6 = (f32[2,128,128]{2,1,0:T(8,128)S(1)}, f32[2,128,128]{2,1,0:T(8,128)}, u32[]{:S(2)}) copy-start(f32[2,128,128]{2,1,0:T(8,128)} %scale_ref.1) | copy-start | bytes 393220
  137.5 8.0 %collective-permute-start.4 = (f32[2,50,8,4]{3,1,2,0:T(8,128)S(1)}, f32[2,50,8,4]{3,1,2,0:T(8,128)S(1)}, u32[]{:S(2)}, u32[]{:S(2)}) collective-permute-start(f32[2,50,8,4]{3,1,2,0:T(8,128)S(1)} %get-tuple-element.34), channel_id=1, source_target_pairs={{0,16},{16,32},{32,48},{48,64},{64,80},{80,96},{96,112},{1,17},{17... | collective-permute-start | bytes 38408 | tf_op jit(solution)/shard_map/ppermute | solution.py:24
  140.2 10.1 %collective-permute-start.5 = (f32[2,50,8,4]{3,1,2,0:T(8,128)S(1)}, f32[2,50,8,4]{3,1,2,0:T(8,128)S(1)}, u32[]{:S(2)}, u32[]{:S(2)}) collective-permute-start(f32[2,50,8,4]{3,1,2,0:T(8,128)S(1)} %get-tuple-element.35), channel_id=1, source_target_pairs={{16,0},{32,16},{48,32},{64,48},{80,64},{96,80},{112,96},{17,1},{33... | collective-permute-start | bytes 38408 | tf_op jit(solution)/shard_map/ppermute | solution.py:25
  150.8 10.7 %collective-permute-start.6 = (f32[2,50,4,136]{3,1,2,0:T(8,128)S(1)}, f32[2,50,4,136]{3,1,2,0:T(8,128)S(1)}, u32[]{:S(2)}, u32[]{:S(2)}) collective-permute-start(f32[2,50,4,136]{3,1,2,0:T(8,128)S(1)} %get-tuple-element.30), channel_id=1, source_target_pairs={{0,1},{1,2},{2,3},{3,4},{4,5},{5,6},{6,7},{7,8},{8,9},{9,10},{10,1... | collective-permute-start | bytes 652808 | tf_op jit(solution)/shard_map/ppermute | solution.py:24
  151.2 10.3 %collective-permute-start.7 = (f32[2,50,4,136]{3,1,2,0:T(8,128)S(1)}, f32[2,50,4,136]{3,1,2,0:T(8,128)S(1)}, u32[]{:S(2)}, u32[]{:S(2)}) collective-permute-start(f32[2,50,4,136]{3,1,2,0:T(8,128)S(1)} %get-tuple-element.31), channel_id=1, source_target_pairs={{1,0},{2,1},{3,2},{4,3},{5,4},{6,5},{7,6},{8,7},{9,8},{10,9},{11,1... | collective-permute-start | bytes 652808 | tf_op jit(solution)/shard_map/ppermute | solution.py:25
  163.8 8.3 %copy-start.4 = (f32[2,50,8,128]{3,2,1,0:T(8,128)S(1)}, f32[2,50,8,128]{3,2,1,0:T(8,128)}, u32[]{:S(2)}) copy-start(f32[2,50,8,128]{3,2,1,0:T(8,128)} %param.13) | copy-start | bytes 1228804
  172.1 28.0 %copy-start.5 = (f32[2,50,8,128]{3,2,1,0:T(8,128)S(1)}, f32[2,50,8,128]{3,2,1,0:T(8,128)}, u32[]{:S(2)}) copy-start(f32[2,50,8,128]{3,2,1,0:T(8,128)} %param.12) | copy-start | bytes 1228804
